TPU v7x, 32 devices: a whole 2x2x4 slice. The times are simulated.
32 devices in a mesh: dp: 2 (over x), seq: 4 (over y, core), tensor: 4 (over z).
Axes of the slice: x: 2, y: 2, z: 4, core: 2. Of those that a mesh axis runs over, the one named last changes fastest.
Arguments:
- inputs: bfloat16 [4, 2048, 1024], P('dp', ('seq', 'tensor')), may hold values from -6 to 6
- seg_starts: int32 [4, 4], P('dp', 'seq'), may hold values from 0 to 256, as said below
- lengths: int32 [4], P('dp'), may hold values from 512 to 2048, as said below
- init_state: float32 [512, 1024], P('tensor'), may hold values from -6 to 6
- attn_gain: float32 [1024], replicated, may hold values from 0.5 to 1.5
- state_gain: float32 [1024], replicated, may hold values from 0.5 to 1.5
- mlp_gain: float32 [1024], replicated, may hold values from 0.5 to 1.5
- w_query: bfloat16 [1024, 1024], P(None, 'tensor'), may hold values from -0.1875 to 0.1875
- w_key: bfloat16 [1024, 1024], P(None, 'tensor'), may hold values from -0.1875 to 0.1875
- w_value: bfloat16 [1024, 1024], P(None, 'tensor'), may hold values from -0.1875 to 0.1875
- w_out: bfloat16 [1024, 1024], P('tensor'), may hold values from -4 to 4
- w_squery: bfloat16 [1024, 1024], P(None, 'tensor'), may hold values from -0.1875 to 0.1875
- w_sout: bfloat16 [1024, 1024], P('tensor'), may hold values from -4 to 4
- w_up: bfloat16 [1024, 4096], P(None, 'tensor'), may hold values from -0.1875 to 0.1875
- w_down: bfloat16 [4096, 1024], P('tensor'), may hold values from -0.125 to 0.125
- rel_bias: float32 [32, 8], P(None, 'tensor'), may hold values from -4 to 4
- gate_bias: float32 [1024], replicated, may hold values from -3 to 3
- out_cot: bfloat16 [4, 2048, 1024], P('dp', ('seq', 'tensor')), may hold values from -6 to 6
- state_cot: bfloat16 [4, 4, 512, 1024], P('dp', 'seq', 'tensor'), may hold values from -6 to 6
Outputs:
- tokens_out: bfloat16 [4, 2048, 1024], P('dp', ('seq', 'tensor'))
- states_out: float32 [4, 4, 512, 1024], P('dp', 'seq', 'tensor')
- inputs_grad: float32 [4, 2048, 1024], P('dp', ('seq', 'tensor'))
- state_grad: float32 [512, 1024], P('tensor')
- attn_gain_grad: float32 [1024], replicated
- state_gain_grad: float32 [1024], replicated
- mlp_gain_grad: float32 [1024], replicated
- query_grad: float32 [1024, 1024], P(None, 'tensor')
- key_grad: float32 [1024, 1024], P(None, 'tensor')
- value_grad: float32 [1024, 1024], P(None, 'tensor')
- out_grad: float32 [1024, 1024], P('tensor')
- squery_grad: float32 [1024, 1024], P(None, 'tensor')
- sout_grad: float32 [1024, 1024], P('tensor')
- up_grad: float32 [1024, 4096], P(None, 'tensor')
- down_grad: float32 [4096, 1024], P('tensor')
- bias_grad: float32 [32, 8], P(None, 'tensor')
- gate_grad: float32 [1024], replicated
Inputs may be any that keep to these rules, and one draw needn't show every extreme that they name: `seg_starts`: each block's bidirectional segment starts at this offset inside the block and covers 256 tokens. `lengths`: tokens at or past a sequence's length are padding that no key may show.
All inputs are finite; a program needn't handle non-finite values.
Results may differ from a plain program's by a relative error of at most 0.025.
Values may be sent and summed in bfloat16 or wider, within the bound.
A program may use at most 192 MiB of HBM per device.

v0:
```python
import jax
import jax.numpy as jnp
from jax import lax
from jax.experimental import pallas as pl
from jax.experimental.pallas import tpu as pltpu
from jax.sharding import PartitionSpec as P

D = 1024
HEAD_DIM = 128
STATES = 512
BLOCK = 512
SEG = 256
BUCKETS = 32


norm_eps = 1e-06
masked_score = -1e30
bucket_edges = (12, 16, 23, 32, 46, 64, 91)


def passed_along(value, axis, steps):
    count = lax.axis_size(axis)
    leading, last = (max(0, -steps), min(count, count - steps))
    return lax.ppermute(value, axis, [(source, source + steps) for source in range(leading, last)])


def bucket_of(relative):
    distance = jnp.abs(relative)
    far_bucket = 8 + sum(((distance >= boundary).astype(jnp.int32) for boundary in bucket_edges))
    near_far = jnp.where(distance < 8, distance, far_bucket)
    return near_far + 16 * (relative > 0).astype(jnp.int32)


def token_mask(seg_start, seq_length, block_index):
    positions = jnp.arange(BLOCK)
    offset = block_index * BLOCK
    prev_valid = (block_index > 0) & (offset - BLOCK + positions < seq_length)
    cur_valid = offset + positions < seq_length
    inside = (positions >= seg_start) & (positions < seg_start + SEG)
    prev_mask = (positions[None, :] > positions[:, None]) & prev_valid[None, :]
    cur_mask = (
        (positions[None, :] <= positions[:, None]) | inside[None, :] & inside[:, None]
    ) & cur_valid[None, :]
    state_mask = jnp.ones((BLOCK, STATES), jnp.bool_)
    return jnp.concatenate([prev_mask, cur_mask, state_mask], axis=1)


def state_mask_of(valid_blk):
    batch_count = valid_blk.shape[0]
    block_part = jnp.broadcast_to(valid_blk[:, None, :], (batch_count, STATES, BLOCK))
    return jnp.concatenate([block_part, jnp.ones((batch_count, STATES, STATES), jnp.bool_)], axis=2)


def layer_norm(values, gain_vec):
    centered = values - jnp.mean(values, axis=-1, keepdims=True)
    spread = jnp.mean(centered * centered, axis=-1, keepdims=True)
    return centered * lax.rsqrt(spread + norm_eps) * gain_vec


def norm_back(values, gain_vec, grad_out):
    _, pullback = jax.vjp(layer_norm, values, gain_vec)
    return pullback(grad_out)


def gelu_back(pre_act, grad_out):
    _, pullback = jax.vjp(jax.nn.gelu, pre_act)
    return pullback(grad_out)[0]


def to_low(array_in):
    return array_in.astype(jnp.bfloat16)


def matmul(left, right):
    return jnp.einsum("...k,kn->...n", left, right, preferred_element_type=jnp.float32)


def matmul_t(left, right):
    return jnp.einsum("...n,kn->...k", left, right, preferred_element_type=jnp.float32)


def outer_sum(left, right):
    left_flat = left.reshape(-1, left.shape[-1])
    right_flat = right.reshape(-1, right.shape[-1])
    return lax.dot_general(
        left_flat, right_flat, (((0,), (0,)), ((), ())), preferred_element_type=jnp.float32
    )


def gather_rows(values):
    return lax.all_gather(values, "tensor", axis=1, tiled=True)


def sum_rows(terms):
    return lax.psum_scatter(
        terms.astype(jnp.bfloat16), "tensor", scatter_dimension=1, tiled=True
    ).astype(jnp.float32)


def pass_state(rows_now):
    return passed_along(rows_now.astype(jnp.bfloat16), "seq", 1).astype(rows_now.dtype)


def pass_back(grad_now):
    return passed_along(grad_now.astype(jnp.bfloat16), "seq", -1).astype(grad_now.dtype)


def split_heads(rows_in):
    return rows_in.reshape(rows_in.shape[0], rows_in.shape[1] // HEAD_DIM, HEAD_DIM)


def score_block(query_rows, key_all, bias_all, allowed):
    scores = (
        jnp.einsum(
            "qhd,khd->hqk",
            split_heads(query_rows),
            split_heads(key_all),
            preferred_element_type=jnp.float32,
        )
        * HEAD_DIM ** (-0.5)
        + bias_all
    )
    return jnp.where(allowed[None], scores, masked_score)


def attend_forward(query_rows, key_all, value_all, bias_all, allowed):
    scores = score_block(query_rows, key_all, bias_all, allowed)
    row_max = jnp.max(scores, axis=-1, keepdims=True)
    exp_scores = jnp.exp(scores - row_max)
    row_total = jnp.sum(exp_scores, axis=-1, keepdims=True)
    weight_all = to_low(exp_scores / row_total)
    mixed_out = jnp.einsum(
        "hqk,khd->qhd", weight_all, split_heads(value_all), preferred_element_type=jnp.float32
    )
    return (
        to_low(mixed_out.reshape(query_rows.shape[0], -1)),
        (row_max + jnp.log(row_total))[..., 0],
    )


def attend_back(query_rows, key_all, value_all, bias_all, allowed, log_total, grad_mixed):
    scores = score_block(query_rows, key_all, bias_all, allowed)
    weight_all = jnp.where(allowed[None], jnp.exp(scores - log_total[..., None]), 0.0)
    grad_heads = split_heads(grad_mixed)
    grad_weight = jnp.einsum(
        "qhd,khd->hqk", grad_heads, split_heads(value_all), preferred_element_type=jnp.float32
    )
    row_inner = jnp.sum(weight_all * grad_weight, axis=-1, keepdims=True)
    grad_scores = to_low(weight_all * (grad_weight - row_inner))
    grad_query = jnp.einsum(
        "hqk,khd->qhd", grad_scores, split_heads(key_all), preferred_element_type=jnp.float32
    ) * HEAD_DIM ** (-0.5)
    grad_keys = jnp.einsum(
        "hqk,qhd->khd", grad_scores, split_heads(query_rows), preferred_element_type=jnp.float32
    ) * HEAD_DIM ** (-0.5)
    grad_values = jnp.einsum(
        "hqk,qhd->khd", to_low(weight_all), grad_heads, preferred_element_type=jnp.float32
    )
    return (
        grad_query.reshape(query_rows.shape[0], -1),
        grad_keys.reshape(key_all.shape[0], -1),
        grad_values.reshape(key_all.shape[0], -1),
        grad_scores,
    )


def bias_lookup(rel_bias, rel_table):
    table_heads = jnp.zeros((rel_bias.shape[1],) + rel_table.shape, jnp.float32)
    for bucket_id in range(BUCKETS):
        table_heads = table_heads + jnp.where(
            rel_table[None] == bucket_id, rel_bias[bucket_id][:, None, None], 0.0
        )
    return table_heads


def bias_sums(score_grad, rel_table):
    grad_wide = score_grad.astype(jnp.float32)
    columns = []
    for bucket_id in range(BUCKETS):
        columns.append(
            jnp.sum(jnp.where(rel_table[None, None] == bucket_id, grad_wide, 0.0), axis=(0, 2, 3))
        )
    return jnp.stack(columns, axis=0)


def body(
    inputs,
    seg_starts,
    lengths,
    init_state,
    attn_gain,
    state_gain,
    mlp_gain,
    w_query,
    w_key,
    w_value,
    w_out,
    w_squery,
    w_sout,
    w_up,
    w_down,
    rel_bias,
    gate_bias,
    out_cot,
    state_cot,
):
    seq_count = inputs.shape[0]
    chain_length = lax.axis_size("seq")
    block_index = lax.axis_index("seq")
    is_first = block_index == 0
    width_local = w_query.shape[1]
    head_count = width_local // HEAD_DIM
    gate_value = jax.nn.sigmoid(gate_bias)
    positions = jnp.arange(BLOCK)
    inputs_wide = inputs.astype(jnp.float32)
    tokens_low = gather_rows(to_low(layer_norm(inputs_wide, attn_gain)))
    query_tok = to_low(matmul(tokens_low, w_query))
    key_tok = to_low(matmul(tokens_low, w_key))
    value_tok = to_low(matmul(tokens_low, w_value))
    key_prev, value_prev = passed_along((key_tok, value_tok), "seq", 1)
    valid_keys = (block_index * BLOCK + positions)[None, :] < lengths[:, None]
    batched_attend = jax.vmap(attend_forward, in_axes=(0, 0, 0, None, 0))
    batched_back = jax.vmap(attend_back, in_axes=(0, 0, 0, None, 0, 0, 0))

    def state_forward(state_rows, key_blk, value_blk, valid_blk):
        state_low = lax.all_gather(
            to_low(layer_norm(state_rows, state_gain)), "tensor", axis=1, tiled=True
        )
        query_st = to_low(matmul(state_low, w_squery))
        key_st = to_low(matmul(state_low, w_key))
        value_st = to_low(matmul(state_low, w_value))
        key_all = jnp.concatenate([key_blk, key_st], axis=1)
        value_all = jnp.concatenate([value_blk, value_st], axis=1)
        mixed_st, lse_st = batched_attend(
            query_st, key_all, value_all, 0.0, state_mask_of(valid_blk)
        )
        update = lax.psum_scatter(
            matmul(mixed_st, w_sout).astype(jnp.bfloat16), "tensor", scatter_dimension=1, tiled=True
        ).astype(jnp.float32)
        state_next = gate_value * state_rows + (1.0 - gate_value) * update
        return (state_next, (state_low, query_st, key_st, value_st, mixed_st, lse_st, update))

    def state_backward(
        grad_out, state_rows, kept_one, key_blk, value_blk, valid_blk, extra_key, extra_value
    ):
        state_low, query_st, key_st, value_st, mixed_st, lse_st, update = kept_one
        gate_part = (
            jnp.sum(grad_out * (state_rows - update), axis=(0, 1)) * gate_value * (1.0 - gate_value)
        )
        grad_update = lax.all_gather(
            to_low((1.0 - gate_value) * grad_out), "tensor", axis=1, tiled=True
        )
        grad_mixed_st = to_low(matmul_t(grad_update, w_sout))
        sout_part = outer_sum(mixed_st, grad_update)
        key_all = jnp.concatenate([key_blk, key_st], axis=1)
        value_all = jnp.concatenate([value_blk, value_st], axis=1)
        grad_query_st, grad_keys_st, grad_values_st, _ = batched_back(
            query_st, key_all, value_all, 0.0, state_mask_of(valid_blk), lse_st, grad_mixed_st
        )
        query_low = to_low(grad_query_st)
        key_low = to_low(grad_keys_st[:, BLOCK:] + extra_key)
        value_low = to_low(grad_values_st[:, BLOCK:] + extra_value)
        squery_part = outer_sum(state_low, query_low)
        key_part = outer_sum(state_low, key_low)
        value_part = outer_sum(state_low, value_low)
        terms = (
            matmul_t(query_low, w_squery) + matmul_t(key_low, w_key) + matmul_t(value_low, w_value)
        )
        grad_normed = lax.psum_scatter(
            terms.astype(jnp.bfloat16), "tensor", scatter_dimension=1, tiled=True
        ).astype(jnp.float32)
        grad_rows_norm, gain_part = norm_back(state_rows, state_gain, grad_normed)
        grad_in = gate_value * grad_out + grad_rows_norm
        block_grads = (grad_keys_st[:, :BLOCK], grad_values_st[:, :BLOCK])
        return (
            grad_in,
            block_grads,
            (squery_part, key_part, value_part, sout_part, gain_part, gate_part),
        )

    zeros_rows = jnp.zeros((seq_count,) + init_state.shape, jnp.float32)
    narrow_zero = jnp.zeros((seq_count, STATES, width_local), jnp.bfloat16)
    stored_start = (
        zeros_rows,
        zeros_rows,
        jnp.zeros((seq_count, STATES, D), jnp.bfloat16),
        narrow_zero,
        narrow_zero,
        narrow_zero,
        narrow_zero,
        jnp.zeros((seq_count, head_count, STATES), jnp.float32),
        zeros_rows,
    )

    def forward_turn(turn_index, carry):
        incoming, stored_now = carry
        order_index = turn_index - block_index
        is_live = (order_index >= 0) & (order_index < seq_count)
        picked = jnp.clip(order_index, 0, seq_count - 1)
        rows_now = jnp.where(is_first, init_state[None], incoming)
        key_one = lax.dynamic_slice_in_dim(key_tok, picked, 1, 0)
        value_one = lax.dynamic_slice_in_dim(value_tok, picked, 1, 0)
        valid_one = lax.dynamic_slice_in_dim(valid_keys, picked, 1, 0)
        rows_next, kept_one = state_forward(rows_now, key_one, value_one, valid_one)
        fresh = (rows_now, rows_next) + kept_one
        stored_now = tuple(
            (
                jnp.where(
                    is_live,
                    lax.dynamic_update_slice_in_dim(whole_array, fresh_part, picked, 0),
                    whole_array,
                )
                for whole_array, fresh_part in zip(stored_now, fresh)
            )
        )
        return (pass_state(rows_next), stored_now)

    incoming_start = jnp.zeros((1,) + init_state.shape, jnp.float32)
    _, stored_all = lax.fori_loop(
        0, chain_length + seq_count - 1, forward_turn, (incoming_start, stored_start)
    )
    state_in = stored_all[0]
    state_out = stored_all[1]
    kept = stored_all[2:]
    key_all_tok = jnp.concatenate([key_prev, key_tok, kept[2]], axis=1)
    value_all_tok = jnp.concatenate([value_prev, value_tok, kept[3]], axis=1)
    allowed_tok = jax.vmap(token_mask, in_axes=(0, 0, None))(seg_starts[:, 0], lengths, block_index)
    rel_table = bucket_of((jnp.arange(2 * BLOCK) - BLOCK)[None, :] - positions[:, None])
    full_bias = jnp.concatenate(
        [bias_lookup(rel_bias, rel_table), jnp.zeros((head_count, BLOCK, STATES), jnp.float32)],
        axis=2,
    )
    mixed_tok, lse_tok = batched_attend(
        query_tok, key_all_tok, value_all_tok, full_bias, allowed_tok
    )
    hidden_in = inputs_wide + sum_rows(matmul(mixed_tok, w_out))
    mid_low = gather_rows(to_low(layer_norm(hidden_in, mlp_gain)))
    pre_act = matmul(mid_low, w_up)
    hidden_low = to_low(jax.nn.gelu(pre_act))
    mlp_rows = sum_rows(matmul(hidden_low, w_down))
    tokens_out = (hidden_in + mlp_rows).astype(jnp.bfloat16)
    cot_wide = out_cot.astype(jnp.float32)
    cot_used = gather_rows(out_cot)
    grad_hidden_act = matmul_t(cot_used, w_down)
    down_grad = outer_sum(hidden_low, cot_used)
    grad_pre = to_low(gelu_back(pre_act, grad_hidden_act))
    up_grad = outer_sum(mid_low, grad_pre)
    grad_normed_mid = sum_rows(matmul_t(grad_pre, w_up))
    grad_mid_in, mlp_gain_grad = norm_back(hidden_in, mlp_gain, grad_normed_mid)
    grad_hidden = cot_wide + grad_mid_in
    grad_attn_low = gather_rows(to_low(grad_hidden))
    grad_mixed = to_low(matmul_t(grad_attn_low, w_out))
    out_grad = outer_sum(mixed_tok, grad_attn_low)
    grad_query_tok, grad_keys_tok, grad_values_tok, grad_scores = batched_back(
        query_tok, key_all_tok, value_all_tok, full_bias, allowed_tok, lse_tok, grad_mixed
    )
    bias_grad = bias_sums(grad_scores[..., : 2 * BLOCK], rel_table)
    grad_key_next, grad_value_next = (
        passed_along(grad_keys_tok[:, :BLOCK].astype(jnp.bfloat16), "seq", -1).astype(jnp.float32),
        passed_along(grad_values_tok[:, :BLOCK].astype(jnp.bfloat16), "seq", -1).astype(
            jnp.float32
        ),
    )
    grad_key_own = grad_keys_tok[:, BLOCK : 2 * BLOCK] + grad_key_next
    grad_value_own = grad_values_tok[:, BLOCK : 2 * BLOCK] + grad_value_next
    grad_key_st_tok = grad_keys_tok[:, 2 * BLOCK :]
    grad_value_st_tok = grad_values_tok[:, 2 * BLOCK :]
    cot_rows = state_cot[:, 0].astype(jnp.float32)
    wide_zero = jnp.zeros((seq_count, BLOCK, width_local), jnp.float32)
    stored_back = (zeros_rows, wide_zero, wide_zero)
    totals_start = (
        jnp.zeros((D, width_local), jnp.float32),
        jnp.zeros((D, width_local), jnp.float32),
        jnp.zeros((D, width_local), jnp.float32),
        jnp.zeros((width_local, D), jnp.float32),
        jnp.zeros((D,), jnp.float32),
        jnp.zeros((D,), jnp.float32),
    )

    def backward_turn(turn_index, carry):
        incoming, stored_now, totals_now = carry
        order_index = turn_index - (chain_length - 1 - block_index)
        is_live = (order_index >= 0) & (order_index < seq_count)
        picked = jnp.clip(order_index, 0, seq_count - 1)

        def slice_one(whole_array):
            return lax.dynamic_slice_in_dim(whole_array, picked, 1, 0)

        grad_out = slice_one(cot_rows) + incoming
        kept_one = tuple((slice_one(kept_array) for kept_array in kept))
        grad_in, block_one, parts_one = state_backward(
            grad_out,
            slice_one(state_in),
            kept_one,
            slice_one(key_tok),
            slice_one(value_tok),
            slice_one(valid_keys),
            slice_one(grad_key_st_tok),
            slice_one(grad_value_st_tok),
        )
        fresh = (grad_in,) + block_one
        stored_now = tuple(
            (
                jnp.where(
                    is_live,
                    lax.dynamic_update_slice_in_dim(whole_array, fresh_part, picked, 0),
                    whole_array,
                )
                for whole_array, fresh_part in zip(stored_now, fresh)
            )
        )
        totals_now = tuple(
            (
                total_now + jnp.where(is_live, part_now, 0.0)
                for total_now, part_now in zip(totals_now, parts_one)
            )
        )
        return (pass_back(grad_in), stored_now, totals_now)

    incoming_start = jnp.zeros((1,) + init_state.shape, jnp.float32)
    _, stored_done, weight_parts = lax.fori_loop(
        0, chain_length + seq_count - 1, backward_turn, (incoming_start, stored_back, totals_start)
    )
    grad_in_all, grad_key_blk, grad_value_blk = stored_done
    query_low = to_low(grad_query_tok)
    key_low = to_low(grad_key_own + grad_key_blk)
    value_low = to_low(grad_value_own + grad_value_blk)
    query_grad = outer_sum(tokens_low, query_low)
    key_grad = outer_sum(tokens_low, key_low) + weight_parts[1]
    value_grad = outer_sum(tokens_low, value_low) + weight_parts[2]
    grad_tokens = sum_rows(
        matmul_t(query_low, w_query) + matmul_t(key_low, w_key) + matmul_t(value_low, w_value)
    )
    grad_in_norm, attn_gain_grad = norm_back(inputs_wide, attn_gain, grad_tokens)
    inputs_grad = grad_hidden + grad_in_norm
    state_part = jnp.where(is_first, jnp.sum(grad_in_all, axis=0), 0.0)
    gains = lax.psum(
        jnp.stack([attn_gain_grad, weight_parts[4], mlp_gain_grad, weight_parts[5]]), "tensor"
    )
    totals = (
        lax.psum(query_grad.astype(jnp.bfloat16), ("dp", "seq")).astype(jnp.float32),
        lax.psum(key_grad.astype(jnp.bfloat16), ("dp", "seq")).astype(jnp.float32),
        lax.psum(value_grad.astype(jnp.bfloat16), ("dp", "seq")).astype(jnp.float32),
        lax.psum(out_grad.astype(jnp.bfloat16), ("dp", "seq")).astype(jnp.float32),
        lax.psum(weight_parts[0].astype(jnp.bfloat16), ("dp", "seq")).astype(jnp.float32),
        lax.psum(weight_parts[3].astype(jnp.bfloat16), ("dp", "seq")).astype(jnp.float32),
        lax.psum(up_grad.astype(jnp.bfloat16), ("dp", "seq")).astype(jnp.float32),
        lax.psum(down_grad.astype(jnp.bfloat16), ("dp", "seq")).astype(jnp.float32),
        lax.psum(bias_grad.astype(jnp.bfloat16), ("dp", "seq")).astype(jnp.float32),
        lax.psum(state_part.astype(jnp.bfloat16), ("dp", "seq")).astype(jnp.float32),
        lax.psum(gains.astype(jnp.bfloat16), ("dp", "seq")).astype(jnp.float32),
    )
    gain_total = totals[10]
    return (
        tokens_out,
        state_out[:, None],
        inputs_grad,
        totals[9],
        gain_total[0],
        gain_total[1],
        gain_total[2],
        totals[0],
        totals[1],
        totals[2],
        totals[3],
        totals[4],
        totals[5],
        totals[6],
        totals[7],
        totals[8],
        gain_total[3],
    )


def chosen_body(mesh):
    if mesh.shape["seq"] == 4 and mesh.shape["tensor"] == 4:
        return line_body
    return body


MESH_ID = pl.DeviceIdType.MESH
ROWS = 128
CHUNKS = BLOCK // ROWS
LINE = 8
SCALE = HEAD_DIM ** (-0.5)
VMEM_LIMIT = 60 * 1024 * 1024


def dot_nn(left, right):
    return lax.dot_general(left, right, (((1,), (0,)), ((), ())), preferred_element_type=jnp.float32)


def dot_nt(left, right):
    return lax.dot_general(left, right, (((1,), (1,)), ((), ())), preferred_element_type=jnp.float32)


def dot_tn(left, right):
    return lax.dot_general(left, right, (((0,), (0,)), ((), ())), preferred_element_type=jnp.float32)


def line_place():
    place = lax.axis_index("seq")
    half = lax.rem(place, 2)
    rank = lax.axis_index("tensor")
    return place, half, rank


def span(index, size):
    return pl.ds(pl.multiple_of(index * size, size), size)


def fetch_pieces(kept, first, rows, target, sem):
    for owner in range(8):
        pltpu.make_async_copy(
            kept.at[owner, :, pl.ds(first, rows), :], target.at[:, owner], sem
        ).start()


def fetched(target, sem):
    pltpu.make_async_copy(target, target, sem).wait()


def norm_parts(rows):
    centered = rows - jnp.mean(rows, axis=-1, keepdims=True)
    spread = jnp.mean(centered * centered, axis=-1, keepdims=True)
    return centered, lax.rsqrt(spread + norm_eps)


def token_masks(scal, block_id, first_row):
    length = scal[0]
    start = scal[1 + block_id]
    row = lax.broadcasted_iota(jnp.int32, (ROWS, BLOCK), 0) + first_row
    col = lax.broadcasted_iota(jnp.int32, (ROWS, BLOCK), 1)
    prev_limit = jnp.where(block_id > 0, length - (block_id - 1) * BLOCK, 0)
    prev_ok = (col > row) & (col < prev_limit)
    row_in = (row >= start) & (row < start + SEG)
    col_in = (col >= start) & (col < start + SEG)
    cur_ok = ((col <= row) | (row_in & col_in)) & (col < length - block_id * BLOCK)
    return prev_ok, cur_ok


def state_block_mask(scal, block_id):
    col = lax.broadcasted_iota(jnp.int32, (ROWS, BLOCK), 1)
    return col < scal[0] - block_id * BLOCK


def softmax_of(score_parts):
    top = jnp.max(score_parts[0], axis=-1, keepdims=True)
    for part in score_parts[1:]:
        top = jnp.maximum(top, jnp.max(part, axis=-1, keepdims=True))
    raised = [jnp.exp(part - top) for part in score_parts]
    total = jnp.sum(raised[0], axis=-1, keepdims=True)
    for part in raised[1:]:
        total = total + jnp.sum(part, axis=-1, keepdims=True)
    inverse = 1.0 / total
    return [to_low(part * inverse) for part in raised], top + jnp.log(total)


def token_scores(scal, qkv, qkvst, bias, block_id, chunk):
    rows = span(chunk, ROWS)
    prev_id = jnp.maximum(block_id - 1, 0)
    query = qkv[block_id, rows, 0:128]
    prev_ok, cur_ok = token_masks(scal, block_id, chunk * ROWS)
    prev = dot_nt(query, qkv[prev_id, :, 128:256]) * SCALE + bias[rows, 0:BLOCK]
    cur = dot_nt(query, qkv[block_id, :, 128:256]) * SCALE + bias[rows, BLOCK : 2 * BLOCK]
    stt = dot_nt(query, qkvst[block_id, :, 128:256]) * SCALE
    prev = jnp.where(prev_ok, prev, masked_score)
    cur = jnp.where(cur_ok, cur, masked_score)
    return query, (prev, cur, stt)


def state_scores(scal, qkv, qkvst, block_id, chunk):
    query = qkvst[block_id, span(chunk, ROWS), 0:128]
    tok = dot_nt(query, qkv[block_id, :, 128:256]) * SCALE
    tok = jnp.where(state_block_mask(scal, block_id), tok, masked_score)
    stt = dot_nt(query, qkvst[block_id, :, 128:256]) * SCALE
    return query, (tok, stt)


def forward_kernel(
    scal, qkv, kept, w_state, vecs, bias,
    o_out, lse_out, state_rows, state_low, qkvst, lse_st, os_rows,
    held, os_all, w_sout, start, send_sem, pass_sem, recv_sem, local_sem,
):
    place, half, rank = line_place()
    fetch_pieces(kept, 32, 16, start, local_sem.at[0])
    fetch_pieces(kept, 0, 32, w_sout, local_sem.at[1])
    partner = place + 1 - 2 * half
    head = 2 * rank + half
    peers = [lax.rem(rank + step, 4) for step in (1, 2, 3)]
    barrier = pltpu.get_barrier_semaphore()
    for peer in peers:
        pl.semaphore_signal(
            barrier, inc=1, device_id={"seq": place, "tensor": peer}, device_id_type=MESH_ID
        )
    pl.semaphore_signal(
        barrier, inc=1, device_id={"seq": partner, "tensor": rank}, device_id_type=MESH_ID
    )
    fetched(start, local_sem.at[0])
    held[...] = start[...].reshape(STATES, D).astype(jnp.float32)
    gain = vecs[0:1, :]
    gate = vecs[1:2, :]
    pl.semaphore_wait(barrier, 4)
    fetched(w_sout, local_sem.at[1])

    def carry_copy(block_id, which, sem, seq_to, rank_to):
        part = os_all.at[block_id, :, span(which, 128)]
        return pltpu.make_async_remote_copy(
            src_ref=part,
            dst_ref=part,
            send_sem=sem,
            recv_sem=recv_sem.at[block_id, which],
            device_id={"seq": seq_to, "tensor": rank_to},
            device_id_type=MESH_ID,
        )

    def one_block(block_id, _):
        def project(chunk, _):
            rows = span(chunk, ROWS)
            centered, scale = norm_parts(held[rows, :])
            low = to_low(centered * scale * gain)
            state_low[block_id, rows, :] = low
            qkvst[block_id, rows, :] = to_low(dot_nn(low, w_state[...]))
            return 0

        lax.fori_loop(0, CHUNKS, project, 0)

        def attend_state(chunk, _):
            rows = span(chunk, ROWS)
            _, parts = state_scores(scal, qkv, qkvst, block_id, chunk)
            (w_tok, w_stt), total = softmax_of(parts)
            mixed = dot_nn(w_tok, qkv[block_id, :, 256:384]) + dot_nn(
                w_stt, qkvst[block_id, :, 256:384]
            )
            os_all[block_id, rows, span(head, 128)] = to_low(mixed)
            lse_st[block_id, rows, :] = total
            return 0

        lax.fori_loop(0, CHUNKS, attend_state, 0)
        for slot, peer in enumerate(peers):
            carry_copy(block_id, head, send_sem.at[block_id, slot], place, peer).start()
        carry_copy(block_id, head, send_sem.at[block_id, 3], partner, rank).start()

        def attend_token(chunk, _):
            rows = span(chunk, ROWS)
            _, parts = token_scores(scal, qkv, qkvst, bias, block_id, chunk)
            weights, total = softmax_of(parts)
            prev_id = jnp.maximum(block_id - 1, 0)
            mixed = (
                dot_nn(weights[0], qkv[prev_id, :, 256:384])
                + dot_nn(weights[1], qkv[block_id, :, 256:384])
                + dot_nn(weights[2], qkvst[block_id, :, 256:384])
            )
            o_out[block_id, rows, :] = to_low(mixed)
            lse_out[block_id, rows, :] = total
            return 0

        lax.fori_loop(0, CHUNKS, attend_token, 0)
        for slot, peer in enumerate(peers):
            other = 2 * peer + half
            carry_copy(block_id, other, send_sem.at[block_id, slot], place, peer).wait_recv()
            carry_copy(block_id, other, pass_sem.at[block_id, slot], partner, rank).start()
        for other_rank in range(4):
            carry_copy(
                block_id, 2 * other_rank + 1 - half, send_sem.at[block_id, 3], partner, rank
            ).wait_recv()

        def update(chunk, _):
            rows = span(chunk, ROWS)
            change = dot_nn(os_all[block_id, rows, :], w_sout[...].reshape(D, D))
            held[rows, :] = gate * held[rows, :] + (1.0 - gate) * change
            return 0

        lax.fori_loop(0, CHUNKS, update, 0)
        state_rows[block_id] = held[span(rank, 128), :]
        os_rows[block_id] = os_all[block_id, span(head, 64), :]
        return 0

    lax.fori_loop(0, 4, one_block, 0)

    def drain(block_id, _):
        for slot, peer in enumerate(peers):
            carry_copy(block_id, head, send_sem.at[block_id, slot], place, peer).wait_send()
            other = 2 * peer + half
            carry_copy(block_id, other, pass_sem.at[block_id, slot], partner, rank).wait_send()
        carry_copy(block_id, head, send_sem.at[block_id, 3], partner, rank).wait_send()
        return 0

    lax.fori_loop(0, 4, drain, 0)


def any_specs(count):
    return [pl.BlockSpec(memory_space=pl.ANY)] * count


def vmem_specs(count):
    return [pl.BlockSpec(memory_space=pltpu.VMEM)] * count


def forward_chain(scal, qkv, kept, w_state, vecs, bias):
    low, wide = jnp.bfloat16, jnp.float32
    shapes = (
        ((4, BLOCK, 128), low),
        ((4, BLOCK, 1), wide),
        ((4, 128, D), wide),
        ((4, STATES, D), low),
        ((4, STATES, 384), low),
        ((4, STATES, 1), wide),
        ((4, 64, D), low),
    )
    return pl.pallas_call(
        forward_kernel,
        out_shape=[jax.ShapeDtypeStruct(*one) for one in shapes],
        in_specs=[pl.BlockSpec(memory_space=pltpu.SMEM)]
        + vmem_specs(1)
        + any_specs(1)
        + vmem_specs(3),
        out_specs=vmem_specs(7),
        scratch_shapes=[
            pltpu.VMEM((STATES, D), wide),
            pltpu.VMEM((4, STATES, D), low),
            pltpu.VMEM((4, 8, 32, D), low),
            pltpu.VMEM((4, 8, 16, D), low),
            pltpu.SemaphoreType.DMA((4, 4)),
            pltpu.SemaphoreType.DMA((4, 3)),
            pltpu.SemaphoreType.DMA((4, 8)),
            pltpu.SemaphoreType.DMA((2,)),
        ],
        compiler_params=pltpu.CompilerParams(
            collective_id=1, has_side_effects=True, vmem_limit_bytes=VMEM_LIMIT
        ),
        cost_estimate=pl.CostEstimate(flops=20000000000, bytes_accessed=20000000, transcendentals=0),
        name="forward_chain",
    )(scal, qkv, kept, w_state, vecs, bias)


def backward_kernel(
    scal, qkv, d_o, lse_tok, qkvst, lse_st, state_rows, begin, cots, back, kept, vecs, bias,
    extra, hidden,
    d_qkv, d_qkvst, du_rows, d_start, sums, dz_sum, state_out, tokens_out, out_part,
    key_acc, value_acc, st_key, st_value, dos_rows, dos_got, d_got, grad_in,
    states, w_back, w_sout, work, core_got, near_got, far_got, total,
    send_sem, recv_sem, local_sem, side_sem, ring_send, ring_recv,
):
    place, half, rank = line_place()
    own_rows = pl.ds(pl.multiple_of(half * 64, 64), 64)
    loads = [
        pltpu.make_async_copy(
            state_rows.at[:, own_rows, :], states.at[pl.ds(1, 4)], local_sem.at[0]
        ),
        pltpu.make_async_copy(
            state_rows.at[place], state_out.at[place // 2], local_sem.at[3]
        ),
        pltpu.make_async_copy(extra, work, local_sem.at[4]),
    ]
    for one in loads:
        one.start()
    fetch_pieces(kept, 0, 32, w_sout, local_sem.at[1])
    for owner in range(8):
        pltpu.make_async_copy(
            back.at[owner], w_back.at[:, owner // 4, :, owner % 4], local_sem.at[2]
        ).start()
    states[0] = to_low(begin[own_rows, :]).astype(jnp.float32)
    head = 2 * rank + half
    peers = []
    for step in range(1, LINE):
        other = lax.rem(head + step, LINE)
        peers.append((other, place - half + lax.rem(other, 2), other // 2))
    barrier = pltpu.get_barrier_semaphore()
    for _, seq_to, rank_to in peers:
        pl.semaphore_signal(
            barrier, inc=1, device_id={"seq": seq_to, "tensor": rank_to}, device_id_type=MESH_ID
        )
    beside = lax.rem(place + 2, 4)
    pl.semaphore_signal(barrier, inc=1, device_id={"seq": beside}, device_id_type=MESH_ID)
    pl.semaphore_signal(
        barrier, inc=1, device_id={"dp": 1 - lax.axis_index("dp")}, device_id_type=MESH_ID
    )
    plane_steps = plane_scatter(
        work, core_got, near_got, far_got, total, 384, ring_send, ring_recv
    )
    next(plane_steps)

    def aside(block_id, row_set):
        return pltpu.make_async_remote_copy(
            src_ref=state_rows.at[block_id],
            dst_ref=state_out.at[row_set],
            send_sem=side_sem.at[0],
            recv_sem=side_sem.at[1],
            device_id={"seq": beside},
            device_id_type=MESH_ID,
        )

    gain = vecs[0:1, :]
    gate = vecs[1:2, :]
    key_acc[...] = jnp.zeros_like(key_acc)
    value_acc[...] = jnp.zeros_like(value_acc)
    dz_sum[...] = jnp.zeros_like(dz_sum)
    sums[...] = jnp.zeros_like(sums)
    grad_in[...] = jnp.zeros_like(grad_in)

    def back_parts(parts, total, grad, values):
        weights = [jnp.exp(part - total) for part in parts]
        d_weights = [dot_nt(grad, value) for value in values]
        inner = jnp.sum(weights[0] * d_weights[0], axis=-1, keepdims=True)
        for one, other in zip(weights[1:], d_weights[1:]):
            inner = inner + jnp.sum(one * other, axis=-1, keepdims=True)
        d_scores = [to_low(one * (other - inner)) for one, other in zip(weights, d_weights)]
        return [to_low(one) for one in weights], d_scores

    def token_back(block_id):
        prev_id = jnp.maximum(block_id - 1, 0)
        st_key[...] = jnp.zeros_like(st_key)
        st_value[...] = jnp.zeros_like(st_value)

        def one_chunk(chunk, _):
            rows = span(chunk, ROWS)
            query, parts = token_scores(scal, qkv, qkvst, bias, block_id, chunk)
            grad = d_o[block_id, rows, :]
            keys = (qkv[prev_id, :, 128:256], qkv[block_id, :, 128:256], qkvst[block_id, :, 128:256])
            values = (
                qkv[prev_id, :, 256:384], qkv[block_id, :, 256:384], qkvst[block_id, :, 256:384]
            )
            weights, d_scores = back_parts(parts, lse_tok[block_id, rows, :], grad, values)
            d_query = dot_nn(d_scores[0], keys[0])
            d_query = d_query + dot_nn(d_scores[1], keys[1]) + dot_nn(d_scores[2], keys[2])
            d_qkv[block_id, rows, 0:128] = to_low(d_query * SCALE)
            key_acc[prev_id] += dot_tn(d_scores[0], query) * SCALE
            value_acc[prev_id] += dot_tn(weights[0], grad)
            key_acc[block_id] += dot_tn(d_scores[1], query) * SCALE
            value_acc[block_id] += dot_tn(weights[1], grad)
            st_key[...] += dot_tn(d_scores[2], query) * SCALE
            st_value[...] += dot_tn(weights[2], grad)
            dz_sum[rows, 0:BLOCK] += d_scores[0].astype(jnp.float32)
            dz_sum[rows, BLOCK : 2 * BLOCK] += d_scores[1].astype(jnp.float32)
            return 0

        lax.fori_loop(0, CHUNKS, one_chunk, 0)

    token_back(3)
    pl.semaphore_wait(barrier, LINE + 1)
    aside(beside, place // 2).start()
    loads[2].wait()
    loads[0].wait()
    fetched(w_sout, local_sem.at[1])
    fetched(w_back, local_sem.at[2])

    def mixed_copy(block_id, slot, sender, other, seq_to, rank_to):
        return pltpu.make_async_remote_copy(
            src_ref=dos_rows.at[block_id, :, span(other, 128)],
            dst_ref=dos_got.at[block_id, span(sender, 64), :],
            send_sem=send_sem.at[0, block_id, slot],
            recv_sem=recv_sem.at[0, block_id, sender],
            device_id={"seq": seq_to, "tensor": rank_to},
            device_id_type=MESH_ID,
        )

    def grads_copy(block_id, slot, sender, other, seq_to, rank_to):
        return pltpu.make_async_remote_copy(
            src_ref=d_qkvst.at[block_id, span(other, 64), :],
            dst_ref=d_got.at[block_id, sender],
            send_sem=send_sem.at[1, block_id, slot],
            recv_sem=recv_sem.at[1, block_id, sender],
            device_id={"seq": seq_to, "tensor": rank_to},
            device_id_type=MESH_ID,
        )

    def one_block(turn, _):
        block_id = 3 - turn
        grad_out = grad_in[...] + cots[block_id].astype(jnp.float32)
        sums[0:1, :] += jnp.sum(
            grad_out * (states[block_id] - states[block_id + 1]), axis=0, keepdims=True
        ) * gate
        change = to_low((1.0 - gate) * grad_out)
        du_rows[block_id] = change
        dos_rows[block_id] = to_low(dot_nt(change, w_sout[...].reshape(D, D)))
        for slot, (other, seq_to, rank_to) in enumerate(peers):
            mixed_copy(block_id, slot, head, other, seq_to, rank_to).start()
        dos_got[block_id, span(head, 64), :] = dos_rows[block_id, :, span(head, 128)]
        for slot, (other, seq_to, rank_to) in enumerate(peers):
            mixed_copy(block_id, slot, other, other, seq_to, rank_to).wait_recv()

        def one_chunk(chunk, _):
            rows = span(chunk, ROWS)
            query, parts = state_scores(scal, qkv, qkvst, block_id, chunk)
            grad = dos_got[block_id, rows, :]
            keys = (qkv[block_id, :, 128:256], qkvst[block_id, :, 128:256])
            values = (qkv[block_id, :, 256:384], qkvst[block_id, :, 256:384])
            weights, d_scores = back_parts(parts, lse_st[block_id, rows, :], grad, values)
            d_query = dot_nn(d_scores[0], keys[0]) + dot_nn(d_scores[1], keys[1])
            d_qkvst[block_id, rows, 0:128] = to_low(d_query * SCALE)
            key_acc[block_id] += dot_tn(d_scores[0], query) * SCALE
            value_acc[block_id] += dot_tn(weights[0], grad)
            st_key[...] += dot_tn(d_scores[1], query) * SCALE
            st_value[...] += dot_tn(weights[1], grad)
            return 0

        lax.fori_loop(0, CHUNKS, one_chunk, 0)
        d_qkvst[block_id, :, 128:256] = to_low(st_key[...])
        d_qkvst[block_id, :, 256:384] = to_low(st_value[...])
        for slot, (other, seq_to, rank_to) in enumerate(peers):
            grads_copy(block_id, slot, head, other, seq_to, rank_to).start()
        d_got[block_id, head] = d_qkvst[block_id, span(head, 64), :]

        for step in range(4):

            @pl.when(turn == step)
            def _():
                next(plane_steps, None)

        @pl.when(turn < 3)
        def _():
            token_back(block_id - 1)

        d_qkv[block_id, :, 128:256] = to_low(key_acc[block_id])
        d_qkv[block_id, :, 256:384] = to_low(value_acc[block_id])
        for slot, (other, seq_to, rank_to) in enumerate(peers):
            grads_copy(block_id, slot, other, other, seq_to, rank_to).wait_recv()
        d_low = dot_nn(d_got[block_id, 0], w_back[0, 0].reshape(384, D))
        for other in range(1, LINE):
            d_low = d_low + dot_nn(
                d_got[block_id, other], w_back[other // 2, other % 2].reshape(384, D)
            )
        centered, scale = norm_parts(states[block_id])
        normed = centered * scale
        sums[1:2, :] += jnp.sum(d_low * normed, axis=0, keepdims=True)
        lifted = d_low * gain
        grad_in[...] = gate * grad_out + scale * (
            lifted
            - jnp.mean(lifted, axis=-1, keepdims=True)
            - normed * jnp.mean(lifted * normed, axis=-1, keepdims=True)
        )
        return 0

    lax.fori_loop(0, 4, one_block, 0)
    d_start[...] = grad_in[...]

    def drain(block_id, _):
        for slot, (other, seq_to, rank_to) in enumerate(peers):
            mixed_copy(block_id, slot, head, other, seq_to, rank_to).wait_send()
            grads_copy(block_id, slot, head, other, seq_to, rank_to).wait_send()
        return 0

    lax.fori_loop(0, 4, drain, 0)
    for _ in plane_steps:
        pass
    for which in range(2):
        rows = pl.ds(128 * which, 128)
        tokens_out[which] = to_low(hidden[which] + total[rows, :])
    out_part[...] = to_low(total[256:384, :])
    loads[1].wait()
    aside(beside, place // 2).wait_send()
    aside(place, 1 - place // 2).wait_recv()


def backward_chain(
    scal, qkv, d_o, lse_tok, qkvst, lse_st, state_rows, begin, cots, back, kept, vecs, bias,
    extra, hidden,
):
    low, wide = jnp.bfloat16, jnp.float32
    shapes = (
        ((4, BLOCK, 384), low),
        ((4, STATES, 384), low),
        ((4, 64, D), low),
        ((64, D), wide),
        ((8, D), wide),
        ((BLOCK, 2 * BLOCK), wide),
        ((2, 128, D), wide),
        ((2, 128, D), low),
        ((128, D), low),
    )
    return pl.pallas_call(
        backward_kernel,
        out_shape=[jax.ShapeDtypeStruct(*one) for one in shapes],
        in_specs=[pl.BlockSpec(memory_space=pltpu.SMEM)]
        + vmem_specs(5)
        + any_specs(1)
        + vmem_specs(2)
        + any_specs(2)
        + vmem_specs(2)
        + any_specs(1)
        + vmem_specs(1),
        out_specs=vmem_specs(6) + any_specs(1) + vmem_specs(2),
        scratch_shapes=[
            pltpu.VMEM((4, BLOCK, 128), wide),
            pltpu.VMEM((4, BLOCK, 128), wide),
            pltpu.VMEM((STATES, 128), wide),
            pltpu.VMEM((STATES, 128), wide),
            pltpu.VMEM((4, 64, D), low),
            pltpu.VMEM((4, STATES, 128), low),
            pltpu.VMEM((4, LINE, 64, 384), low),
            pltpu.VMEM((64, D), wide),
            pltpu.VMEM((5, 64, D), wide),
            pltpu.VMEM((4, 2, 3, 4, 32, D), low),
            pltpu.VMEM((4, 8, 32, D), low),
            pltpu.VMEM((8, 384, D), low),
            pltpu.VMEM((4, 384, D), low),
            pltpu.VMEM((4, 192, D), low),
            pltpu.VMEM((2, 192, D), low),
            pltpu.VMEM((384, D), wide),
            pltpu.SemaphoreType.DMA((2, 4, LINE - 1)),
            pltpu.SemaphoreType.DMA((2, 4, LINE)),
            pltpu.SemaphoreType.DMA((5,)),
            pltpu.SemaphoreType.DMA((2,)),
            pltpu.SemaphoreType.DMA((10,)),
            pltpu.SemaphoreType.DMA((10,)),
        ],
        compiler_params=pltpu.CompilerParams(
            collective_id=2, has_side_effects=True, vmem_limit_bytes=VMEM_LIMIT
        ),
        cost_estimate=pl.CostEstimate(flops=40000000000, bytes_accessed=40000000, transcendentals=0),
        name="backward_chain",
    )(
        scal, qkv, d_o, lse_tok, qkvst, lse_st, state_rows, begin, cots, back, kept, vecs, bias,
        extra, hidden,
    )


def plane_place():
    place, half, rank = line_place()
    side = lax.axis_index("dp")
    return side, place, half, rank


def plane_index(side, place):
    return 4 * side + place


def plane_gather(buf, rows, send_sem, recv_sem):
    side, place, half, rank = plane_place()
    across, beside = 1 - side, lax.rem(place + 2, 4)
    core = place + 1 - 2 * half
    me = plane_index(side, place)
    at_x, at_y = plane_index(across, place), plane_index(side, beside)
    at_d = plane_index(across, beside)
    to_x = {"dp": across}
    to_y = {"seq": beside}
    to_c = {"seq": core}
    size = rows // 2

    def piece(owner, part, slot, target):
        view = buf.at[owner, pl.ds(part * size, size), :]
        return pltpu.make_async_remote_copy(
            src_ref=view,
            dst_ref=view,
            send_sem=send_sem.at[slot],
            recv_sem=recv_sem.at[owner, part],
            device_id=target,
            device_id_type=MESH_ID,
        )

    sent = []

    def send(owner, part, target):
        one = piece(owner, part, len(sent), target)
        sent.append(one)
        one.start()

    def arrived(owner, part):
        piece(owner, part, 0, to_c).wait_recv()

    send(me, 0, to_x)
    send(me, 1, to_y)
    send(me, 1, to_x)
    send(me, 0, to_y)
    send(me, 0, to_c)
    send(me, 1, to_c)
    yield
    arrived(at_x, 0)
    send(at_x, 0, to_y)
    arrived(at_y, 1)
    send(at_y, 1, to_x)
    send(at_x, 0, to_c)
    send(at_y, 1, to_c)
    yield
    arrived(at_x, 1)
    send(at_x, 1, to_c)
    arrived(at_y, 0)
    send(at_y, 0, to_c)
    yield
    arrived(at_d, 0)
    send(at_d, 0, to_c)
    arrived(at_d, 1)
    send(at_d, 1, to_c)
    yield
    for owner in (
        plane_index(side, core),
        plane_index(across, core),
        plane_index(side, lax.rem(core + 2, 4)),
        plane_index(across, lax.rem(core + 2, 4)),
    ):
        arrived(owner, 0)
        arrived(owner, 1)
    for one in sent:
        one.wait_send()


def run_all(*steps):
    waiting = list(steps)
    while waiting:
        for one in list(waiting):
            try:
                next(one)
            except StopIteration:
                waiting.remove(one)


def plane_scatter(part, core_got, near_got, far_got, total, rows, send_sem, recv_sem):
    side, place, half, rank = plane_place()
    across, beside = 1 - side, lax.rem(place + 2, 4)
    core = place + 1 - 2 * half
    me = plane_index(side, place)
    at_x, at_y = plane_index(across, place), plane_index(side, beside)
    at_d = plane_index(across, beside)
    size = rows // 2
    halves = (pl.ds(0, size), pl.ds(size, size))

    def moved(source, target_ref, slot, target):
        return pltpu.make_async_remote_copy(
            src_ref=source,
            dst_ref=target_ref,
            send_sem=send_sem.at[slot],
            recv_sem=recv_sem.at[slot],
            device_id=target,
            device_id_type=MESH_ID,
        )

    order = (at_d, at_x, at_y, me)
    swapped = (
        plane_index(across, lax.rem(core + 2, 4)),
        plane_index(across, core),
        plane_index(side, lax.rem(core + 2, 4)),
        plane_index(side, core),
    )
    def add_into(owner, view, other):
        part[owner, view, :] = to_low(
            part[owner, view, :].astype(jnp.float32) + other.astype(jnp.float32)
        )

    near = [
        moved(part.at[at_d, halves[0], :], near_got.at[0], 4, {"dp": across}),
        moved(part.at[at_d, halves[1], :], near_got.at[1], 5, {"seq": beside}),
        moved(part.at[at_x, halves[0], :], near_got.at[2], 6, {"dp": across}),
        moved(part.at[at_y, halves[1], :], near_got.at[3], 7, {"seq": beside}),
    ]
    first = [
        moved(part.at[owner], core_got.at[slot], slot, {"seq": core})
        for slot, owner in enumerate(swapped)
    ]
    far = [
        moved(part.at[at_y, halves[0], :], far_got.at[0], 8, {"seq": beside}),
        moved(part.at[at_x, halves[1], :], far_got.at[1], 9, {"dp": across}),
    ]
    yield
    for one in first:
        one.start()
    for slot, owner in enumerate(order):
        first[slot].wait_recv()
        for view in halves:
            add_into(owner, view, core_got[slot, view, :])
        if slot == 0:
            near[0].start()
            near[1].start()
        if slot == 1:
            near[2].start()
        if slot == 2:
            near[3].start()
    yield
    near[0].wait_recv()
    add_into(at_y, halves[0], near_got[0])
    far[0].start()
    near[1].wait_recv()
    add_into(at_x, halves[1], near_got[1])
    far[1].start()
    yield
    near[2].wait_recv()
    add_into(me, halves[0], near_got[2])
    near[3].wait_recv()
    add_into(me, halves[1], near_got[3])
    yield
    for slot, view in enumerate(halves):
        far[slot].wait_recv()
        total[view, :] = part[me, view, :].astype(jnp.float32) + far_got[slot].astype(jnp.float32)
    for one in first + near + far:
        one.wait_send()


def group_peers():
    place, half, rank = line_place()
    here = 4 * place + rank
    peers = []
    for step in range(1, 16):
        other = lax.rem(here + step, 16)
        peers.append((other, other // 4, lax.rem(other, 4)))
    return here, peers


def greet(peers):
    side = lax.axis_index("dp")
    barrier = pltpu.get_barrier_semaphore()
    for _, seq_to, rank_to in peers:
        pl.semaphore_signal(
            barrier, inc=1, device_id={"seq": seq_to, "tensor": rank_to}, device_id_type=MESH_ID
        )
    pl.semaphore_signal(barrier, inc=1, device_id={"dp": 1 - side}, device_id_type=MESH_ID)
    pl.semaphore_wait(barrier, len(peers) + 1)


def middle_kernel(
    mixed, tokens, kept, spread, cot_hbm, vecs,
    hidden, d_hidden, d_line, sums, extra, ff_grads,
    mixed_rows, mid_all, gl_all, dpre_all, work, core_got, near_got, far_got, total, d_rows,
    d_low, w_out, up, down, cot_all,
    send_sem, recv_sem, ring_send, ring_recv, sum_send, sum_recv, back_send, back_recv, local_sem,
):
    low, wide = jnp.bfloat16, jnp.float32
    side, place, half, rank = plane_place()
    mine = place // 2
    head = 2 * rank + half
    across, beside = 1 - side, lax.rem(place + 2, 4)
    core = place + 1 - 2 * half
    core_beside = lax.rem(core + 2, 4)
    me = plane_index(side, place)
    at_x, at_y = plane_index(across, place), plane_index(side, beside)
    at_d = plane_index(across, beside)
    me_c, x_c = plane_index(side, core), plane_index(across, core)
    y_c, d_c = plane_index(side, core_beside), plane_index(across, core_beside)
    to_x, to_y, to_c = {"dp": across}, {"seq": beside}, {"seq": core}
    here, peers = group_peers()
    fetch_pieces(kept, 48, 32, w_out, local_sem.at[0])
    ff_own = up.shape[1]
    first = spread.shape[1] - 2 * ff_own
    loads = [
        pltpu.make_async_copy(spread.at[:, pl.ds(first, ff_own), :], up, local_sem.at[1]),
        pltpu.make_async_copy(spread.at[:, pl.ds(first + ff_own, ff_own), :], down, local_sem.at[2]),
        pltpu.make_async_copy(cot_hbm, cot_all, local_sem.at[3]),
    ]
    for one in loads:
        one.start()
    greet(peers)

    def rows_copy(slot, sender, seq_from, rank_from, seq_to, rank_to):
        return pltpu.make_async_remote_copy(
            src_ref=mixed.at[seq_to, span(rank_to, 128), :],
            dst_ref=mixed_rows.at[
                seq_from // 2, :, span(2 * rank_from + lax.rem(seq_from, 2), 128)
            ],
            send_sem=send_sem.at[slot],
            recv_sem=recv_sem.at[sender],
            device_id={"seq": seq_to, "tensor": rank_to},
            device_id_type=MESH_ID,
        )

    for slot, (_, seq_to, rank_to) in enumerate(peers):
        rows_copy(slot, here, place, rank, seq_to, rank_to).start()
    mixed_rows[mine, :, span(head, 128)] = mixed[place, span(rank, 128), :]
    fetched(w_out, local_sem.at[0])
    for slot, (other, seq_to, rank_to) in enumerate(peers):
        rows_copy(slot, other, seq_to, rank_to, seq_to, rank_to).wait_recv()
    gain = vecs[2:3, :]

    def project(which, _):
        added = dot_nn(mixed_rows[which], w_out[...].reshape(D, D)) + tokens[which].astype(wide)
        hidden[which] = added
        centered, scale = norm_parts(added)
        mid_all[me, span(which, 128), :] = to_low(centered * scale * gain)
        return 0

    lax.fori_loop(0, 2, project, 0)

    def piece(owner, part, slot, target):
        view = mid_all.at[owner, pl.ds(part * 128, 128), :]
        return pltpu.make_async_remote_copy(
            src_ref=view,
            dst_ref=view,
            send_sem=ring_send.at[slot],
            recv_sem=ring_recv.at[owner, part],
            device_id=target,
            device_id_type=MESH_ID,
        )

    own = [
        piece(me, 0, 0, to_x), piece(me, 1, 1, to_y), piece(me, 1, 2, to_x), piece(me, 0, 3, to_y),
        piece(me, 0, 4, to_c), piece(me, 1, 5, to_c),
    ]
    on_x0, on_y1 = piece(at_x, 0, 6, to_y), piece(at_y, 1, 7, to_x)
    to_core = [
        piece(at_x, 0, 8, to_c), piece(at_y, 1, 9, to_c), piece(at_x, 1, 10, to_c),
        piece(at_y, 0, 11, to_c), piece(at_d, 0, 12, to_c), piece(at_d, 1, 13, to_c),
    ]
    wait_of = {
        (name, part): piece(owner, part, 0, to_c)
        for name, owner in (
            ("x", at_x), ("y", at_y), ("d", at_d), ("mc", me_c), ("xc", x_c), ("yc", y_c), ("dc", d_c)
        )
        for part in (0, 1)
    }

    def moved(source, target_ref, slot, target):
        return pltpu.make_async_remote_copy(
            src_ref=source,
            dst_ref=target_ref,
            send_sem=sum_send.at[slot],
            recv_sem=sum_recv.at[slot],
            device_id=target,
            device_id_type=MESH_ID,
        )

    views = (pl.ds(0, 128), pl.ds(128, 128))
    swap = [
        moved(work.at[owner], core_got.at[slot], slot, to_c)
        for slot, owner in enumerate((d_c, x_c, y_c, me_c))
    ]
    near = [
        moved(work.at[at_d, views[0], :], near_got.at[0], 4, to_x),
        moved(work.at[at_d, views[1], :], near_got.at[1], 5, to_y),
        moved(work.at[at_x, views[0], :], near_got.at[2], 6, to_x),
        moved(work.at[at_y, views[1], :], near_got.at[3], 7, to_y),
    ]
    far = [
        moved(work.at[at_y, views[0], :], far_got.at[0], 8, to_y),
        moved(work.at[at_x, views[1], :], far_got.at[1], 9, to_x),
    ]

    def add_into(owner, view, other):
        work[owner, view, :] = to_low(work[owner, view, :].astype(wide) + other.astype(wide))

    def add_core(slot, owner):
        swap[slot].wait_recv()
        for view in views:
            add_into(owner, view, core_got[slot, view, :])

    for one in own:
        one.start()
    loads[0].wait()
    loads[1].wait()
    loads[2].wait()
    owners = (me, me_c, at_x, at_y, x_c, y_c, at_d, d_c)

    def one_chunk(turn, _):
        @pl.when(turn == 1)
        def _():
            wait_of["mc", 0].wait_recv()
            wait_of["mc", 1].wait_recv()

        @pl.when(turn == 2)
        def _():
            swap[3].start()
            wait_of["x", 0].wait_recv()
            on_x0.start()
            wait_of["y", 1].wait_recv()
            on_y1.start()
            to_core[0].start()
            to_core[1].start()
            wait_of["x", 1].wait_recv()
            to_core[2].start()
            wait_of["y", 0].wait_recv()
            to_core[3].start()

        @pl.when(turn == 4)
        def _():
            wait_of["xc", 0].wait_recv()
            wait_of["xc", 1].wait_recv()

        @pl.when(turn == 5)
        def _():
            swap[1].start()
            wait_of["yc", 0].wait_recv()
            wait_of["yc", 1].wait_recv()

        @pl.when(turn == 6)
        def _():
            swap[2].start()
            wait_of["d", 0].wait_recv()
            to_core[4].start()
            wait_of["d", 1].wait_recv()
            to_core[5].start()
            add_core(1, at_x)
            near[2].start()
            add_core(2, at_y)
            near[3].start()

        @pl.when(turn == 7)
        def _():
            wait_of["dc", 0].wait_recv()
            wait_of["dc", 1].wait_recv()

        owner = owners[7]
        for index in range(7):
            owner = jnp.where(turn == index, owners[index], owner)
        up_rows = up[...].reshape(4 * ff_own, D)
        down_rows = down[...].reshape(4 * ff_own, D)

        def part(which, _):
            rows = span(which, 128)
            pre = dot_nt(mid_all[owner, rows, :], up_rows)
            square = pre * pre
            bend = jnp.tanh(GELU_SCALE * (pre + 0.044715 * (pre * square)))
            gl_all[owner, rows, :] = to_low(0.5 * pre * (1.0 + bend))
            slope = 0.5 * (1.0 + bend) + 0.5 * pre * (1.0 - bend * bend) * (
                GELU_SCALE * (1.0 + 3.0 * 0.044715 * square)
            )
            grad = to_low(dot_nt(cot_all[owner, rows, :], down_rows) * slope)
            dpre_all[owner, rows, :] = grad
            work[owner, rows, :] = to_low(dot_nn(grad, up_rows))
            return 0

        lax.fori_loop(0, 2, part, 0)
        return 0

    lax.fori_loop(0, 8, one_chunk, 0)
    swap[0].start()
    add_core(0, at_d)
    near[0].start()
    near[1].start()
    add_core(3, me)

    def grads(index, _):
        quarter, kind = index // 2, lax.rem(index, 2)
        columns = span(quarter, 128)

        @pl.when(kind == 0)
        def _():
            def add(owner, acc):
                return acc + dot_tn(dpre_all[owner, :, columns], mid_all[owner])

            ff_grads[quarter, 0] = to_low(lax.fori_loop(0, 8, add, jnp.zeros((128, D), wide)))

        @pl.when(kind == 1)
        def _():
            def add(owner, acc):
                return acc + dot_tn(gl_all[owner, :, columns], cot_all[owner])

            ff_grads[quarter, 1] = to_low(lax.fori_loop(0, 8, add, jnp.zeros((128, D), wide)))

        return 0

    lax.fori_loop(0, 8, grads, 0)
    near[0].wait_recv()
    add_into(at_y, views[0], near_got[0])
    far[0].start()
    near[1].wait_recv()
    add_into(at_x, views[1], near_got[1])
    far[1].start()
    near[2].wait_recv()
    add_into(me, views[0], near_got[2])
    near[3].wait_recv()
    add_into(me, views[1], near_got[3])

    def outward(owner, _):
        down_rows = down[...].reshape(4 * ff_own, D)
        for which in range(2):
            rows = pl.ds(128 * which, 128)
            extra[owner, rows, :] = to_low(dot_nn(gl_all[owner, rows, :], down_rows))
        return 0

    lax.fori_loop(0, 8, outward, 0)
    for slot, view in enumerate(views):
        far[slot].wait_recv()
        total[view, :] = work[me, view, :].astype(wide) + far_got[slot].astype(wide)
    sums[...] = jnp.zeros_like(sums)

    def back(which, _):
        rows = span(which, 128)
        grad = total[rows, :]
        centered, scale = norm_parts(hidden[which])
        normed = centered * scale
        sums[0:1, :] += jnp.sum(grad * normed, axis=0, keepdims=True)
        lifted = grad * gain
        row_grad = cot_all[me, rows, :].astype(wide) + scale * (
            lifted
            - jnp.mean(lifted, axis=-1, keepdims=True)
            - normed * jnp.mean(lifted * normed, axis=-1, keepdims=True)
        )
        d_hidden[which] = row_grad
        d_low[which] = to_low(row_grad)
        d_rows[which] = to_low(dot_nt(to_low(row_grad), w_out[...].reshape(D, D)))
        return 0

    lax.fori_loop(0, 2, back, 0)

    def line_copy(slot, sender, seq_from, rank_from, seq_to, rank_to):
        return pltpu.make_async_remote_copy(
            src_ref=d_rows.at[seq_to // 2, :, span(2 * rank_to + lax.rem(seq_to, 2), 128)],
            dst_ref=d_line.at[seq_from, span(rank_from, 128), :],
            send_sem=back_send.at[slot],
            recv_sem=back_recv.at[sender],
            device_id={"seq": seq_to, "tensor": rank_to},
            device_id_type=MESH_ID,
        )

    for slot, (_, seq_to, rank_to) in enumerate(peers):
        line_copy(slot, here, place, rank, seq_to, rank_to).start()
    d_line[place, span(rank, 128), :] = d_rows[mine, :, span(head, 128)]
    for index in range(LINE):
        columns = pl.ds(128 * index, 128)
        part = dot_tn(mixed_rows[0, :, columns], d_low[0]) + dot_tn(
            mixed_rows[1, :, columns], d_low[1]
        )
        part = to_low(part)
        for block in range(4):
            extra[
                4 * (index % 2) + block, 256 + 32 * (index // 2) : 288 + 32 * (index // 2), :
            ] = part[32 * block : 32 * block + 32, :]
    for slot, (other, seq_to, rank_to) in enumerate(peers):
        line_copy(slot, other, seq_to, rank_to, seq_to, rank_to).wait_recv()
    for slot, (_, seq_to, rank_to) in enumerate(peers):
        rows_copy(slot, here, place, rank, seq_to, rank_to).wait_send()
        line_copy(slot, here, place, rank, seq_to, rank_to).wait_send()
    for one in own + [on_x0, on_y1] + to_core + swap + near + far:
        one.wait_send()


GELU_SCALE = 0.7978845608028654


def middle(mixed, tokens, kept, spread, cot_all, vecs):
    low, wide = jnp.bfloat16, jnp.float32
    ff_own = (spread.shape[1] - SPREAD_FIRST) // 2
    shapes = (
        ((2, 128, D), wide),
        ((2, 128, D), wide),
        ((4, BLOCK, 128), low),
        ((8, D), wide),
        ((8, 384, D), low),
        ((4, 2, ff_own, D), low),
    )
    dma = pltpu.SemaphoreType.DMA
    return pl.pallas_call(
        middle_kernel,
        out_shape=[jax.ShapeDtypeStruct(*one) for one in shapes],
        in_specs=vmem_specs(2) + any_specs(3) + vmem_specs(1),
        out_specs=vmem_specs(6),
        scratch_shapes=[
            pltpu.VMEM((2, 128, D), low),
            pltpu.VMEM((8, 256, D), low),
            pltpu.VMEM((8, 256, 4 * ff_own), low),
            pltpu.VMEM((8, 256, 4 * ff_own), low),
            pltpu.VMEM((8, 256, D), low),
            pltpu.VMEM((4, 256, D), low),
            pltpu.VMEM((4, 128, D), low),
            pltpu.VMEM((2, 128, D), low),
            pltpu.VMEM((256, D), wide),
            pltpu.VMEM((2, 128, D), low),
            pltpu.VMEM((2, 128, D), low),
            pltpu.VMEM((4, 8, 32, D), low),
            pltpu.VMEM((4, ff_own, D), low),
            pltpu.VMEM((4, ff_own, D), low),
            pltpu.VMEM((8, 256, D), low),
            dma((15,)), dma((16,)), dma((14,)), dma((8, 2)), dma((10,)), dma((10,)), dma((15,)),
            dma((16,)), dma((4,)),
        ],
        compiler_params=pltpu.CompilerParams(
            collective_id=3, has_side_effects=True, vmem_limit_bytes=VMEM_LIMIT
        ),
        cost_estimate=pl.CostEstimate(
            flops=60000000000, bytes_accessed=60000000, transcendentals=0
        ),
        name="middle",
    )(mixed, tokens, kept, spread, cot_all, vecs)


SPREAD_FIRST = 96


WIDE = 2048


def opening_kernel(
    tokens, w_qkv, piece, vecs, line,
    rows_all, qkv, kept, table,
    stage, send_sem, core_sem, recv_sem, piece_send, piece_recv, ring_send, ring_recv,
):
    side, place, half, rank = plane_place()
    mine = place // 2
    core = place + 1 - 2 * half
    other = lax.rem(place + 2, 4)
    me = plane_index(side, place)
    extra = piece.shape[0]
    barrier = pltpu.get_barrier_semaphore()
    greeted = [{"tensor": lax.rem(rank + step, 4)} for step in (1, 2, 3)]
    greeted += [{"seq": core}, {"seq": other}, {"dp": 1 - side}]
    for target in greeted:
        pl.semaphore_signal(barrier, inc=1, device_id=target, device_id_type=MESH_ID)
    gain = vecs[3:4, :]

    def normed(which):
        centered, scale = norm_parts(tokens[which].astype(jnp.float32))
        return to_low(centered * scale * gain)

    def moved(block_id, origin, sem, target):
        view = rows_all.at[block_id, span(origin, 128), :]
        return pltpu.make_async_remote_copy(
            src_ref=view,
            dst_ref=view,
            send_sem=sem,
            recv_sem=recv_sem.at[block_id, origin],
            device_id=target,
            device_id_type=MESH_ID,
        )

    stage[...] = normed(1 - mine)
    kept[me, span(rank, extra), :] = piece[...]
    pl.semaphore_wait(barrier, 6)
    aside = pltpu.make_async_remote_copy(
        src_ref=stage,
        dst_ref=rows_all.at[place, span(rank, 128), :],
        send_sem=send_sem.at[0, 0, 3],
        recv_sem=recv_sem.at[place, rank],
        device_id={"seq": other},
        device_id_type=MESH_ID,
    )
    aside.start()
    rows_all[place, span(rank, 128), :] = normed(mine)
    right, left = {"tensor": lax.rem(rank + 1, 4)}, {"tensor": lax.rem(rank + 3, 4)}
    blocks = (place, other)

    def pass_on(which, distance):
        block_id = blocks[which]

        @pl.when((rank < 3) & (rank >= distance))
        def _():
            moved(block_id, jnp.maximum(rank - distance, 0), send_sem.at[which, distance, 0], right).start()

        @pl.when((rank > 0) & (rank + distance <= 3))
        def _():
            moved(block_id, jnp.minimum(rank + distance, 3), send_sem.at[which, distance, 1], left).start()

    def pass_done(which, distance):
        block_id = blocks[which]

        @pl.when((rank < 3) & (rank >= distance))
        def _():
            moved(block_id, jnp.maximum(rank - distance, 0), send_sem.at[which, distance, 0], right).wait_send()

        @pl.when((rank > 0) & (rank + distance <= 3))
        def _():
            moved(block_id, jnp.minimum(rank + distance, 3), send_sem.at[which, distance, 1], left).wait_send()

    def project(block_id, origin):
        view = span(origin, 128)
        qkv[block_id, view, :] = to_low(dot_nn(rows_all[block_id, view, :], w_qkv[...]))

    def rows_steps():
        pass_on(0, 0)
        moved(place, rank, core_sem.at[0, rank], {"seq": core}).start()
        project(place, rank)
        moved(other, rank, send_sem.at[0, 0, 3], {"seq": other}).wait_recv()
        pass_on(1, 0)
        moved(other, rank, core_sem.at[1, rank], {"seq": core}).start()
        project(other, rank)
        yield
        for distance in (1, 2, 3):
            for which in (0, 1):
                block_id = blocks[which]
                for way, ok, origin in (
                    (0, rank >= distance, jnp.maximum(rank - distance, 0)),
                    (1, rank + distance <= 3, jnp.minimum(rank + distance, 3)),
                ):

                    @pl.when(ok)
                    def _():
                        moved(block_id, origin, send_sem.at[which, distance, way], right).wait_recv()
                        if distance < 3:
                            if way == 0:

                                @pl.when(rank < 3)
                                def _():
                                    moved(
                                        block_id, origin, send_sem.at[which, distance, 0], right
                                    ).start()

                            else:

                                @pl.when(rank > 0)
                                def _():
                                    moved(
                                        block_id, origin, send_sem.at[which, distance, 1], left
                                    ).start()

                        moved(block_id, origin, core_sem.at[which, origin], {"seq": core}).start()
                        project(block_id, origin)

                yield
        for which, block_id in enumerate((core, lax.rem(core + 2, 4))):
            for origin in range(4):
                moved(block_id, origin, core_sem.at[which, origin], {"seq": core}).wait_recv()
                project(block_id, origin)
        for which in (0, 1):
            for distance in (0, 1, 2):
                pass_done(which, distance)
            for origin in range(4):
                moved(blocks[which], origin, core_sem.at[which, origin], {"seq": core}).wait_send()

    def piece_move(slot, origin, target):
        view = kept.at[me, span(origin, extra), :]
        return pltpu.make_async_remote_copy(
            src_ref=view,
            dst_ref=view,
            send_sem=piece_send.at[slot],
            recv_sem=piece_recv.at[origin],
            device_id=target,
            device_id_type=MESH_ID,
        )

    def piece_steps():
        for slot in range(3):
            piece_move(slot, rank, greeted[slot]).start()
        first = line[...]
        row = lax.broadcasted_iota(jnp.int32, (8, WIDE), 0)
        for step in (1, 2, 4):
            first = jnp.where(row // step % 2 == 1, pltpu.roll(first, step, 1), first)

        def one(group, _):
            table[span(group, 8), :] = pltpu.roll(first, 8 * group, 1)[:, 0 : 2 * BLOCK]
            return 0

        lax.fori_loop(0, BLOCK // 8, one, 0)
        yield
        for slot in range(3):
            piece_move(slot, lax.rem(rank + slot + 1, 4), greeted[slot]).wait_recv()
        for _ in plane_gather(kept, 4 * extra, ring_send, ring_recv):
            yield
        for slot in range(3):
            piece_move(slot, rank, greeted[slot]).wait_send()

    run_all(rows_steps(), piece_steps())
    aside.wait_send()


def opening(tokens, w_qkv, piece, vecs, line):
    low, wide = jnp.bfloat16, jnp.float32
    extra = piece.shape[0]
    shapes = (
        ((4, BLOCK, D), low),
        ((4, BLOCK, 384), low),
        ((8, 4 * extra, D), low),
        ((BLOCK, 2 * BLOCK), wide),
    )
    return pl.pallas_call(
        opening_kernel,
        out_shape=[jax.ShapeDtypeStruct(*one) for one in shapes],
        in_specs=vmem_specs(5),
        out_specs=vmem_specs(4),
        scratch_shapes=[
            pltpu.VMEM((128, D), low),
            pltpu.SemaphoreType.DMA((2, 4, 4)),
            pltpu.SemaphoreType.DMA((2, 4)),
            pltpu.SemaphoreType.DMA((4, 4)),
            pltpu.SemaphoreType.DMA((3,)),
            pltpu.SemaphoreType.DMA((4,)),
            pltpu.SemaphoreType.DMA((16,)),
            pltpu.SemaphoreType.DMA((8, 2)),
        ],
        compiler_params=pltpu.CompilerParams(
            collective_id=5, has_side_effects=True, vmem_limit_bytes=VMEM_LIMIT
        ),
        cost_estimate=pl.CostEstimate(
            flops=30000000000, bytes_accessed=30000000, transcendentals=0
        ),
        name="opening",
    )(tokens, w_qkv, piece, vecs, line)


def pair_sum(part, near_got, far_got, result, rows, send_sem, recv_sem):
    side, place, half, rank = plane_place()
    mine = place // 2
    across, beside = 1 - side, 1 - mine
    me = 2 * side + mine
    at_x, at_y, at_d = 2 * across + mine, 2 * side + beside, 2 * across + beside
    to_x, to_y = {"dp": across}, {"seq": lax.rem(place + 2, 4)}
    size = rows // 2
    views = (pl.ds(0, size), pl.ds(size, size))

    def moved(source, target_ref, slot, target):
        return pltpu.make_async_remote_copy(
            src_ref=source,
            dst_ref=target_ref,
            send_sem=send_sem.at[slot],
            recv_sem=recv_sem.at[slot],
            device_id=target,
            device_id_type=MESH_ID,
        )

    def add_into(owner, view, other):
        part[owner, view, :] = to_low(
            part[owner, view, :].astype(jnp.float32) + other.astype(jnp.float32)
        )

    near = [
        moved(part.at[at_d, views[0], :], near_got.at[0], 0, to_x),
        moved(part.at[at_d, views[1], :], near_got.at[1], 1, to_y),
        moved(part.at[at_x, views[0], :], near_got.at[2], 2, to_x),
        moved(part.at[at_y, views[1], :], near_got.at[3], 3, to_y),
    ]
    for one in near:
        one.start()
    yield
    near[0].wait_recv()
    add_into(at_y, views[0], near_got[0])
    far = [
        moved(part.at[at_y, views[0], :], far_got.at[0], 4, to_y),
        moved(part.at[at_x, views[1], :], far_got.at[1], 5, to_x),
    ]
    far[0].start()
    near[1].wait_recv()
    add_into(at_x, views[1], near_got[1])
    far[1].start()
    yield
    near[2].wait_recv()
    add_into(me, views[0], near_got[2])
    near[3].wait_recv()
    add_into(me, views[1], near_got[3])
    for slot, view in enumerate(views):
        far[slot].wait_recv()
        result[me, view, :] = to_low(
            part[me, view, :].astype(jnp.float32) + far_got[slot].astype(jnp.float32)
        )

    def given(owner, which, slot, target):
        view = result.at[owner, views[which], :]
        return moved(view, view, slot, target)

    own = [
        given(me, 0, 6, to_x),
        given(me, 1, 7, to_y),
        given(me, 1, 8, to_x),
        given(me, 0, 9, to_y),
    ]
    for one in own:
        one.start()
    yield
    given(at_x, 0, 6, to_x).wait_recv()
    last = [given(at_x, 0, 10, to_y), given(at_y, 1, 11, to_x)]
    last[0].start()
    given(at_y, 1, 7, to_y).wait_recv()
    last[1].start()
    yield
    given(at_x, 1, 8, to_x).wait_recv()
    given(at_y, 0, 9, to_y).wait_recv()
    given(at_d, 0, 10, to_y).wait_recv()
    given(at_d, 1, 11, to_x).wait_recv()
    for one in near + far + own + last:
        one.wait_send()


PAIR_ROWS = 640


def closing_kernel(
    d_qkv, w_qkv, tokens, d_hidden, vecs, rows_hbm, low_hbm, d_qkvst_hbm, os_hbm, du_hbm,
    d_start, dz_hbm, small, out_part,
    inputs_grad, pair_out, sout_out, small_out,
    rows_all, state_low, d_qkvst, os_rows, du_rows, dz_sum,
    leave, came, sums, got, final, cross, cross_got,
    pair_part, pair_near, pair_far,
    work, core_got, near_got, far_got, total, z_part, z_got,
    diag, small_z, small_p,
    line_send, line_recv, way_send, way_recv, pair_send, pair_recv, core_sem,
    ring_send, ring_recv, zs_send, zs_recv, gather_send, gather_recv, small_send, small_recv, local_sem,
):
    loads = [
        pltpu.make_async_copy(source, target, local_sem.at[slot])
        for slot, (source, target) in enumerate(
            (
                (rows_hbm, rows_all),
                (d_qkvst_hbm, d_qkvst),
                (low_hbm, state_low),
                (os_hbm, os_rows),
                (du_hbm, du_rows),
                (dz_hbm, dz_sum),
            )
        )
    ]
    for one in loads:
        one.start()
    side, place, half, rank = plane_place()
    mine = place // 2
    core = place + 1 - 2 * half
    other = lax.rem(place + 2, 4)
    me = plane_index(side, place)
    ranks = [lax.rem(rank + step, 4) for step in (1, 2, 3)]
    spots_of = [lax.rem(me + step, 8) for step in range(1, 8)]
    barrier = pltpu.get_barrier_semaphore()
    for target in ranks:
        pl.semaphore_signal(barrier, inc=1, device_id={"tensor": target}, device_id_type=MESH_ID)
    for target in spots_of:
        pl.semaphore_signal(
            barrier,
            inc=1,
            device_id={"dp": target // 4, "seq": lax.rem(target, 4)},
            device_id_type=MESH_ID,
        )
    gain = vecs[3:4, :]
    right, left = {"tensor": lax.rem(rank + 1, 4)}, {"tensor": lax.rem(rank + 3, 4)}

    def moved(source, target_ref, send, recv, target):
        return pltpu.make_async_remote_copy(
            src_ref=source,
            dst_ref=target_ref,
            send_sem=send,
            recv_sem=recv,
            device_id=target,
            device_id_type=MESH_ID,
        )

    def to_core(which):
        return moved(
            leave.at[which], came.at[which], line_send.at[which], line_recv.at[which], {"seq": core}
        )

    def crossing():
        return moved(cross, cross_got, line_send.at[2], line_recv.at[2], {"seq": other})

    near = rank // 2
    at_end = (rank == 0) | (rank == 3)

    def hop(way, which, target):
        return moved(
            sums.at[which, target],
            got.at[way, which, target],
            way_send.at[which, target],
            way_recv.at[way, which, target],
            {"tensor": lax.rem(rank + 5 - 2 * way, 4)},
        )

    def target_of(way, distance):
        return (1 - way) * (3 - distance) + way * distance

    def pass_first(which):
        @pl.when(at_end)
        def _():
            for distance in range(3):
                hop(near, which, target_of(near, distance)).start()

    def pass_on(way, which, distance):
        @pl.when(jnp.logical_not(at_end))
        def _():
            target = target_of(way, distance)
            hop(way, which, target).wait_recv()
            sums[which, target] = to_low(
                sums[which, target].astype(jnp.float32)
                + got[way, which, target].astype(jnp.float32)
            )
            hop(way, which, target).start()

    def finish(which):
        final[which] = sums[which, rank].astype(jnp.float32)

        @pl.when(rank > 0)
        def _():
            hop(0, which, rank).wait_recv()
            final[which] += got[0, which, rank].astype(jnp.float32)

        @pl.when(rank < 3)
        def _():
            hop(1, which, rank).wait_recv()
            final[which] += got[1, which, rank].astype(jnp.float32)

    def line_steps():
        for which, block_id in enumerate((lax.rem(core + 2, 4), core)):

            def partner(chunk, _):
                rows = span(chunk, ROWS)
                leave[which, rows, :] = to_low(dot_nt(d_qkv[block_id, rows, :], w_qkv[...]))
                return 0

            lax.fori_loop(0, CHUNKS, partner, 0)
            if which == 0:
                pl.semaphore_wait(barrier, 10)
            to_core(which).start()
        for which, block_id in enumerate((other, place)):
            to_core(which).wait_recv()

            def own(chunk, _):
                rows = span(chunk, ROWS)
                sums[which, chunk] = to_low(
                    dot_nt(d_qkv[block_id, rows, :], w_qkv[...])
                    + came[which, rows, :].astype(jnp.float32)
                )
                return 0

            lax.fori_loop(0, CHUNKS, own, 0)
            pass_first(which)
        yield
        for which in (0, 1):
            pass_on(near, which, 0)
            yield
            pass_on(near, which, 1)
            pass_on(1 - near, which, 0)
            yield
            finish(which)
            if which == 0:
                cross[...] = to_low(final[0])
                crossing().start()
            yield
        crossing().wait_recv()
        final[0] = cross_got[...].astype(jnp.float32)
        small_z[rank] = small[...]
        for which, row_set in ((1, mine), (0, 1 - mine)):
            grad = final[which]
            centered, scale = norm_parts(tokens[row_set].astype(jnp.float32))
            normed = centered * scale
            small_z[rank, 0:1, :] += jnp.sum(grad * normed, axis=0, keepdims=True)
            lifted = grad * gain
            inputs_grad[row_set] = d_hidden[row_set] + scale * (
                lifted
                - jnp.mean(lifted, axis=-1, keepdims=True)
                - normed * jnp.mean(lifted * normed, axis=-1, keepdims=True)
            )
        crossing().wait_send()
        for which in (0, 1):
            to_core(which).wait_send()
            for target in range(4):

                @pl.when(rank != target)
                def _():
                    hop(0, which, target).wait_send()

    def pair_steps():
        loads[0].wait()
        loads[1].wait()
        loads[2].wait()
        for chunk in range(4):
            if chunk < 3:
                first = 128 * chunk

                def one(block_id, acc):
                    acc = acc + dot_tn(d_qkv[block_id, :, first : first + 128], rows_all[block_id])
                    if chunk > 0:
                        acc = acc + dot_tn(
                            d_qkvst[block_id, :, first : first + 128], state_low[block_id]
                        )
                    return acc

            else:

                def one(block_id, acc):
                    return acc + dot_tn(d_qkvst[block_id, :, 0:128], state_low[block_id])

            acc = lax.fori_loop(0, 4, one, jnp.zeros((128, D), jnp.float32))
            low = to_low(acc)
            first = 128 * chunk
            while first < 128 * (chunk + 1):
                owner, inside = first // 160, first % 160
                size = min(160 - inside, 128 * (chunk + 1) - first)
                begin = first - 128 * chunk
                pair_part[owner, inside : inside + size, :] = low[begin : begin + size, :]
                first += size
        pair_part[3, 32:96, :] = to_low(d_start[...])
        pair_part[3, 96:160, :] = jnp.zeros((64, D), jnp.bfloat16)
        for _ in pair_sum(
            pair_part, pair_near, pair_far, pair_out.at[half], 160, pair_send, pair_recv
        ):
            yield
        full = moved(
            pair_out.at[half], pair_out.at[half], core_sem.at[0], core_sem.at[1], {"seq": core}
        )
        full.start()
        yield
        moved(
            pair_out.at[1 - half], pair_out.at[1 - half], core_sem.at[0], core_sem.at[1],
            {"seq": core},
        ).wait_recv()
        full.wait_send()

    def sout_steps():
        loads[3].wait()
        loads[4].wait()
        for head in range(LINE):
            low = to_low(dot_tn(os_rows[:, 128 * head : 128 * head + 128], du_rows[...]))
            for piece in range(4):
                work[
                    4 * (head % 2) + piece, 32 * (head // 2) : 32 * (head // 2) + 32, :
                ] = low[32 * piece : 32 * piece + 32, :]
        for _ in plane_scatter(
            work, core_got, near_got, far_got, total, 128, ring_send, ring_recv
        ):
            yield
        z_part[:, 0:32, :] = to_low(total[...]).reshape(4, 32, D)
        z_part[:, 32:64, :] = out_part[...].reshape(4, 32, D)
        out = [
            moved(
                z_part.at[target], z_got.at[rank], zs_send.at[slot], zs_recv.at[rank],
                {"tensor": target},
            )
            for slot, target in enumerate(ranks)
        ]
        for one in out:
            one.start()
        z_got[rank] = z_part[rank]
        yield
        for slot, target in enumerate(ranks):
            moved(
                z_part.at[target], z_got.at[target], zs_send.at[slot], zs_recv.at[target],
                {"tensor": target},
            ).wait_recv()
        acc = z_got[0].astype(jnp.float32)
        for target in range(1, 4):
            acc = acc + z_got[target].astype(jnp.float32)
        sout_out[me] = to_low(acc)
        for _ in plane_gather(sout_out, 64, gather_send, gather_recv):
            yield
        for one in out:
            one.wait_send()

    def diag_steps():
        loads[5].wait()
        diag[...] = jnp.zeros_like(diag)
        for part in range(4):

            def one(group, _):
                rows = dz_sum[span(group, 8), :]
                wide = jnp.concatenate(
                    [rows, jnp.zeros((8, WIDE - 2 * BLOCK), jnp.float32)], axis=1
                )
                diag[...] += pltpu.roll(wide, lax.rem(WIDE - 8 * group, WIDE), 1)
                return 0

            lax.fori_loop(16 * part, 16 * part + 16, one, 0)
            yield
        total_line = diag[...]
        row = lax.broadcasted_iota(jnp.int32, (8, WIDE), 0)
        for step in (1, 2, 4):
            total_line = jnp.where(
                row // step % 2 == 1, pltpu.roll(total_line, WIDE - step, 1), total_line
            )
        lane = lax.broadcasted_iota(jnp.int32, (8, WIDE), 1)
        offset = jnp.where(lane >= WIDE - BLOCK, lane - WIDE - BLOCK, lane - BLOCK)
        bucket_ids = bucket_of(offset)
        spot = lax.broadcasted_iota(jnp.int32, (1, 256), 1) - BUCKETS * (2 * rank + half)
        placed = jnp.zeros((1, 256), jnp.float32)
        for bucket_id in range(BUCKETS):
            chosen = jnp.where(bucket_ids == bucket_id, total_line, 0.0)
            value = jnp.sum(jnp.sum(chosen, axis=0, keepdims=True), axis=1, keepdims=True)
            placed = jnp.where(spot == bucket_id, value, placed)
        diag[0:1, 0:256] = placed

    extra = sout_steps()
    run_all(line_steps(), pair_steps(), extra, diag_steps(), extra)
    small_z[rank, 4:5, 0:256] = diag[0:1, 0:256]

    def small_over_z(slot, sender, target):
        return moved(
            small_z.at[sender], small_z.at[sender], small_send.at[slot], small_recv.at[sender],
            {"tensor": target},
        )

    for slot, target in enumerate(ranks):
        small_over_z(slot, rank, target).start()
    for slot, target in enumerate(ranks):
        small_over_z(slot, target, target).wait_recv()
    small_p[me] = small_z[0] + small_z[1] + small_z[2] + small_z[3]

    def small_over_plane(slot, sender, target):
        return moved(
            small_p.at[sender], small_p.at[sender], small_send.at[3 + slot],
            small_recv.at[4 + sender],
            {"dp": target // 4, "seq": lax.rem(target, 4)},
        )

    for slot, target in enumerate(spots_of):
        small_over_plane(slot, me, target).start()
    for slot, target in enumerate(spots_of):
        small_over_plane(slot, target, target).wait_recv()
    acc = small_p[0]
    for target in range(1, 8):
        acc = acc + small_p[target]
    small_out[...] = acc
    for slot, target in enumerate(ranks):
        small_over_z(slot, rank, target).wait_send()
    for slot, target in enumerate(spots_of):
        small_over_plane(slot, me, target).wait_send()


def closing(
    d_qkv, w_qkv, tokens, d_hidden, vecs, rows_all, state_low, d_qkvst, os_rows, du_rows,
    d_start, dz_sum, small, out_part,
):
    low, wide = jnp.bfloat16, jnp.float32
    shapes = (
        ((2, 128, D), wide),
        ((2, 4, PAIR_ROWS // 4, D), low),
        ((8, 64, D), low),
        ((8, D), wide),
    )
    dma = pltpu.SemaphoreType.DMA
    return pl.pallas_call(
        closing_kernel,
        out_shape=[jax.ShapeDtypeStruct(*one) for one in shapes],
        in_specs=vmem_specs(5) + any_specs(5) + vmem_specs(1) + any_specs(1) + vmem_specs(2),
        out_specs=vmem_specs(4),
        scratch_shapes=[
            pltpu.VMEM((4, BLOCK, D), low),
            pltpu.VMEM((4, BLOCK, D), low),
            pltpu.VMEM((4, BLOCK, 384), low),
            pltpu.VMEM((256, D), low),
            pltpu.VMEM((256, D), low),
            pltpu.VMEM((BLOCK, 2 * BLOCK), wide),
            pltpu.VMEM((2, BLOCK, D), low),
            pltpu.VMEM((2, BLOCK, D), low),
            pltpu.VMEM((2, 4, 128, D), low),
            pltpu.VMEM((2, 2, 4, 128, D), low),
            pltpu.VMEM((2, 128, D), wide),
            pltpu.VMEM((128, D), low),
            pltpu.VMEM((128, D), low),
            pltpu.VMEM((4, PAIR_ROWS // 4, D), low),
            pltpu.VMEM((4, PAIR_ROWS // 8, D), low),
            pltpu.VMEM((2, PAIR_ROWS // 8, D), low),
            pltpu.VMEM((8, 128, D), low),
            pltpu.VMEM((4, 128, D), low),
            pltpu.VMEM((4, 64, D), low),
            pltpu.VMEM((2, 64, D), low),
            pltpu.VMEM((128, D), wide),
            pltpu.VMEM((4, 64, D), low),
            pltpu.VMEM((4, 64, D), low),
            pltpu.VMEM((8, WIDE), wide),
            pltpu.VMEM((4, 8, D), wide),
            pltpu.VMEM((8, 8, D), wide),
            dma((3,)), dma((3,)), dma((2, 4)), dma((2, 2, 4)), dma((12,)), dma((12,)), dma((2,)),
            dma((10,)), dma((10,)), dma((3,)), dma((4,)), dma((16,)), dma((8, 2)), dma((10,)),
            dma((12,)), dma((6,)),
        ],
        compiler_params=pltpu.CompilerParams(
            collective_id=6, has_side_effects=True, vmem_limit_bytes=VMEM_LIMIT
        ),
        cost_estimate=pl.CostEstimate(
            flops=30000000000, bytes_accessed=30000000, transcendentals=0
        ),
        name="closing",
    )(
        d_qkv, w_qkv, tokens, d_hidden, vecs, rows_all, state_low, d_qkvst, os_rows, du_rows,
        d_start, dz_sum, small, out_part,
    )


def finish_kernel(
    pair, pair_tail, two, ff,
    query, key, value, squery, out, sout, up, down, state,
):
    step = pl.program_id(0)
    wide = jnp.float32
    up[...] = ff[0, 0].astype(wide).T
    down[...] = ff[0, 1].astype(wide)
    sout[...] = two[0, 0:32].astype(wide)
    out[...] = two[0, 32:64].astype(wide)
    for which, target in enumerate((query, key, value, squery)):

        @pl.when(step // 2 == which)
        def _():
            target[...] = pair[0].astype(wide).T

    @pl.when(step == 0)
    def _():
        state[...] = pair_tail[...].reshape(128, D).astype(wide)


def finish_grads(pair, two, ff):
    wide = jnp.float32
    turned = [
        pl.BlockSpec((D, 128), lambda i, w=which: (0, jnp.clip(i - 2 * w, 0, 1)))
        for which in range(4)
    ]
    square = jax.ShapeDtypeStruct((D, 256), wide)
    rows = jax.ShapeDtypeStruct((256, D), wide)
    whole = jax.ShapeDtypeStruct((D, D), wide)
    return pl.pallas_call(
        finish_kernel,
        grid=(8,),
        out_shape=[square] * 4 + [rows] * 2 + [whole] * 2 + [jax.ShapeDtypeStruct((128, D), wide)],
        in_specs=[
            pl.BlockSpec((1, 128, D), lambda i: (i % 2, i // 2, 0)),
            pl.BlockSpec((2, 64, D), lambda i: (0, 8, 0)),
            pl.BlockSpec((1, 64, D), lambda i: (i, 0, 0)),
            pl.BlockSpec((1, 2, 128, D), lambda i: (i, 0, 0, 0)),
        ],
        out_specs=turned
        + [pl.BlockSpec((32, D), lambda i: (i, 0))] * 2
        + [pl.BlockSpec((D, 128), lambda i: (0, i)), pl.BlockSpec((128, D), lambda i: (i, 0))]
        + [pl.BlockSpec((128, D), lambda i: (0, 0))],
        compiler_params=pltpu.CompilerParams(vmem_limit_bytes=VMEM_LIMIT),
        name="finish_grads",
    )(pair, pair, two, ff)


def swap_seq(value):
    return lax.all_to_all(value, "seq", 0, 0, tiled=False)


def line_body(
    inputs,
    seg_starts,
    lengths,
    init_state,
    attn_gain,
    state_gain,
    mlp_gain,
    w_query,
    w_key,
    w_value,
    w_out,
    w_squery,
    w_sout,
    w_up,
    w_down,
    rel_bias,
    gate_bias,
    out_cot,
    state_cot,
):
    low, wide = jnp.bfloat16, jnp.float32
    place = lax.axis_index("seq")
    half = lax.rem(place, 2)
    mine = place // 2
    plane = ("dp", "seq")
    spot = 4 * lax.axis_index("dp") + place
    head_of = lambda weight: lax.dynamic_slice_in_dim(weight, half * 128, 128, 1)
    gate_value = jax.nn.sigmoid(gate_bias)
    vecs = jnp.stack(
        [state_gain, gate_value, mlp_gain, attn_gain] + [jnp.zeros_like(gate_value)] * 4
    )
    offsets = jnp.arange(WIDE) - BLOCK
    offsets = jnp.where(offsets >= WIDE - 2 * BLOCK, offsets - WIDE, offsets)
    bucket_ids = bucket_of(offsets)
    one_hot = bucket_ids[:, None] == jnp.arange(BUCKETS)[None, :]
    my_bias = jnp.where(half == 0, rel_bias[:, 0], rel_bias[:, 1])
    bias_line = jnp.sum(jnp.where(one_hot, my_bias[None, :], 0.0), axis=1)
    segs = jnp.broadcast_to(jnp.repeat(seg_starts[:, 0], 2)[:, None, None], (4, 1, 128))
    segs = swap_seq(segs)[:, 0, 0]
    cots = swap_seq(state_cot.reshape(4, 64, D))
    cot_used = lax.all_gather(out_cot.reshape(256, D), plane, axis=0, tiled=True)

    w_qkv = jnp.concatenate([head_of(w_query), head_of(w_key), head_of(w_value)], axis=1)
    w_state = jnp.concatenate([head_of(w_squery), w_qkv[:, 128:]], axis=1)
    piece = jnp.concatenate(
        [
            lax.dynamic_slice_in_dim(w_sout, spot * 32, 32, 0),
            to_low(lax.dynamic_slice_in_dim(init_state, spot * 16, 16, 0)),
            lax.dynamic_slice_in_dim(w_out, spot * 32, 32, 0),
        ],
        axis=0,
    )
    rows_all, qkv, kept, bias = opening(
        inputs, w_qkv, piece, vecs, jnp.broadcast_to(bias_line[None, :], (8, WIDE))
    )
    kept = kept.reshape(8, 4, 80, D)

    ff_own = w_up.shape[1] // 8
    piece_of = lambda weight: lax.dynamic_slice_in_dim(weight, spot * 32, 32, 1).T
    pieces = jnp.concatenate(
        [
            piece_of(w_squery),
            piece_of(w_key),
            piece_of(w_value),
            lax.dynamic_slice_in_dim(w_up, spot * ff_own, ff_own, 1).T,
            lax.dynamic_slice_in_dim(w_down, spot * ff_own, ff_own, 0),
        ],
        axis=0,
    )
    qkv, pieces, segs, cot_used = lax.optimization_barrier((qkv, pieces, segs, cot_used))
    scal = jnp.concatenate([lax.dynamic_slice_in_dim(lengths, mine, 1, 0), segs])
    spread = lax.all_gather(pieces, "tensor", axis=0, tiled=True).reshape(4, 96 + 2 * ff_own, D)
    mixed, lse_tok, state_rows, state_low, qkvst, lse_st, os_rows = forward_chain(
        scal, qkv, kept, w_state, vecs, bias
    )
    mixed, back_piece, cots = lax.optimization_barrier(
        (mixed, spread[:, 0:96].reshape(384, D), cots)
    )
    w_back = lax.all_gather(back_piece, plane, axis=0, tiled=True)
    hidden_in, grad_hidden, d_mixed, mlp_sums, extra, ff_grads = middle(
        mixed, inputs, kept, spread, cot_used.reshape(8, 256, D), vecs
    )
    d_mixed, w_back, ff_grads = lax.optimization_barrier((d_mixed, w_back, ff_grads))
    ff_sum = lax.psum_scatter(
        ff_grads.reshape(ff_grads.shape[2] * 8, D), "tensor", scatter_dimension=0, tiled=True
    )
    (
        d_qkv, d_qkvst, du_rows, d_start, sums, dz_sum, state_out, tokens_out, out_part,
    ) = backward_chain(
        scal, qkv, d_mixed, lse_tok, qkvst, lse_st, state_rows, init_state, cots,
        w_back.reshape(8, 4, 3, 32, D), kept, vecs, bias, extra, hidden_in,
    )
    d_qkv, ff_sum = lax.optimization_barrier((d_qkv, ff_sum))
    ff_total = lax.all_gather(ff_sum, plane, axis=0, tiled=True).reshape(8, 2, ff_own, D)
    small = jnp.concatenate(
        [jnp.zeros((1, D), wide), sums[1:2], mlp_sums[0:1], sums[0:1], jnp.zeros((4, D), wide)]
    )
    inputs_grad, pair, two_grads, small = closing(
        d_qkv, w_qkv, inputs, grad_hidden, vecs, rows_all, state_low, d_qkvst,
        os_rows.reshape(256, D), du_rows.reshape(256, D), d_start, dz_sum, small, out_part,
    )
    pair = pair.reshape(2, PAIR_ROWS, D)
    (
        query_grad, key_grad, value_grad, squery_grad, out_grad, sout_grad, up_grad, down_grad,
        state_grad,
    ) = finish_grads(pair, two_grads, ff_total)
    bias_grad = lax.dynamic_slice_in_dim(
        small[4, : LINE * BUCKETS].reshape(4, 2, BUCKETS), lax.axis_index("tensor"), 1, 0
    )[0].T
    return (
        tokens_out,
        state_out[:, None],
        inputs_grad,
        state_grad,
        small[0],
        small[1],
        small[2],
        query_grad,
        key_grad,
        value_grad,
        out_grad,
        squery_grad,
        sout_grad,
        up_grad,
        down_grad,
        bias_grad,
        small[3],
    )


def solution(mesh):
    return jax.shard_map(
        chosen_body(mesh),
        mesh=mesh,
        in_specs=(
            P("dp", ("seq", "tensor"), None),
            P("dp", "seq"),
            P("dp"),
            P("tensor", None),
            P(),
            P(),
            P(),
            P(None, "tensor"),
            P(None, "tensor"),
            P(None, "tensor"),
            P("tensor", None),
            P(None, "tensor"),
            P("tensor", None),
            P(None, "tensor"),
            P("tensor", None),
            P(None, "tensor"),
            P(),
            P("dp", ("seq", "tensor"), None),
            P("dp", "seq", "tensor", None),
        ),
        out_specs=(
            P("dp", ("seq", "tensor"), None),
            P("dp", "seq", "tensor", None),
            P("dp", ("seq", "tensor"), None),
            P("tensor", None),
            P(),
            P(),
            P(),
            P(None, "tensor"),
            P(None, "tensor"),
            P(None, "tensor"),
            P("tensor", None),
            P(None, "tensor"),
            P("tensor", None),
            P(None, "tensor"),
            P("tensor", None),
            P(None, "tensor"),
            P(),
        ),
        check_vma=False,
    )
```

profile of v0, /device:TPU:0, one launch (start us, length us, event | category | flops | bytes accessed | tf_op | source)
XLA Modules:
  0.0 546.5 jit_solution(7529754648824074984)
XLA Ops:
  7.2 0.0 copy-start
  7.2 0.0 all-gather.5.cloned.1.call-start
  7.3 0.7 all-gather.5.cloned.1.call-update
  8.0 0.8 broadcast_in_dim.40
  8.8 0.1 broadcast_in_dim.41
  8.8 0.7 broadcast_in_dim.42
  9.5 4.2 all-to-all-start
  13.7 1.2 constant_dynamic-slice_fusion.3
  15.0 0.1 copy.57
  15.1 0.1 constant_dynamic-slice_fusion.5
  15.3 0.8 copy.56
  16.0 0.1 copy.58
  16.1 0.1 constant_dynamic-slice_fusion.2
  16.2 0.0 copy-start.9
  16.2 0.1 copy.59
  16.4 0.7 add_divide_fusion
  17.1 0.0 copy-done.14
  17.1 0.0 copy-start.11
  17.1 0.7 stack.19.vecs
  17.8 0.9 dynamic-slice_convert_fusion
  18.7 0.9 constant_dynamic-slice_fusion.6
  19.6 0.7 pad_maximum_fusion.4.piece
  20.2 0.8 fusion.11
  21.0 0.1 select_reduce_fusion
  21.2 0.0 copy-start.10
  21.2 1.0 constant_dynamic-slice_fusion.9
  22.2 1.3 pad_maximum_fusion
  23.6 0.6 broadcast_in_dim.39.line
  24.2 65.8 %opening.1 = (bf16[4,512,1024]{2,1,0:T(8,128)(2,1)}, bf16[4,512,384]{2,1,0:T(8,128)(2,1)}, bf16[8,320,1024]{2,1,0:T(8,128)(2,1)}, f32[512,1024]{1,0:T(8,128)}) custom-call(bf16[2,128,1024]{2,1,0:T(8,128)(2,1)} %tokens.5, bf16[1024,384]{1,0:T(8,128)(2,1)} %get-tuple-element.188.w_qkv, bf16[80,1024]{1,0:T(8,128)(2,1)} %pad_maximum_fusion.4.piece, ...), custom_call_target="tpu_custom_call" | custom-call | flops 30000001024 | bytes 30000000 | tf_op jit(solution)/shard_map/opening/pallas_call | solution.py:1740
  90.1 0.0 copy-start.16
  90.1 1.0 dynamic-slice_dynamic-update-slice_fusion
  91.1 0.0 copy-start.4
  91.1 0.2 slice_reduce_fusion
  91.3 0.0 all-gather.5.cloned.1.call-done
  91.3 0.7 copy-done.4
  91.9 0.0 all-gather.7.cloned.1.call-update
  92.0 3.5 all-to-all-start.1
  95.5 0.0 all-gather.9.cloned.1.call-start
  95.5 0.6 dynamic_slice.42
  96.1 1.2 pad_add_fusion.scal
  97.4 110.0 %forward_chain.1 = (bf16[4,512,128]{2,1,0:T(8,128)(2,1)}, f32[4,512,1]{2,1,0:T(8,128)}, f32[4,128,1024]{2,1,0:T(8,128)}, bf16[4,512,1024]{2,1,0:T(8,128)(2,1)}, ...) custom-call(s32[5]{0:T(128)} %pad_add_fusion.scal, ...), custom_call_target="tpu_custom_call" | custom-call | flops 20000000000 | bytes 20000000 | tf_op jit(solution)/shard_map/forward_chain/pallas_call | solution.py:711
  207.4 0.0 all-gather.7.cloned.1.call-done
  207.4 2.1 slice.51
  209.5 0.0 all-gather.9.cloned.1.call-update
  209.5 0.2 reduce-scatter.2.cloned.1.call-start
  209.7 105.4 %middle.1 = (f32[2,128,1024]{2,1,0:T(8,128)}, f32[2,128,1024]{2,1,0:T(8,128)}, bf16[4,512,128]{2,1,0:T(8,128)(2,1)}, f32[8,1024]{1,0:T(8,128)}, bf16[8,384,1024]...) custom-call(bf16[4,512,128]{2,1,0:T(8,128)(2,1)} %get-tuple-element.75.mixed, bf16[2,128,1024]{2,1,0:T(8,128)(2,1)} %tokens.5, ...), custom_call_target="tpu_custom_call" | custom-call | flops 60000002048 | bytes 60000000 | tf_op jit(solution)/shard_map/middle/pallas_call | solution.py:1529
  315.1 0.0 all-gather.9.cloned.1.call-done
  315.1 0.0 reduce-scatter.2.cloned.1.call-update
  315.2 0.0 all-gather.11.cloned.1.call-start
  315.2 104.8 %backward_chain.1 = (bf16[4,512,384]{2,1,0:T(8,128)(2,1)}, bf16[4,512,384]{2,1,0:T(8,128)(2,1)}, bf16[4,64,1024]{2,1,0:T(8,128)(2,1)}, f32[64,1024]{1,0:T(8,128)...) custom-call(s32[5]{0:T(128)} %pad_add_fusion.scal, ...), custom_call_target="tpu_custom_call" | custom-call | flops 40000000000 | bytes 40000000 | tf_op jit(solution)/shard_map/backward_chain/pallas_call | solution.py:972
  420.0 0.0 reduce-scatter.2.cloned.1.call-done
  420.0 0.0 all-gather.11.cloned.1.call-update
  420.1 0.8 slice.43
  420.8 0.8 fusion.13
  421.7 0.7 concatenate.25.small
  422.3 100.5 %closing.1 = (f32[2,128,1024]{2,1,0:T(8,128)}, bf16[2,4,160,1024]{3,2,1,0:T(8,128)(2,1)}, bf16[8,64,1024]{2,1,0:T(8,128)(2,1)}, f32[8,1024]{1,0:T(8,128)}) custom-call(bf16[4,512,384]{2,1,0:T(8,128)(2,1)} %get-tuple-element.93.d_qkv, bf16[1024,384]{1,0:T(8,128)(2,1)} %get-tuple-element.188.w_qkv, bf16[2,128,1024]{2,1,0:T(8,128)(2,1)} %tokens.5, ...), custom_call_target="tpu_custom_call" | custom-call | flops 30000001024 | bytes 30000000 | tf_op jit(solution)/shard_map/closing/pallas_call | solution.py:2188
  522.8 0.7 slice_reduce_fusion.1
  523.5 0.1 reshape_squeeze.3
  523.6 0.6 fusion.10
  524.2 1.5 fusion.12
  525.7 11.4 %finish_grads.1 = (f32[1024,256]{1,0:T(8,128)}, f32[1024,256]{1,0:T(8,128)}, f32[1024,256]{1,0:T(8,128)}, f32[1024,256]{1,0:T(8,128)}, f32[256,1024]{1,0:T(8,128...) custom-call(bf16[2,640,1024]{2,1,0:T(8,128)(2,1)} %bitcast.38, ...), custom_call_target="tpu_custom_call" | custom-call | tf_op jit(solution)/shard_map/finish_grads/pallas_call | solution.py:2267
  537.2 0.8 copy.67
  538.0 1.0 copy.68
  539.0 1.0 copy.69
  (38 shorter events, 0.2 us)
Async XLA Ops:
  7.2 8.9 %copy-start = (bf16[1024,1024]{1,0:T(8,128)(2,1)S(1)}, bf16[1024,1024]{1,0:T(8,128)(2,1)}, u32[]{:S(2)}) copy-start(bf16[1024,1024]{1,0:T(8,128)(2,1)} %param.32) | copy-start | bytes 6291460
  7.2 7.9 %copy-start.5 = (bf16[1024,256]{1,0:T(8,128)(2,1)S(1)}, bf16[1024,256]{1,0:T(8,128)(2,1)}, u32[]{:S(2)}) copy-start(bf16[1024,256]{1,0:T(8,128)(2,1)} %param.30) | copy-start | bytes 1572868
  7.2 84.1 %all-gather.5.cloned.1.call-start = ((), (), s32[]{:S(2)}) async-start(), calls=%async_computation.3 | async-start | bytes 4718592 | tf_op jit(solution)/shard_map/all_gather | solution.py:2331
  7.3 9.8 %copy-start.13 = (f32[1024]{0:T(1024)S(1)}, f32[1024]{0:T(1024)}, u32[]{:S(2)}) copy-start(f32[1024]{0:T(1024)} %param.24) | copy-start | bytes 12292
  7.3 9.8 %copy-start.14 = (f32[1024]{0:T(1024)S(1)}, f32[1024]{0:T(1024)}, u32[]{:S(2)}) copy-start(f32[1024]{0:T(1024)} %param.25) | copy-start | bytes 12292
  7.3 9.8 %copy-start.15 = (f32[1024]{0:T(1024)S(1)}, f32[1024]{0:T(1024)}, u32[]{:S(2)}) copy-start(f32[1024]{0:T(1024)} %param.23) | copy-start | bytes 12292
  9.5 81.6 %all-to-all-start = ((s32[4,1,128]{2,1,0:T(1,128)}), s32[4,1,128]{2,1,0:T(1,128)S(1)}, u32[]{:S(2)}, u32[]{:S(2)}) async-start(s32[4,1,128]{2,1,0:T(1,128)} %broadcast_in_dim.42), calls=%async_computation | async-start | bytes 4096 | tf_op jit(solution)/shard_map/all_to_all | solution.py:2287
  13.7 193.7 %all-gather.7.cloned.1.call-start = ((), (), s32[]{:S(2)}) async-start(), calls=%async_computation.4 | async-start | bytes 3604480 | tf_op jit(solution)/shard_map/all_gather | solution.py:2362
  16.0 5.1 copy-start.8
  16.2 5.0 copy-start.9
  17.1 0.7 copy-start.11
  21.2 2.3 copy-start.10
  90.1 5.4 copy-start.16
  91.1 0.9 copy-start.4
  92.0 117.5 %all-to-all-start.1 = ((bf16[4,64,1024]{2,1,0:T(8,128)(2,1)}), bf16[4,64,1024]{2,1,0:T(8,128)(2,1)S(1)}, u32[]{:S(2)}, u32[]{:S(2)}) async-start(bf16[4,64,1024]{2,1,0:T(8,128)(2,1)} %bitcast.14), calls=%async_computation.1 | async-start | bytes 1048576 | tf_op jit(solution)/shard_map/all_to_all | solution.py:2287
  95.5 219.7 %all-gather.9.cloned.1.call-start = ((), (), s32[]{:S(2)}) async-start(), calls=%async_computation.5 | async-start | bytes 7077888 | tf_op jit(solution)/shard_map/all_gather | solution.py:2369
  209.5 105.7 %copy-start.7 = (bf16[4,64,1024]{2,1,0:T(8,128)(2,1)}, bf16[4,64,1024]{2,1,0:T(8,128)(2,1)S(1)}, u32[]{:S(2)}) copy-start(bf16[4,64,1024]{2,1,0:T(8,128)(2,1)S(1)} %all-to-all-done.1.cots) | copy-start | bytes 1572868
  209.5 210.5 %reduce-scatter.2.cloned.1.call-start = ((), (), s32[]{:S(2)}) async-start(), calls=%async_computation.6 | async-start | bytes 2621440 | tf_op jit(solution)/shard_map/reduce_scatter | solution.py:2374
  315.2 210.5 %all-gather.11.cloned.1.call-start = ((), (), s32[]{:S(2)}) async-start(), calls=%async_computation.7 | async-start | bytes 4718592 | tf_op jit(solution)/shard_map/all_gather | solution.py:2384
  315.2 106.5 %copy-start.12 = (f32[4,1024]{1,0:T(4,128)S(1)}, f32[4,1024]{1,0:T(4,128)}, u32[]{:S(2)}) copy-start(f32[4,1024]{1,0:T(4,128)} %copy-done.11) | copy-start | bytes 49156
  525.7 11.5 %copy-start.6 = (bf16[2,128,1024]{2,1,0:T(8,128)(2,1)S(1)}, bf16[2,128,1024]{2,1,0:T(8,128)(2,1)}, u32[]{:S(2)}) copy-start(bf16[2,128,1024]{2,1,0:T(8,128)(2,1)} %get-tuple-element.220) | copy-start | bytes 1572868
  525.7 12.3 %copy-start.2 = (f32[2,128,1024]{2,1,0:T(8,128)S(1)}, f32[2,128,1024]{2,1,0:T(8,128)}, u32[]{:S(2)}) copy-start(f32[2,128,1024]{2,1,0:T(8,128)} %get-tuple-element.90) | copy-start | bytes 3145732
  537.1 1.8 copy-start.3
  537.2 2.8 copy-start.1
Sparse Core Ops, SparseCore 0:
  9.9 40.9 all-gather.4
  92.1 78.8 all-gather.6
  209.6 66.1 all-gather.8
  315.3 52.4 reduce-scatter.1
  420.2 50.1 all-gather.10
where the time goes:
time: 547 us; the launch traced here: 546 us
  Pallas kernels  498 us (91%)
  local copies, waits for them, and re-layouts  20.7 us (4%)
  between operations  14.2 us (3%)
  starting transfers between devices  8.06 us (1%)
    pallas_call x1, Pallas kernels, forward_chain(): pl.pallas_call(forward_kernel, out_shape=[jax.ShapeDtypeStruct(*one) for...  110 us
    pallas_call x1, Pallas kernels, middle(): pl.pallas_call(middle_kernel, out_shape=[jax.ShapeDtypeStruct(*one) for o...  105 us
    pallas_call x1, Pallas kernels, backward_chain(): pl.pallas_call(backward_kernel, out_shape=[jax.ShapeDtypeStruct(*one) for...  105 us
    pallas_call x1, Pallas kernels, closing(): pl.pallas_call(closing_kernel, out_shape=[jax.ShapeDtypeStruct(*one) for...  100 us
    pallas_call x1, Pallas kernels, opening(): pl.pallas_call(opening_kernel, out_shape=[jax.ShapeDtypeStruct(*one) for...  65.8 us
    pallas_call x1, Pallas kernels, finish_grads(): pl.pallas_call(finish_kernel, grid=(8,), out_shape=[square] * 4 + [rows]...  11.4 us
  transfers between devices with their start and end apart: 7, of which 0 were waited for; matrix products, arithmetic and copies ran while one was open for 4% of the time, Pallas kernels for 89%

commit v1 on v0

--- a/solution.py
+++ b/solution.py
@@ -516,6 +516,14 @@
         ).start()
 
 
+def fetch_columns(weights, target, sem):
+    half = lax.rem(lax.axis_index("seq"), 2)
+    for index, weight in enumerate(weights):
+        pltpu.make_async_copy(
+            weight.at[:, span(half, 128)], target.at[:, pl.ds(128 * index, 128)], sem
+        ).start()
+
+
 def fetched(target, sem):
     pltpu.make_async_copy(target, target, sem).wait()
 
@@ -526,9 +534,17 @@
     return centered, lax.rsqrt(spread + norm_eps)
 
 
-def token_masks(scal, block_id, first_row):
-    length = scal[0]
-    start = scal[1 + block_id]
+def mark(marks, block_id, row):
+    return marks[block_id, pl.ds(row, 1), 0:1]
+
+
+def sequence_marks(marks, block_id):
+    mine = lax.axis_index("seq") // 2
+    return mark(marks, block_id, mine), mark(marks, 0, 2 + mine)
+
+
+def token_masks(marks, block_id, first_row):
+    start, length = sequence_marks(marks, block_id)
     row = lax.broadcasted_iota(jnp.int32, (ROWS, BLOCK), 0) + first_row
     col = lax.broadcasted_iota(jnp.int32, (ROWS, BLOCK), 1)
     prev_limit = jnp.where(block_id > 0, length - (block_id - 1) * BLOCK, 0)
@@ -539,9 +555,10 @@
     return prev_ok, cur_ok
 
 
-def state_block_mask(scal, block_id):
+def state_block_mask(marks, block_id):
+    _, length = sequence_marks(marks, block_id)
     col = lax.broadcasted_iota(jnp.int32, (ROWS, BLOCK), 1)
-    return col < scal[0] - block_id * BLOCK
+    return col < length - block_id * BLOCK
 
 
 def softmax_of(score_parts):
@@ -577,57 +594,154 @@
     return query, (tok, stt)
 
 
+HALVES = 2
+HALF_ROWS = STATES // HALVES
+HALF_CHUNKS = HALF_ROWS // ROWS
+
+
 def forward_kernel(
-    scal, qkv, kept, w_state, vecs, bias,
-    o_out, lse_out, state_rows, state_low, qkvst, lse_st, os_rows,
-    held, os_all, w_sout, start, send_sem, pass_sem, recv_sem, local_sem,
+    marks, qkv, kept, w_squery, w_qkv, vecs, bias, state_cot, back_own,
+    o_out, lse_out, state_rows, low_out, qkvst, lse_st, os_rows, cots, back,
+    held, os_all, state_low, w_sout, start, w_state,
+    way_send, core_send, recv_sem, local_sem, low_sem, cot_send, cot_recv,
+    piece_send, piece_recv, ring_send, ring_recv,
 ):
-    place, half, rank = line_place()
-    fetch_pieces(kept, 32, 16, start, local_sem.at[0])
-    fetch_pieces(kept, 0, 32, w_sout, local_sem.at[1])
+    side, place, half, rank = plane_place()
+    me = plane_index(side, place)
     partner = place + 1 - 2 * half
     head = 2 * rank + half
-    peers = [lax.rem(rank + step, 4) for step in (1, 2, 3)]
+    fetch_pieces(kept, 32, 16, start, local_sem.at[0])
+    fetch_columns((w_squery,), w_state, local_sem.at[2])
+    fetch_pieces(kept, 0, 32, w_sout, local_sem.at[1])
+    own_cot = pltpu.make_async_copy(state_cot.at[place], cots.at[place], local_sem.at[4])
+    own_cot.start()
+    own_piece = pltpu.make_async_copy(back_own, back.at[me, rank], local_sem.at[3])
+    own_piece.start()
+    ranks = [lax.rem(rank + step, 4) for step in (1, 2, 3)]
+    seats = [lax.rem(place + step, 4) for step in (1, 2, 3)]
     barrier = pltpu.get_barrier_semaphore()
-    for peer in peers:
-        pl.semaphore_signal(
-            barrier, inc=1, device_id={"seq": place, "tensor": peer}, device_id_type=MESH_ID
-        )
-    pl.semaphore_signal(
-        barrier, inc=1, device_id={"seq": partner, "tensor": rank}, device_id_type=MESH_ID
-    )
+    for target in [{"tensor": one} for one in ranks] + [{"seq": one} for one in seats] + [
+        {"dp": 1 - side}
+    ]:
+        pl.semaphore_signal(barrier, inc=1, device_id=target, device_id_type=MESH_ID)
     fetched(start, local_sem.at[0])
     held[...] = start[...].reshape(STATES, D).astype(jnp.float32)
     gain = vecs[0:1, :]
     gate = vecs[1:2, :]
-    pl.semaphore_wait(barrier, 4)
-    fetched(w_sout, local_sem.at[1])
-
-    def carry_copy(block_id, which, sem, seq_to, rank_to):
-        part = os_all.at[block_id, :, span(which, 128)]
-        return pltpu.make_async_remote_copy(
-            src_ref=part,
-            dst_ref=part,
-            send_sem=sem,
-            recv_sem=recv_sem.at[block_id, which],
-            device_id={"seq": seq_to, "tensor": rank_to},
-            device_id_type=MESH_ID,
-        )
-
-    def one_block(block_id, _):
-        def project(chunk, _):
+    fetched(w_state, local_sem.at[2])
+
+    def project(block_id, part):
+        def one(chunk, _):
             rows = span(chunk, ROWS)
             centered, scale = norm_parts(held[rows, :])
             low = to_low(centered * scale * gain)
             state_low[block_id, rows, :] = low
-            qkvst[block_id, rows, :] = to_low(dot_nn(low, w_state[...]))
+            qkvst[block_id, rows, 0:128] = to_low(dot_nn(low, w_state[...]))
+            qkvst[block_id, rows, 128:384] = to_low(dot_nn(low, w_qkv[:, 128:384]))
             return 0
 
-        lax.fori_loop(0, CHUNKS, project, 0)
-
+        lax.fori_loop(HALF_CHUNKS * part, HALF_CHUNKS * (part + 1), one, 0)
+
+    pl.semaphore_wait(barrier, 7)
+
+    def piece_move(origin, part, slot, target):
+        return pltpu.make_async_remote_copy(
+            src_ref=back_own.at[part],
+            dst_ref=back.at[me, origin, part],
+            send_sem=piece_send.at[part, slot],
+            recv_sem=piece_recv.at[part, origin],
+            device_id={"tensor": target},
+            device_id_type=MESH_ID,
+        )
+
+    def send_piece(part):
+        for slot, target in enumerate(ranks):
+            piece_move(rank, part, slot, target).start()
+
+    gather = plane_gather(
+        lambda owner, part: back.at[owner, pl.ds(2 * part, 2)], ring_send, ring_recv
+    )
+    next(gather)
+    send_piece(0)
+    for part in range(HALVES):
+        project(0, part)
+    right, left = {"tensor": lax.rem(rank + 1, 4)}, {"tensor": lax.rem(rank + 3, 4)}
+
+    def moved(block_id, part, which, sem, target):
+        view = os_all.at[block_id, pl.ds(HALF_ROWS * part, HALF_ROWS), span(which, 128)]
+        return pltpu.make_async_remote_copy(
+            src_ref=view,
+            dst_ref=view,
+            send_sem=sem,
+            recv_sem=recv_sem.at[block_id, part, which],
+            device_id=target,
+            device_id_type=MESH_ID,
+        )
+
+    def cot_move(index, origin, slot, target):
+        return pltpu.make_async_remote_copy(
+            src_ref=state_cot.at[index],
+            dst_ref=cots.at[origin],
+            send_sem=cot_send.at[slot],
+            recv_sem=cot_recv.at[origin],
+            device_id={"seq": target},
+            device_id_type=MESH_ID,
+        )
+
+    for slot, target in enumerate(seats):
+        cot_move(target, place, slot, target).start()
+    fetched(w_sout, local_sem.at[1])
+
+    def origin_of(way, distance):
+        if way == 0:
+            return jnp.maximum(rank - distance, 0)
+        return jnp.minimum(rank + distance, 3)
+
+    def ways(distance):
+        return (
+            (0, rank >= distance, (rank >= distance) & (rank < 3), right),
+            (1, rank + distance <= 3, (rank + distance <= 3) & (rank > 0), left),
+        )
+
+    def relay(block_id, part, distance, waiting):
+        for way, comes, goes, target in ways(distance):
+            which = 2 * origin_of(way, distance) + half
+            sem = way_send.at[block_id, part, min(distance, 2), way]
+            core_sem = core_send.at[block_id, part, which // 2]
+            if distance > 0:
+
+                @pl.when(comes)
+                def _():
+                    to_core = moved(block_id, part, which, core_sem, {"seq": partner})
+                    if waiting:
+                        moved(block_id, part, which, sem, target).wait_recv()
+                        to_core.start()
+                    else:
+                        to_core.wait_send()
+
+            if distance < 3:
+
+                @pl.when(goes)
+                def _():
+                    one = moved(block_id, part, which, sem, target)
+                    if waiting:
+                        one.start()
+                    else:
+                        one.wait_send()
+
+        if distance == 0:
+            mine = moved(
+                block_id, part, head, core_send.at[block_id, part, rank], {"seq": partner}
+            )
+            if waiting:
+                mine.start()
+            else:
+                mine.wait_send()
+
+    def one_block(block_id, _):
         def attend_state(chunk, _):
             rows = span(chunk, ROWS)
-            _, parts = state_scores(scal, qkv, qkvst, block_id, chunk)
+            _, parts = state_scores(marks, qkv, qkvst, block_id, chunk)
             (w_tok, w_stt), total = softmax_of(parts)
             mixed = dot_nn(w_tok, qkv[block_id, :, 256:384]) + dot_nn(
                 w_stt, qkvst[block_id, :, 256:384]
@@ -636,14 +750,9 @@
             lse_st[block_id, rows, :] = total
             return 0
 
-        lax.fori_loop(0, CHUNKS, attend_state, 0)
-        for slot, peer in enumerate(peers):
-            carry_copy(block_id, head, send_sem.at[block_id, slot], place, peer).start()
-        carry_copy(block_id, head, send_sem.at[block_id, 3], partner, rank).start()
-
         def attend_token(chunk, _):
             rows = span(chunk, ROWS)
-            _, parts = token_scores(scal, qkv, qkvst, bias, block_id, chunk)
+            _, parts = token_scores(marks, qkv, qkvst, bias, block_id, chunk)
             weights, total = softmax_of(parts)
             prev_id = jnp.maximum(block_id - 1, 0)
             mixed = (
@@ -655,23 +764,79 @@
             lse_out[block_id, rows, :] = total
             return 0
 
-        lax.fori_loop(0, CHUNKS, attend_token, 0)
-        for slot, peer in enumerate(peers):
-            other = 2 * peer + half
-            carry_copy(block_id, other, send_sem.at[block_id, slot], place, peer).wait_recv()
-            carry_copy(block_id, other, pass_sem.at[block_id, slot], partner, rank).start()
-        for other_rank in range(4):
-            carry_copy(
-                block_id, 2 * other_rank + 1 - half, send_sem.at[block_id, 3], partner, rank
-            ).wait_recv()
-
-        def update(chunk, _):
-            rows = span(chunk, ROWS)
-            change = dot_nn(os_all[block_id, rows, :], w_sout[...].reshape(D, D))
-            held[rows, :] = gate * held[rows, :] + (1.0 - gate) * change
+        def attend_both(part, _):
+            lax.fori_loop(HALF_CHUNKS * part, HALF_CHUNKS * (part + 1), attend_state, 0)
+            for value in range(HALVES):
+
+                @pl.when(part == value)
+                def _():
+                    relay(block_id, value, 0, True)
+
             return 0
 
-        lax.fori_loop(0, CHUNKS, update, 0)
+        lax.fori_loop(0, HALVES, attend_both, 0)
+        pltpu.make_async_copy(
+            state_low.at[block_id], low_out.at[block_id], low_sem.at[block_id]
+        ).start()
+
+        @pl.when(block_id == 2)
+        def _():
+            own_piece.wait()
+            for part in range(3):
+                for slot, target in enumerate(ranks):
+                    piece_move(target, part, slot, target).wait_recv()
+            next(gather)
+
+        @pl.when(block_id == 3)
+        def _():
+            next(gather)
+            next(gather)
+
+        def between(step, _):
+            for value, (distance, part) in enumerate(((1, 0), (1, 1), (2, 0), (2, 1))):
+
+                @pl.when(step == value)
+                def _():
+                    relay(block_id, part, distance, True)
+
+            return attend_token(step, 0)
+
+        lax.fori_loop(0, 4, between, 0)
+
+        def settle(part, _):
+            for value in range(HALVES):
+
+                @pl.when(part == value)
+                def _():
+                    relay(block_id, value, 3, True)
+                    for origin in range(4):
+                        moved(
+                            block_id, value, 2 * origin + 1 - half,
+                            core_send.at[block_id, value, origin], {"seq": partner},
+                        ).wait_recv()
+
+                    if value == HALVES - 1:
+                        for turn in (0, 1):
+
+                            @pl.when(block_id == turn)
+                            def _():
+                                send_piece(turn + 1)
+
+            def update(chunk, _):
+                rows = span(chunk, ROWS)
+                change = dot_nn(os_all[block_id, rows, :], w_sout[...].reshape(D, D))
+                held[rows, :] = gate * held[rows, :] + (1.0 - gate) * change
+                return 0
+
+            lax.fori_loop(HALF_CHUNKS * part, HALF_CHUNKS * (part + 1), update, 0)
+
+            @pl.when(block_id < 3)
+            def _():
+                project(block_id + 1, part)
+
+            return 0
+
+        lax.fori_loop(0, HALVES, settle, 0)
         state_rows[block_id] = held[span(rank, 128), :]
         os_rows[block_id] = os_all[block_id, span(head, 64), :]
         return 0
@@ -679,14 +844,24 @@
     lax.fori_loop(0, 4, one_block, 0)
 
     def drain(block_id, _):
-        for slot, peer in enumerate(peers):
-            carry_copy(block_id, head, send_sem.at[block_id, slot], place, peer).wait_send()
-            other = 2 * peer + half
-            carry_copy(block_id, other, pass_sem.at[block_id, slot], partner, rank).wait_send()
-        carry_copy(block_id, head, send_sem.at[block_id, 3], partner, rank).wait_send()
+        for part in range(HALVES):
+            for distance in range(4):
+                relay(block_id, part, distance, False)
+        pltpu.make_async_copy(
+            state_low.at[block_id], low_out.at[block_id], low_sem.at[block_id]
+        ).wait()
         return 0
 
     lax.fori_loop(0, 4, drain, 0)
+    own_cot.wait()
+    for part in range(3):
+        for slot, target in enumerate(ranks):
+            piece_move(rank, part, slot, target).wait_send()
+    for _ in gather:
+        pass
+    for slot, target in enumerate(seats):
+        cot_move(target, place, slot, target).wait_send()
+        cot_move(place, target, slot, target).wait_recv()
 
 
 def any_specs(count):
@@ -697,7 +872,9 @@
     return [pl.BlockSpec(memory_space=pltpu.VMEM)] * count
 
 
-def forward_chain(scal, qkv, kept, w_state, vecs, bias):
+def forward_chain(
+    marks, qkv, kept, w_squery, w_qkv, vecs, bias, state_cot, back_own
+):
     low, wide = jnp.bfloat16, jnp.float32
     shapes = (
         ((4, BLOCK, 128), low),
@@ -707,31 +884,42 @@
         ((4, STATES, 384), low),
         ((4, STATES, 1), wide),
         ((4, 64, D), low),
-    )
+        ((4, 64, D), low),
+        ((8, 4, 3, 32, D), low),
+    )
+    dma = pltpu.SemaphoreType.DMA
     return pl.pallas_call(
         forward_kernel,
         out_shape=[jax.ShapeDtypeStruct(*one) for one in shapes],
-        in_specs=[pl.BlockSpec(memory_space=pltpu.SMEM)]
-        + vmem_specs(1)
-        + any_specs(1)
-        + vmem_specs(3),
-        out_specs=vmem_specs(7),
+        in_specs=vmem_specs(2) + any_specs(2) + vmem_specs(3) + any_specs(2),
+        out_specs=vmem_specs(3) + any_specs(1) + vmem_specs(3) + any_specs(2),
         scratch_shapes=[
             pltpu.VMEM((STATES, D), wide),
             pltpu.VMEM((4, STATES, D), low),
+            pltpu.VMEM((4, STATES, D), low),
             pltpu.VMEM((4, 8, 32, D), low),
             pltpu.VMEM((4, 8, 16, D), low),
-            pltpu.SemaphoreType.DMA((4, 4)),
-            pltpu.SemaphoreType.DMA((4, 3)),
-            pltpu.SemaphoreType.DMA((4, 8)),
-            pltpu.SemaphoreType.DMA((2,)),
+            pltpu.VMEM((D, 128), low),
+            dma((4, HALVES, 3, 2)),
+            dma((4, HALVES, 4)),
+            dma((4, HALVES, 8)),
+            dma((5,)),
+            dma((4,)),
+            dma((3,)),
+            dma((4,)),
+            dma((3, 3)),
+            dma((3, 4)),
+            dma((14,)),
+            dma((8, 2)),
         ],
         compiler_params=pltpu.CompilerParams(
             collective_id=1, has_side_effects=True, vmem_limit_bytes=VMEM_LIMIT
         ),
-        cost_estimate=pl.CostEstimate(flops=20000000000, bytes_accessed=20000000, transcendentals=0),
+        cost_estimate=pl.CostEstimate(
+            flops=60000000000, bytes_accessed=60000000, transcendentals=0
+        ),
         name="forward_chain",
-    )(scal, qkv, kept, w_state, vecs, bias)
+    )(marks, qkv, kept, w_squery, w_qkv, vecs, bias, state_cot, back_own)
 
 
 def backward_kernel(
@@ -972,8 +1160,7 @@
     return pl.pallas_call(
         backward_kernel,
         out_shape=[jax.ShapeDtypeStruct(*one) for one in shapes],
-        in_specs=[pl.BlockSpec(memory_space=pltpu.SMEM)]
-        + vmem_specs(5)
+        in_specs=vmem_specs(6)
         + any_specs(1)
         + vmem_specs(2)
         + any_specs(2)
@@ -1026,72 +1213,74 @@
     return 4 * side + place
 
 
-def plane_gather(buf, rows, send_sem, recv_sem):
+def row_halves(buf, rows):
+    size = rows // 2
+    return lambda owner, part: buf.at[owner, pl.ds(part * size, size), :]
+
+
+def plane_gather(view, send_sem, recv_sem):
     side, place, half, rank = plane_place()
     across, beside = 1 - side, lax.rem(place + 2, 4)
     core = place + 1 - 2 * half
     me = plane_index(side, place)
     at_x, at_y = plane_index(across, place), plane_index(side, beside)
     at_d = plane_index(across, beside)
-    to_x = {"dp": across}
-    to_y = {"seq": beside}
-    to_c = {"seq": core}
-    size = rows // 2
+    to_x, to_y, to_c = {"dp": across}, {"seq": beside}, {"seq": core}
 
     def piece(owner, part, slot, target):
-        view = buf.at[owner, pl.ds(part * size, size), :]
+        one = view(owner, part)
         return pltpu.make_async_remote_copy(
-            src_ref=view,
-            dst_ref=view,
+            src_ref=one,
+            dst_ref=one,
             send_sem=send_sem.at[slot],
             recv_sem=recv_sem.at[owner, part],
             device_id=target,
             device_id_type=MESH_ID,
         )
 
-    sent = []
-
-    def send(owner, part, target):
-        one = piece(owner, part, len(sent), target)
-        sent.append(one)
+    own = [
+        piece(me, 0, 0, to_x), piece(me, 1, 1, to_y), piece(me, 1, 2, to_x), piece(me, 0, 3, to_y),
+        piece(me, 0, 4, to_c), piece(me, 1, 5, to_c),
+    ]
+    on_x0, on_y1 = piece(at_x, 0, 6, to_y), piece(at_y, 1, 7, to_x)
+    came = [
+        (piece(owner, part, 0, to_c), piece(owner, part, slot, to_c))
+        for owner, part, slot in (
+            (at_x, 0, 8), (at_y, 1, 9), (at_x, 1, 10), (at_y, 0, 11), (at_d, 0, 12), (at_d, 1, 13)
+        )
+    ]
+    core_came = [
+        piece(owner, part, 0, to_c)
+        for owner in (
+            plane_index(side, core),
+            plane_index(across, core),
+            plane_index(side, lax.rem(core + 2, 4)),
+            plane_index(across, lax.rem(core + 2, 4)),
+        )
+        for part in (0, 1)
+    ]
+    yield
+    for one in own:
         one.start()
-
-    def arrived(owner, part):
-        piece(owner, part, 0, to_c).wait_recv()
-
-    send(me, 0, to_x)
-    send(me, 1, to_y)
-    send(me, 1, to_x)
-    send(me, 0, to_y)
-    send(me, 0, to_c)
-    send(me, 1, to_c)
     yield
-    arrived(at_x, 0)
-    send(at_x, 0, to_y)
-    arrived(at_y, 1)
-    send(at_y, 1, to_x)
-    send(at_x, 0, to_c)
-    send(at_y, 1, to_c)
+    came[0][0].wait_recv()
+    on_x0.start()
+    came[1][0].wait_recv()
+    on_y1.start()
+    came[0][1].start()
+    came[1][1].start()
     yield
-    arrived(at_x, 1)
-    send(at_x, 1, to_c)
-    arrived(at_y, 0)
-    send(at_y, 0, to_c)
+    for index in (2, 3):
+        came[index][0].wait_recv()
+        came[index][1].start()
     yield
-    arrived(at_d, 0)
-    send(at_d, 0, to_c)
-    arrived(at_d, 1)
-    send(at_d, 1, to_c)
+    for index in (4, 5):
+        came[index][0].wait_recv()
+        came[index][1].start()
     yield
-    for owner in (
-        plane_index(side, core),
-        plane_index(across, core),
-        plane_index(side, lax.rem(core + 2, 4)),
-        plane_index(across, lax.rem(core + 2, 4)),
-    ):
-        arrived(owner, 0)
-        arrived(owner, 1)
-    for one in sent:
+    for one in core_came:
+        one.wait_recv()
+    for one in own + [on_x0, on_y1] + [two for _, two in came]:
         one.wait_send()
 
 
@@ -1560,26 +1749,40 @@
     )(mixed, tokens, kept, spread, cot_all, vecs)
 
 
-SPREAD_FIRST = 96
+SPREAD_FIRST = 0
 
 
 WIDE = 2048
 
 
 def opening_kernel(
-    tokens, w_qkv, piece, vecs, line,
-    rows_all, qkv, kept, table,
-    stage, send_sem, core_sem, recv_sem, piece_send, piece_recv, ring_send, ring_recv,
+    tokens, w_query, w_key, w_value, w_sout, w_out, begin, vecs, rel_bias, marks_own,
+    rows_all, qkv, kept, table, marks, w_qkv,
+    begin_rows, bias_rows, stage, send_sem, core_sem, recv_sem, piece_send, piece_recv, ring_send, ring_recv,
+    mark_send, mark_recv, local_sem,
 ):
     side, place, half, rank = plane_place()
     mine = place // 2
     core = place + 1 - 2 * half
     other = lax.rem(place + 2, 4)
     me = plane_index(side, place)
-    extra = piece.shape[0]
+    extra = 80
+    fetch_columns((w_query, w_key, w_value), w_qkv, local_sem.at[0])
+    loads = [
+        pltpu.make_async_copy(
+            w_sout.at[span(me, 32), :], kept.at[me, pl.ds(80 * rank, 32), :], local_sem.at[1]
+        ),
+        pltpu.make_async_copy(
+            w_out.at[span(me, 32), :], kept.at[me, pl.ds(80 * rank + 48, 32), :], local_sem.at[3]
+        ),
+        pltpu.make_async_copy(begin.at[span(me, 16), :], begin_rows, local_sem.at[2]),
+    ]
+    for one in loads:
+        one.start()
     barrier = pltpu.get_barrier_semaphore()
     greeted = [{"tensor": lax.rem(rank + step, 4)} for step in (1, 2, 3)]
-    greeted += [{"seq": core}, {"seq": other}, {"dp": 1 - side}]
+    seats = [lax.rem(place + step, 4) for step in (1, 2, 3)]
+    greeted += [{"seq": one} for one in seats] + [{"dp": 1 - side}]
     for target in greeted:
         pl.semaphore_signal(barrier, inc=1, device_id=target, device_id_type=MESH_ID)
     gain = vecs[3:4, :]
@@ -1600,8 +1803,8 @@
         )
 
     stage[...] = normed(1 - mine)
-    kept[me, span(rank, extra), :] = piece[...]
-    pl.semaphore_wait(barrier, 6)
+    marks[place] = marks_own[...]
+    pl.semaphore_wait(barrier, 7)
     aside = pltpu.make_async_remote_copy(
         src_ref=stage,
         dst_ref=rows_all.at[place, span(rank, 128), :],
@@ -1611,6 +1814,35 @@
         device_id_type=MESH_ID,
     )
     aside.start()
+
+    def mark_move(slot, origin, target):
+        return pltpu.make_async_remote_copy(
+            src_ref=marks.at[origin],
+            dst_ref=marks.at[origin],
+            send_sem=mark_send.at[slot],
+            recv_sem=mark_recv.at[origin],
+            device_id={"seq": target},
+            device_id_type=MESH_ID,
+        )
+
+    def piece_move(slot, origin, target):
+        view = kept.at[me, span(origin, extra), :]
+        return pltpu.make_async_remote_copy(
+            src_ref=view,
+            dst_ref=view,
+            send_sem=piece_send.at[slot],
+            recv_sem=piece_recv.at[origin],
+            device_id=target,
+            device_id_type=MESH_ID,
+        )
+
+    for one in loads:
+        one.wait()
+    kept[me, pl.ds(pl.multiple_of(80 * rank + 32, 16), 16), :] = to_low(begin_rows[...])
+    for slot in range(3):
+        piece_move(slot, rank, greeted[slot]).start()
+    for slot, target in enumerate(seats):
+        mark_move(slot, place, target).start()
     rows_all[place, span(rank, 128), :] = normed(mine)
     right, left = {"tensor": lax.rem(rank + 1, 4)}, {"tensor": lax.rem(rank + 3, 4)}
     blocks = (place, other)
@@ -1643,6 +1875,7 @@
 
     def rows_steps():
         pass_on(0, 0)
+        fetched(w_qkv, local_sem.at[0])
         moved(place, rank, core_sem.at[0, rank], {"seq": core}).start()
         project(place, rank)
         moved(other, rank, send_sem.at[0, 0, 3], {"seq": other}).wait_recv()
@@ -1692,65 +1925,75 @@
             for origin in range(4):
                 moved(blocks[which], origin, core_sem.at[which, origin], {"seq": core}).wait_send()
 
-    def piece_move(slot, origin, target):
-        view = kept.at[me, span(origin, extra), :]
-        return pltpu.make_async_remote_copy(
-            src_ref=view,
-            dst_ref=view,
-            send_sem=piece_send.at[slot],
-            recv_sem=piece_recv.at[origin],
-            device_id=target,
-            device_id_type=MESH_ID,
-        )
-
     def piece_steps():
         for slot in range(3):
-            piece_move(slot, rank, greeted[slot]).start()
-        first = line[...]
+            piece_move(slot, lax.rem(rank + slot + 1, 4), greeted[slot]).wait_recv()
+        for _ in plane_gather(row_halves(kept, 4 * extra), ring_send, ring_recv):
+            yield
+        for slot in range(3):
+            piece_move(slot, rank, greeted[slot]).wait_send()
+
+    def bias_steps():
+        lane = lax.broadcasted_iota(jnp.int32, (8, WIDE), 1)
+        bucket_ids = bucket_of(jnp.where(lane >= WIDE - BLOCK, lane - WIDE - BLOCK, lane - BLOCK))
+        first = jnp.zeros((8, WIDE), jnp.float32)
+        for bucket_id in range(BUCKETS):
+            first = jnp.where(bucket_ids == bucket_id, rel_bias[bucket_id, half], first)
         row = lax.broadcasted_iota(jnp.int32, (8, WIDE), 0)
         for step in (1, 2, 4):
             first = jnp.where(row // step % 2 == 1, pltpu.roll(first, step, 1), first)
+        bias_rows[...] = first
+        yield
 
         def one(group, _):
-            table[span(group, 8), :] = pltpu.roll(first, 8 * group, 1)[:, 0 : 2 * BLOCK]
+            table[span(group, 8), :] = pltpu.roll(bias_rows[...], 8 * group, 1)[:, 0 : 2 * BLOCK]
             return 0
 
-        lax.fori_loop(0, BLOCK // 8, one, 0)
-        yield
-        for slot in range(3):
-            piece_move(slot, lax.rem(rank + slot + 1, 4), greeted[slot]).wait_recv()
-        for _ in plane_gather(kept, 4 * extra, ring_send, ring_recv):
+        for part in range(4):
+            lax.fori_loop(16 * part, 16 * part + 16, one, 0)
             yield
-        for slot in range(3):
-            piece_move(slot, rank, greeted[slot]).wait_send()
-
-    run_all(rows_steps(), piece_steps())
+
+    run_all(rows_steps(), piece_steps(), bias_steps())
     aside.wait_send()
-
-
-def opening(tokens, w_qkv, piece, vecs, line):
+    for slot, target in enumerate(seats):
+        mark_move(slot, place, target).wait_send()
+        mark_move(slot, target, target).wait_recv()
+
+
+def opening(tokens, w_query, w_key, w_value, w_sout, w_out, begin, vecs, rel_bias, marks):
     low, wide = jnp.bfloat16, jnp.float32
-    extra = piece.shape[0]
     shapes = (
         ((4, BLOCK, D), low),
         ((4, BLOCK, 384), low),
-        ((8, 4 * extra, D), low),
+        ((8, 4 * 80, D), low),
         ((BLOCK, 2 * BLOCK), wide),
-    )
-    return pl.pallas_call(
+        ((4, 8, 128), jnp.int32),
+        ((D, 384), low),
+    )
+    dma = pltpu.SemaphoreType.DMA
+    outs = pl.pallas_call(
         opening_kernel,
         out_shape=[jax.ShapeDtypeStruct(*one) for one in shapes],
-        in_specs=vmem_specs(5),
-        out_specs=vmem_specs(4),
+        in_specs=vmem_specs(1)
+        + any_specs(6)
+        + vmem_specs(1)
+        + [pl.BlockSpec(memory_space=pltpu.SMEM)]
+        + vmem_specs(1),
+        out_specs=vmem_specs(6),
         scratch_shapes=[
+            pltpu.VMEM((16, D), wide),
+            pltpu.VMEM((8, WIDE), wide),
             pltpu.VMEM((128, D), low),
-            pltpu.SemaphoreType.DMA((2, 4, 4)),
-            pltpu.SemaphoreType.DMA((2, 4)),
-            pltpu.SemaphoreType.DMA((4, 4)),
-            pltpu.SemaphoreType.DMA((3,)),
-            pltpu.SemaphoreType.DMA((4,)),
-            pltpu.SemaphoreType.DMA((16,)),
-            pltpu.SemaphoreType.DMA((8, 2)),
+            dma((2, 4, 4)),
+            dma((2, 4)),
+            dma((4, 4)),
+            dma((3,)),
+            dma((4,)),
+            dma((14,)),
+            dma((8, 2)),
+            dma((3,)),
+            dma((4,)),
+            dma((4,)),
         ],
         compiler_params=pltpu.CompilerParams(
             collective_id=5, has_side_effects=True, vmem_limit_bytes=VMEM_LIMIT
@@ -1759,7 +2002,9 @@
             flops=30000000000, bytes_accessed=30000000, transcendentals=0
         ),
         name="opening",
-    )(tokens, w_qkv, piece, vecs, line)
+    )(tokens, w_query, w_key, w_value, w_sout, w_out, begin, vecs, rel_bias, marks)
+    rows_all, qkv, kept, table, marks, w_qkv = outs
+    return rows_all, qkv, kept.reshape(8, 4, 80, D), table, marks, w_qkv
 
 
 def pair_sum(part, near_got, far_got, result, rows, send_sem, recv_sem):
@@ -2099,7 +2344,7 @@
         for target in range(1, 4):
             acc = acc + z_got[target].astype(jnp.float32)
         sout_out[me] = to_low(acc)
-        for _ in plane_gather(sout_out, 64, gather_send, gather_recv):
+        for _ in plane_gather(row_halves(sout_out, 64), gather_send, gather_recv):
             yield
         for one in out:
             one.wait_send()
@@ -2314,71 +2559,52 @@
     mine = place // 2
     plane = ("dp", "seq")
     spot = 4 * lax.axis_index("dp") + place
-    head_of = lambda weight: lax.dynamic_slice_in_dim(weight, half * 128, 128, 1)
     gate_value = jax.nn.sigmoid(gate_bias)
     vecs = jnp.stack(
         [state_gain, gate_value, mlp_gain, attn_gain] + [jnp.zeros_like(gate_value)] * 4
     )
-    offsets = jnp.arange(WIDE) - BLOCK
-    offsets = jnp.where(offsets >= WIDE - 2 * BLOCK, offsets - WIDE, offsets)
-    bucket_ids = bucket_of(offsets)
-    one_hot = bucket_ids[:, None] == jnp.arange(BUCKETS)[None, :]
-    my_bias = jnp.where(half == 0, rel_bias[:, 0], rel_bias[:, 1])
-    bias_line = jnp.sum(jnp.where(one_hot, my_bias[None, :], 0.0), axis=1)
-    segs = jnp.broadcast_to(jnp.repeat(seg_starts[:, 0], 2)[:, None, None], (4, 1, 128))
-    segs = swap_seq(segs)[:, 0, 0]
-    cots = swap_seq(state_cot.reshape(4, 64, D))
+    marks = jnp.concatenate([seg_starts[:, 0], lengths, jnp.zeros((4,), jnp.int32)])
+    marks = jnp.broadcast_to(marks[:, None], (8, 128))
     cot_used = lax.all_gather(out_cot.reshape(256, D), plane, axis=0, tiled=True)
-
-    w_qkv = jnp.concatenate([head_of(w_query), head_of(w_key), head_of(w_value)], axis=1)
-    w_state = jnp.concatenate([head_of(w_squery), w_qkv[:, 128:]], axis=1)
-    piece = jnp.concatenate(
-        [
-            lax.dynamic_slice_in_dim(w_sout, spot * 32, 32, 0),
-            to_low(lax.dynamic_slice_in_dim(init_state, spot * 16, 16, 0)),
-            lax.dynamic_slice_in_dim(w_out, spot * 32, 32, 0),
-        ],
-        axis=0,
-    )
-    rows_all, qkv, kept, bias = opening(
-        inputs, w_qkv, piece, vecs, jnp.broadcast_to(bias_line[None, :], (8, WIDE))
-    )
-    kept = kept.reshape(8, 4, 80, D)
+    rows_all, qkv, kept, bias, marks, w_qkv = opening(
+        inputs, w_query, w_key, w_value, w_sout, w_out, init_state, vecs, rel_bias, marks
+    )
 
     ff_own = w_up.shape[1] // 8
     piece_of = lambda weight: lax.dynamic_slice_in_dim(weight, spot * 32, 32, 1).T
-    pieces = jnp.concatenate(
+    back_own = jnp.stack(
         [
             piece_of(w_squery),
             piece_of(w_key),
             piece_of(w_value),
+        ]
+    )
+    pieces = jnp.concatenate(
+        [
             lax.dynamic_slice_in_dim(w_up, spot * ff_own, ff_own, 1).T,
             lax.dynamic_slice_in_dim(w_down, spot * ff_own, ff_own, 0),
         ],
         axis=0,
     )
-    qkv, pieces, segs, cot_used = lax.optimization_barrier((qkv, pieces, segs, cot_used))
-    scal = jnp.concatenate([lax.dynamic_slice_in_dim(lengths, mine, 1, 0), segs])
-    spread = lax.all_gather(pieces, "tensor", axis=0, tiled=True).reshape(4, 96 + 2 * ff_own, D)
-    mixed, lse_tok, state_rows, state_low, qkvst, lse_st, os_rows = forward_chain(
-        scal, qkv, kept, w_state, vecs, bias
-    )
-    mixed, back_piece, cots = lax.optimization_barrier(
-        (mixed, spread[:, 0:96].reshape(384, D), cots)
-    )
-    w_back = lax.all_gather(back_piece, plane, axis=0, tiled=True)
+    qkv, pieces, cot_used, back_own = lax.optimization_barrier(
+        (qkv, pieces, cot_used, back_own)
+    )
+    spread = lax.all_gather(pieces, "tensor", axis=0, tiled=True).reshape(4, 2 * ff_own, D)
+    mixed, lse_tok, state_rows, state_low, qkvst, lse_st, os_rows, cots, back = forward_chain(
+        marks, qkv, kept, w_squery, w_qkv, vecs, bias, state_cot.reshape(4, 64, D), back_own
+    )
     hidden_in, grad_hidden, d_mixed, mlp_sums, extra, ff_grads = middle(
         mixed, inputs, kept, spread, cot_used.reshape(8, 256, D), vecs
     )
-    d_mixed, w_back, ff_grads = lax.optimization_barrier((d_mixed, w_back, ff_grads))
+    d_mixed, ff_grads = lax.optimization_barrier((d_mixed, ff_grads))
     ff_sum = lax.psum_scatter(
         ff_grads.reshape(ff_grads.shape[2] * 8, D), "tensor", scatter_dimension=0, tiled=True
     )
     (
         d_qkv, d_qkvst, du_rows, d_start, sums, dz_sum, state_out, tokens_out, out_part,
     ) = backward_chain(
-        scal, qkv, d_mixed, lse_tok, qkvst, lse_st, state_rows, init_state, cots,
-        w_back.reshape(8, 4, 3, 32, D), kept, vecs, bias, extra, hidden_in,
+        marks, qkv, d_mixed, lse_tok, qkvst, lse_st, state_rows, init_state, cots,
+        back, kept, vecs, bias, extra, hidden_in,
     )
     d_qkv, ff_sum = lax.optimization_barrier((d_qkv, ff_sum))
     ff_total = lax.all_gather(ff_sum, plane, axis=0, tiled=True).reshape(8, 2, ff_own, D)

time: 547 us -> 528 us (0.965)
  local copies, waits for them, and re-layouts: 20.7 us -> 12.9 us
  starting transfers between devices: 8.06 us -> 0.56 us
    pallas_call x1, Pallas kernels: 105 us -> 96.1 us  [middle(): pl.pallas_call(middle_kernel, out_shape=[jax.ShapeDtypeStruct(*one) for o...]
    all_to_all x2 -> x0, starting transfers between devices: 7.72 us -> none  [swap_seq(): return lax.all_to_all(value, 'seq', 0, 0, tiled=False)]
  transfers between devices with their start and end apart: 7 -> 4, of which waited for: 0 -> 0; matrix products, arithmetic and copies ran while one was open for 4% -> 2% of each run, Pallas kernels for 89% -> 74%
where the time goes in v1:
time: 528 us; the launch traced here: 527 us
  Pallas kernels  497 us (94%)
  between operations  14.1 us (3%)
  local copies, waits for them, and re-layouts  12.9 us (2%)
    pallas_call x1, Pallas kernels, forward_chain(): pl.pallas_call(forward_kernel, out_shape=[jax.ShapeDtypeStruct(*one) for...  113 us
    pallas_call x1, Pallas kernels, backward_chain(): pl.pallas_call(backward_kernel, out_shape=[jax.ShapeDtypeStruct(*one) for...  104 us
    pallas_call x1, Pallas kernels, closing(): pl.pallas_call(closing_kernel, out_shape=[jax.ShapeDtypeStruct(*one) for...  104 us
    pallas_call x1, Pallas kernels, middle(): pl.pallas_call(middle_kernel, out_shape=[jax.ShapeDtypeStruct(*one) for o...  96.1 us
    pallas_call x1, Pallas kernels, opening(): pl.pallas_call(opening_kernel, out_shape=[jax.ShapeDtypeStruct(*one) for...  68.9 us
    pallas_call x1, Pallas kernels, finish_grads(): pl.pallas_call(finish_kernel, grid=(8,), out_shape=[square] * 4 + [rows]...  11.4 us
  transfers between devices with their start and end apart: 4, of which 0 were waited for; matrix products, arithmetic and copies ran while one was open for 2% of the time, Pallas kernels for 74%

profile of v1, /device:TPU:0, one launch (start us, length us, event | category | flops | bytes accessed | tf_op | source)
XLA Modules:
  0.0 527.1 jit_solution(4493422748650767739)
XLA Ops:
  7.2 0.0 copy-start
  7.2 0.0 copy-start.7
  7.2 0.0 copy-start.12
  7.2 0.0 copy-start.11
  7.2 0.0 all-gather.4.cloned.1.call-start
  7.3 0.0 copy-start.8
  7.3 0.0 copy-start.9
  7.3 0.0 copy-start.10
  7.3 0.0 copy-start.13
  7.3 0.0 copy-start.14
  7.3 0.6 all-gather.4.cloned.1.call-update
  8.0 0.0 all-gather.6.cloned.1.call-start
  8.0 1.3 constant_dynamic-slice_fusion.1
  9.3 0.1 copy.44
  9.4 0.1 copy.45
  9.6 0.0 copy-done.7
  9.6 0.1 constant_dynamic-slice_fusion.3
  9.7 0.1 copy.43
  9.8 0.0 copy-done
  9.9 0.1 constant_dynamic-slice_fusion.5
  9.9 0.1 copy.42
  10.1 0.0 copy-done.12
  10.1 0.7 copy.36.rel_bias
  10.8 0.0 copy-done.11
  10.8 0.0 copy-done.8
  10.8 0.0 copy-done.9
  10.8 0.0 copy-done.10
  10.8 0.0 copy-start.5
  10.9 0.7 stack.31.vecs
  11.5 0.0 copy-done.13
  11.5 0.0 copy-done.14
  11.5 0.1 pad_add_fusion
  11.6 0.7 pad_maximum_fusion.1.back_own
  12.3 1.0 constant_dynamic-slice_fusion.4
  13.3 0.8 pad_maximum_fusion
  14.1 0.7 broadcast_in_dim.12.marks_own
  14.8 68.9 %opening.1 = (bf16[4,512,1024]{2,1,0:T(8,128)(2,1)}, bf16[4,512,384]{2,1,0:T(8,128)(2,1)}, bf16[8,320,1024]{2,1,0:T(8,128)(2,1)}, f32[512,1024]{1,0:T(8,128)}, s...) custom-call(bf16[2,128,1024]{2,1,0:T(8,128)(2,1)} %tokens.5, bf16[1024,256]{1,0:T(8,128)(2,1)} %w_query.1, ...), custom_call_target="tpu_custom_call" | custom-call | flops 30000001024 | bytes 30000000 | tf_op jit(solution)/shard_map/opening/pallas_call | solution.py:1974
  83.6 0.0 copy-done.5
  83.7 0.0 all-gather.4.cloned.1.call-done
  83.7 0.0 all-gather.6.cloned.1.call-update
  83.7 0.2 reduce-scatter.2.cloned.1.call-start
  83.9 113.3 %forward_chain.1 = (bf16[4,512,128]{2,1,0:T(8,128)(2,1)}, f32[4,512,1]{2,1,0:T(8,128)}, f32[4,128,1024]{2,1,0:T(8,128)}, bf16[4,512,1024]{2,1,0:T(8,128)(2,1)}, ...) custom-call(s32[4,8,128]{2,1,0:T(8,128)} %get-tuple-element.68.marks, ...), custom_call_target="tpu_custom_call" | custom-call | flops 60000002048 | bytes 60000000 | tf_op jit(solution)/shard_map/forward_chain/pallas_call | solution.py:891
  197.2 0.0 all-gather.6.cloned.1.call-done
  197.2 96.1 %middle.1 = (f32[2,128,1024]{2,1,0:T(8,128)}, f32[2,128,1024]{2,1,0:T(8,128)}, bf16[4,512,128]{2,1,0:T(8,128)(2,1)}, f32[8,1024]{1,0:T(8,128)}, bf16[8,384,1024]...) custom-call(bf16[4,512,128]{2,1,0:T(8,128)(2,1)} %get-tuple-element.75.mixed, bf16[2,128,1024]{2,1,0:T(8,128)(2,1)} %tokens.5, ...), custom_call_target="tpu_custom_call" | custom-call | flops 60000002048 | bytes 60000000 | tf_op jit(solution)/shard_map/middle/pallas_call | solution.py:1718
  293.3 0.0 reduce-scatter.2.cloned.1.call-update
  293.4 0.3 all-gather.8.cloned.1.call-start
  293.6 0.0 copy-start.6
  293.6 103.7 %backward_chain.1 = (bf16[4,512,384]{2,1,0:T(8,128)(2,1)}, bf16[4,512,384]{2,1,0:T(8,128)(2,1)}, bf16[4,64,1024]{2,1,0:T(8,128)(2,1)}, f32[64,1024]{1,0:T(8,128)...) custom-call(s32[4,8,128]{2,1,0:T(8,128)} %get-tuple-element.68.marks, ...), custom_call_target="tpu_custom_call" | custom-call | flops 40000000000 | bytes 40000000 | tf_op jit(solution)/shard_map/backward_chain/pallas_call | solution.py:1160
  397.4 0.0 reduce-scatter.2.cloned.1.call-done
  397.4 0.0 all-gather.8.cloned.1.call-update
  397.5 0.8 slice.25
  398.2 0.8 fusion.2
  399.1 0.0 copy-done.6
  399.1 0.7 concatenate.11.small
  399.7 103.7 %closing.1 = (f32[2,128,1024]{2,1,0:T(8,128)}, bf16[2,4,160,1024]{3,2,1,0:T(8,128)(2,1)}, bf16[8,64,1024]{2,1,0:T(8,128)(2,1)}, f32[8,1024]{1,0:T(8,128)}) custom-call(bf16[4,512,384]{2,1,0:T(8,128)(2,1)} %get-tuple-element.93.d_qkv, bf16[1024,384]{1,0:T(8,128)(2,1)} %get-tuple-element.72.w_qkv, bf16[2,128,1024]{2,1,0:T(8,128)(2,1)} %tokens.5, ...), custom_call_target="tpu_custom_call" | custom-call | flops 30000001024 | bytes 30000000 | tf_op jit(solution)/shard_map/closing/pallas_call | solution.py:2433
  503.4 0.7 slice_reduce_fusion
  504.1 0.1 reshape_squeeze.3
  504.2 0.6 fusion
  504.8 1.5 fusion.1
  506.3 11.4 %finish_grads.1 = (f32[1024,256]{1,0:T(8,128)}, f32[1024,256]{1,0:T(8,128)}, f32[1024,256]{1,0:T(8,128)}, f32[1024,256]{1,0:T(8,128)}, f32[256,1024]{1,0:T(8,128...) custom-call(bf16[2,640,1024]{2,1,0:T(8,128)(2,1)} %bitcast.36, ...), custom_call_target="tpu_custom_call" | custom-call | tf_op jit(solution)/shard_map/finish_grads/pallas_call | solution.py:2512
  517.8 0.0 copy-start.1
  517.8 0.8 copy.49
  518.6 1.0 copy.50
  519.6 1.0 copy.51
  (12 shorter events, 0.0 us)
Async XLA Ops:
  7.2 2.7 copy-start
  7.2 2.4 copy-start.7
  7.2 2.9 copy-start.12
  7.2 3.6 copy-start.11
  7.2 76.4 %all-gather.4.cloned.1.call-start = ((), (), s32[]{:S(2)}) async-start(), calls=%async_computation.1 | async-start | bytes 4718592 | tf_op jit(solution)/shard_map/all_gather | solution.py:2568
  7.3 3.5 copy-start.8
  7.3 3.5 copy-start.9
  7.3 3.5 copy-start.10
  7.3 4.2 copy-start.13
  7.3 4.2 copy-start.14
  8.0 189.3 %all-gather.6.cloned.1.call-start = ((), (), s32[]{:S(2)}) async-start(), calls=%async_computation.2 | async-start | bytes 2621440 | tf_op jit(solution)/shard_map/all_gather | solution.py:2592
  10.8 72.8 %copy-start.5 = (f32[4,1024]{1,0:T(4,128)}, f32[4,1024]{1,0:T(4,128)S(1)}, u32[]{:S(2)}) copy-start(f32[4,1024]{1,0:T(4,128)S(1)} %broadcast.11) | copy-start | bytes 49156
  83.7 313.7 %reduce-scatter.2.cloned.1.call-start = ((), (), s32[]{:S(2)}) async-start(), calls=%async_computation.3 | async-start | bytes 2621440 | tf_op jit(solution)/shard_map/reduce_scatter | solution.py:2600
  293.4 212.9 %all-gather.8.cloned.1.call-start = ((), (), s32[]{:S(2)}) async-start(), calls=%async_computation.4 | async-start | bytes 4718592 | tf_op jit(solution)/shard_map/all_gather | solution.py:2610
  293.6 105.4 %copy-start.6 = (f32[4,1024]{1,0:T(4,128)S(1)}, f32[4,1024]{1,0:T(4,128)}, u32[]{:S(2)}) copy-start(f32[4,1024]{1,0:T(4,128)} %copy-done.5) | copy-start | bytes 49156
  506.3 11.5 %copy-start.4 = (bf16[2,128,1024]{2,1,0:T(8,128)(2,1)S(1)}, bf16[2,128,1024]{2,1,0:T(8,128)(2,1)}, u32[]{:S(2)}) copy-start(bf16[2,128,1024]{2,1,0:T(8,128)(2,1)} %get-tuple-element.161) | copy-start | bytes 1572868
  506.3 12.3 %copy-start.2 = (f32[2,128,1024]{2,1,0:T(8,128)S(1)}, f32[2,128,1024]{2,1,0:T(8,128)}, u32[]{:S(2)}) copy-start(f32[2,128,1024]{2,1,0:T(8,128)} %get-tuple-element.90) | copy-start | bytes 3145732
  517.8 1.8 copy-start.3
  517.8 2.8 copy-start.1
Sparse Core Ops, SparseCore 0:
  10.0 54.8 all-gather.3
  83.8 61.5 all-gather.5
  293.5 51.8 reduce-scatter.1
  397.6 50.4 all-gather.7

commit v2 on v1

--- a/solution.py
+++ b/solution.py
@@ -1681,16 +1681,21 @@
     for slot, (_, seq_to, rank_to) in enumerate(peers):
         line_copy(slot, here, place, rank, seq_to, rank_to).start()
     d_line[place, span(rank, 128), :] = d_rows[mine, :, span(head, 128)]
-    for index in range(LINE):
-        columns = pl.ds(128 * index, 128)
+    def outer(index, _):
+        columns = span(index, 128)
         part = dot_tn(mixed_rows[0, :, columns], d_low[0]) + dot_tn(
             mixed_rows[1, :, columns], d_low[1]
         )
         part = to_low(part)
         for block in range(4):
             extra[
-                4 * (index % 2) + block, 256 + 32 * (index // 2) : 288 + 32 * (index // 2), :
+                4 * lax.rem(index, 2) + block,
+                pl.ds(pl.multiple_of(256 + 32 * (index // 2), 32), 32),
+                :,
             ] = part[32 * block : 32 * block + 32, :]
+        return 0
+
+    lax.fori_loop(0, LINE, outer, 0)
     for slot, (other, seq_to, rank_to) in enumerate(peers):
         line_copy(slot, other, seq_to, rank_to, seq_to, rank_to).wait_recv()
     for slot, (_, seq_to, rank_to) in enumerate(peers):
@@ -2098,7 +2103,7 @@
     inputs_grad, pair_out, sout_out, small_out,
     rows_all, state_low, d_qkvst, os_rows, du_rows, dz_sum,
     leave, came, sums, got, final, cross, cross_got,
-    pair_part, pair_near, pair_far,
+    pair_whole, pair_part, pair_near, pair_far,
     work, core_got, near_got, far_got, total, z_part, z_got,
     diag, small_z, small_p,
     line_send, line_recv, way_send, way_recv, pair_send, pair_recv, core_sem,
@@ -2266,32 +2271,27 @@
         loads[0].wait()
         loads[1].wait()
         loads[2].wait()
-        for chunk in range(4):
-            if chunk < 3:
-                first = 128 * chunk
-
-                def one(block_id, acc):
-                    acc = acc + dot_tn(d_qkv[block_id, :, first : first + 128], rows_all[block_id])
-                    if chunk > 0:
-                        acc = acc + dot_tn(
-                            d_qkvst[block_id, :, first : first + 128], state_low[block_id]
-                        )
-                    return acc
-
-            else:
-
-                def one(block_id, acc):
-                    return acc + dot_tn(d_qkvst[block_id, :, 0:128], state_low[block_id])
-
-            acc = lax.fori_loop(0, 4, one, jnp.zeros((128, D), jnp.float32))
-            low = to_low(acc)
-            first = 128 * chunk
-            while first < 128 * (chunk + 1):
-                owner, inside = first // 160, first % 160
-                size = min(160 - inside, 128 * (chunk + 1) - first)
-                begin = first - 128 * chunk
-                pair_part[owner, inside : inside + size, :] = low[begin : begin + size, :]
-                first += size
+        def one_part(part, _):
+            token_columns = span(jnp.minimum(part, 2), 128)
+            state_columns = span(lax.rem(part, 3), 128)
+
+            def token_add(block_id, acc):
+                return acc + dot_tn(d_qkv[block_id, :, token_columns], rows_all[block_id])
+
+            def state_add(block_id, acc):
+                return acc + dot_tn(d_qkvst[block_id, :, state_columns], state_low[block_id])
+
+            acc = lax.fori_loop(
+                0, jnp.where(part < 3, 4, 0), token_add, jnp.zeros((128, D), jnp.float32)
+            )
+            acc = lax.fori_loop(0, jnp.where(part > 0, 4, 0), state_add, acc)
+            pair_whole[span(part, 128), :] = to_low(acc)
+            return 0
+
+        lax.fori_loop(0, 4, one_part, 0)
+        for owner in range(3):
+            pair_part[owner] = pair_whole[160 * owner : 160 * owner + 160, :]
+        pair_part[3, 0:32, :] = pair_whole[480:512, :]
         pair_part[3, 32:96, :] = to_low(d_start[...])
         pair_part[3, 96:160, :] = jnp.zeros((64, D), jnp.bfloat16)
         for _ in pair_sum(
@@ -2312,12 +2312,15 @@
     def sout_steps():
         loads[3].wait()
         loads[4].wait()
-        for head in range(LINE):
-            low = to_low(dot_tn(os_rows[:, 128 * head : 128 * head + 128], du_rows[...]))
-            for piece in range(4):
-                work[
-                    4 * (head % 2) + piece, 32 * (head // 2) : 32 * (head // 2) + 32, :
-                ] = low[32 * piece : 32 * piece + 32, :]
+        def one_head(head, _):
+            part = to_low(dot_tn(os_rows[:, span(head, 128)], du_rows[...]))
+            for block in range(4):
+                work[4 * lax.rem(head, 2) + block, span(head // 2, 32), :] = part[
+                    32 * block : 32 * block + 32, :
+                ]
+            return 0
+
+        lax.fori_loop(0, LINE, one_head, 0)
         for _ in plane_scatter(
             work, core_got, near_got, far_got, total, 128, ring_send, ring_recv
         ):
@@ -2449,6 +2452,7 @@
             pltpu.VMEM((2, 128, D), wide),
             pltpu.VMEM((128, D), low),
             pltpu.VMEM((128, D), low),
+            pltpu.VMEM((512, D), low),
             pltpu.VMEM((4, PAIR_ROWS // 4, D), low),
             pltpu.VMEM((4, PAIR_ROWS // 8, D), low),
             pltpu.VMEM((2, PAIR_ROWS // 8, D), low),
@@ -2565,7 +2569,6 @@
     )
     marks = jnp.concatenate([seg_starts[:, 0], lengths, jnp.zeros((4,), jnp.int32)])
     marks = jnp.broadcast_to(marks[:, None], (8, 128))
-    cot_used = lax.all_gather(out_cot.reshape(256, D), plane, axis=0, tiled=True)
     rows_all, qkv, kept, bias, marks, w_qkv = opening(
         inputs, w_query, w_key, w_value, w_sout, w_out, init_state, vecs, rel_bias, marks
     )
@@ -2586,10 +2589,9 @@
         ],
         axis=0,
     )
-    qkv, pieces, cot_used, back_own = lax.optimization_barrier(
-        (qkv, pieces, cot_used, back_own)
-    )
+    qkv, pieces, back_own, cot_own = lax.optimization_barrier((qkv, pieces, back_own, out_cot))
     spread = lax.all_gather(pieces, "tensor", axis=0, tiled=True).reshape(4, 2 * ff_own, D)
+    cot_used = lax.all_gather(cot_own.reshape(256, D), plane, axis=0, tiled=True)
     mixed, lse_tok, state_rows, state_low, qkvst, lse_st, os_rows, cots, back = forward_chain(
         marks, qkv, kept, w_squery, w_qkv, vecs, bias, state_cot.reshape(4, 64, D), back_own
     )

time: 528 us -> 534 us (1.011)
    pallas_call x1, Pallas kernels: 113 us -> 123 us  [forward_chain(): pl.pallas_call(forward_kernel, out_shape=[jax.ShapeDtypeStruct(*one) for...]
    pallas_call x1, Pallas kernels: 68.9 us -> 60.4 us  [opening(): pl.pallas_call(opening_kernel, out_shape=[jax.ShapeDtypeStruct(*one) for...]
  transfers between devices with their start and end apart: 4 -> 4, of which waited for: 0 -> 0; matrix products, arithmetic and copies ran while one was open for 2% -> 1% of each run, Pallas kernels for 74% -> 62%
where the time goes in v2:
time: 534 us; the launch traced here: 533 us
  Pallas kernels  502 us (94%)
  between operations  14.1 us (3%)
  local copies, waits for them, and re-layouts  14 us (3%)
    pallas_call x1, Pallas kernels, forward_chain(): pl.pallas_call(forward_kernel, out_shape=[jax.ShapeDtypeStruct(*one) for...  123 us
    pallas_call x1, Pallas kernels, closing(): pl.pallas_call(closing_kernel, out_shape=[jax.ShapeDtypeStruct(*one) for...  105 us
    pallas_call x1, Pallas kernels, backward_chain(): pl.pallas_call(backward_kernel, out_shape=[jax.ShapeDtypeStruct(*one) for...  104 us
    pallas_call x1, Pallas kernels, middle(): pl.pallas_call(middle_kernel, out_shape=[jax.ShapeDtypeStruct(*one) for o...  98 us
    pallas_call x1, Pallas kernels, opening(): pl.pallas_call(opening_kernel, out_shape=[jax.ShapeDtypeStruct(*one) for...  60.4 us
    pallas_call x1, Pallas kernels, finish_grads(): pl.pallas_call(finish_kernel, grid=(8,), out_shape=[square] * 4 + [rows]...  11.4 us
  transfers between devices with their start and end apart: 4, of which 0 were waited for; matrix products, arithmetic and copies ran while one was open for 1% of the time, Pallas kernels for 62%

profile of v2, /device:TPU:0, one launch (start us, length us, event | category | flops | bytes accessed | tf_op | source)
XLA Modules:
  0.0 533.2 jit_solution(13144155836977722211)
XLA Ops:
  7.2 0.0 copy-start
  7.2 0.0 copy-start.10
  7.2 0.0 copy-start.11
  7.2 0.0 all-gather.4.cloned.1.call-start
  7.3 1.4 constant_dynamic-slice_fusion.1
  8.7 0.1 copy.45
  8.8 0.0 copy-start.12
  8.8 0.0 copy-start.13
  8.8 0.0 copy-start.7
  8.8 0.0 copy-start.8
  8.8 0.0 copy-start.9
  8.8 0.1 copy.44
  9.0 1.1 constant_dynamic-slice_fusion.3
  10.1 0.1 copy.43
  10.2 0.0 copy-done
  10.2 0.1 constant_dynamic-slice_fusion.5
  10.3 0.1 copy.42
  10.4 1.0 constant_dynamic-slice_fusion.4
  11.4 0.0 copy-done.10
  11.4 0.0 copy-done.11
  11.4 0.7 copy.36.rel_bias
  12.1 0.8 pad_maximum_fusion
  13.0 0.7 pad_maximum_fusion.1.back_own
  13.7 0.0 copy-done.12
  13.7 0.0 copy-done.13
  13.7 0.1 pad_add_fusion
  13.7 0.0 copy-done.7
  13.7 0.0 copy-done.8
  13.7 0.0 copy-done.9
  13.8 0.0 copy-start.5
  13.8 0.7 stack.31.vecs
  14.4 0.7 broadcast_in_dim.12.marks_own
  15.1 60.4 %opening.1 = (bf16[4,512,1024]{2,1,0:T(8,128)(2,1)}, bf16[4,512,384]{2,1,0:T(8,128)(2,1)}, bf16[8,320,1024]{2,1,0:T(8,128)(2,1)}, f32[512,1024]{1,0:T(8,128)}, s...) custom-call(bf16[2,128,1024]{2,1,0:T(8,128)(2,1)} %tokens.5, bf16[1024,256]{1,0:T(8,128)(2,1)} %w_query.1, ...), custom_call_target="tpu_custom_call" | custom-call | flops 30000001024 | bytes 30000000 | tf_op jit(solution)/shard_map/opening/pallas_call | solution.py:1979
  75.5 0.0 all-gather.4.cloned.1.call-update
  75.6 0.0 all-gather.6.cloned.1.call-start
  75.6 0.7 all-gather.6.cloned.1.call-update
  76.3 0.2 reduce-scatter.2.cloned.1.call-start
  76.5 122.9 %forward_chain.1 = (bf16[4,512,128]{2,1,0:T(8,128)(2,1)}, f32[4,512,1]{2,1,0:T(8,128)}, f32[4,128,1024]{2,1,0:T(8,128)}, bf16[4,512,1024]{2,1,0:T(8,128)(2,1)}, ...) custom-call(s32[4,8,128]{2,1,0:T(8,128)} %get-tuple-element.68.marks, ...), custom_call_target="tpu_custom_call" | custom-call | flops 60000002048 | bytes 60000000 | tf_op jit(solution)/shard_map/forward_chain/pallas_call | solution.py:891
  199.4 0.0 all-gather.4.cloned.1.call-done
  199.4 0.0 all-gather.6.cloned.1.call-done
  199.5 98.0 %middle.1 = (f32[2,128,1024]{2,1,0:T(8,128)}, f32[2,128,1024]{2,1,0:T(8,128)}, bf16[4,512,128]{2,1,0:T(8,128)(2,1)}, f32[8,1024]{1,0:T(8,128)}, bf16[8,384,1024]...) custom-call(bf16[4,512,128]{2,1,0:T(8,128)(2,1)} %get-tuple-element.75.mixed, bf16[2,128,1024]{2,1,0:T(8,128)(2,1)} %tokens.5, ...), custom_call_target="tpu_custom_call" | custom-call | flops 60000002048 | bytes 60000000 | tf_op jit(solution)/shard_map/middle/pallas_call | solution.py:1723
  297.5 0.0 reduce-scatter.2.cloned.1.call-update
  297.5 0.3 all-gather.8.cloned.1.call-start
  297.8 0.0 copy-start.6
  297.8 104.4 %backward_chain.1 = (bf16[4,512,384]{2,1,0:T(8,128)(2,1)}, bf16[4,512,384]{2,1,0:T(8,128)(2,1)}, bf16[4,64,1024]{2,1,0:T(8,128)(2,1)}, f32[64,1024]{1,0:T(8,128)...) custom-call(s32[4,8,128]{2,1,0:T(8,128)} %get-tuple-element.68.marks, ...), custom_call_target="tpu_custom_call" | custom-call | flops 40000000000 | bytes 40000000 | tf_op jit(solution)/shard_map/backward_chain/pallas_call | solution.py:1160
  402.1 0.0 reduce-scatter.2.cloned.1.call-done
  402.2 0.0 all-gather.8.cloned.1.call-update
  402.2 0.8 slice.25
  403.0 0.8 fusion.2
  403.8 0.7 concatenate.11.small
  404.5 105.1 %closing.1 = (f32[2,128,1024]{2,1,0:T(8,128)}, bf16[2,4,160,1024]{3,2,1,0:T(8,128)(2,1)}, bf16[8,64,1024]{2,1,0:T(8,128)(2,1)}, f32[8,1024]{1,0:T(8,128)}) custom-call(bf16[4,512,384]{2,1,0:T(8,128)(2,1)} %get-tuple-element.93.d_qkv, bf16[1024,384]{1,0:T(8,128)(2,1)} %get-tuple-element.72.w_qkv, bf16[2,128,1024]{2,1,0:T(8,128)(2,1)} %tokens.5, ...), custom_call_target="tpu_custom_call" | custom-call | flops 30000001024 | bytes 30000000 | tf_op jit(solution)/shard_map/closing/pallas_call | solution.py:2436
  509.6 0.7 slice_reduce_fusion
  510.3 0.1 reshape_squeeze.3
  510.4 0.6 fusion
  510.9 1.5 fusion.1
  512.5 11.4 %finish_grads.1 = (f32[1024,256]{1,0:T(8,128)}, f32[1024,256]{1,0:T(8,128)}, f32[1024,256]{1,0:T(8,128)}, f32[1024,256]{1,0:T(8,128)}, f32[256,1024]{1,0:T(8,128...) custom-call(bf16[2,640,1024]{2,1,0:T(8,128)(2,1)} %bitcast.36, ...), custom_call_target="tpu_custom_call" | custom-call | tf_op jit(solution)/shard_map/finish_grads/pallas_call | solution.py:2516
  523.9 0.0 copy-start.3
  523.9 0.0 copy-done.4
  524.0 0.0 copy-start.1
  524.0 0.8 copy.49
  524.8 0.0 copy-done.2
  524.8 1.0 copy.50
  525.7 0.0 copy-done.3
  525.7 1.0 copy.51
  (10 shorter events, 0.0 us)
Async XLA Ops:
  7.2 3.0 copy-start
  7.2 4.2 copy-start.10
  7.2 4.2 copy-start.11
  7.2 192.2 %all-gather.4.cloned.1.call-start = ((), (), s32[]{:S(2)}) async-start(), calls=%async_computation.1 | async-start | bytes 2621440 | tf_op jit(solution)/shard_map/all_gather | solution.py:2593
  8.8 4.9 copy-start.12
  8.8 4.9 copy-start.13
  8.8 4.9 copy-start.7
  8.8 4.9 copy-start.8
  8.8 4.9 copy-start.9
  13.8 61.8 %copy-start.5 = (f32[4,1024]{1,0:T(4,128)}, f32[4,1024]{1,0:T(4,128)S(1)}, u32[]{:S(2)}) copy-start(f32[4,1024]{1,0:T(4,128)S(1)} %broadcast.11) | copy-start | bytes 49156
  75.6 123.9 %all-gather.6.cloned.1.call-start = ((), (), s32[]{:S(2)}) async-start(), calls=%async_computation.2 | async-start | bytes 4718592 | tf_op jit(solution)/shard_map/all_gather | solution.py:2594
  76.3 325.9 %reduce-scatter.2.cloned.1.call-start = ((), (), s32[]{:S(2)}) async-start(), calls=%async_computation.3 | async-start | bytes 2621440 | tf_op jit(solution)/shard_map/reduce_scatter | solution.py:2602
  297.5 215.0 %all-gather.8.cloned.1.call-start = ((), (), s32[]{:S(2)}) async-start(), calls=%async_computation.4 | async-start | bytes 4718592 | tf_op jit(solution)/shard_map/all_gather | solution.py:2612
  297.8 106.1 %copy-start.6 = (f32[4,1024]{1,0:T(4,128)S(1)}, f32[4,1024]{1,0:T(4,128)}, u32[]{:S(2)}) copy-start(f32[4,1024]{1,0:T(4,128)} %copy-done.5) | copy-start | bytes 49156
  512.5 11.5 %copy-start.4 = (bf16[2,128,1024]{2,1,0:T(8,128)(2,1)S(1)}, bf16[2,128,1024]{2,1,0:T(8,128)(2,1)}, u32[]{:S(2)}) copy-start(bf16[2,128,1024]{2,1,0:T(8,128)(2,1)} %get-tuple-element.161) | copy-start | bytes 1572868
  512.5 12.3 %copy-start.2 = (f32[2,128,1024]{2,1,0:T(8,128)S(1)}, f32[2,128,1024]{2,1,0:T(8,128)}, u32[]{:S(2)}) copy-start(f32[2,128,1024]{2,1,0:T(8,128)} %get-tuple-element.90) | copy-start | bytes 3145732
  523.9 1.8 copy-start.3
  524.0 2.8 copy-start.1
Sparse Core Ops, SparseCore 0:
  75.7 62.4 all-gather.3
  140.0 52.2 all-gather.5
  297.6 51.9 reduce-scatter.1
  402.3 48.4 all-gather.7

commit v3 on v1

--- a/solution.py
+++ b/solution.py
@@ -924,11 +924,12 @@
 
 def backward_kernel(
     scal, qkv, d_o, lse_tok, qkvst, lse_st, state_rows, begin, cots, back, kept, vecs, bias,
-    extra, hidden,
-    d_qkv, d_qkvst, du_rows, d_start, sums, dz_sum, state_out, tokens_out, out_part,
+    extra, hidden, rows_hbm, low_hbm, w_qkv,
+    du_rows, d_start, sums, state_out, tokens_out, out_part, partial, pair_grads,
+    dz_sum, diag, d_qkv, d_qkvst, rows_buf, low_buf, leave, came, grad_acc,
     key_acc, value_acc, st_key, st_value, dos_rows, dos_got, d_got, grad_in,
     states, w_back, w_sout, work, core_got, near_got, far_got, total,
-    send_sem, recv_sem, local_sem, side_sem, ring_send, ring_recv,
+    send_sem, recv_sem, local_sem, side_sem, ring_send, ring_recv, buf_sem, core_sem, came_sem,
 ):
     place, half, rank = line_place()
     own_rows = pl.ds(pl.multiple_of(half * 64, 64), 64)
@@ -949,6 +950,18 @@
             back.at[owner], w_back.at[:, owner // 4, :, owner % 4], local_sem.at[2]
         ).start()
     states[0] = to_low(begin[own_rows, :]).astype(jnp.float32)
+
+    def block_loads(block_id):
+        slot = lax.rem(block_id, 2)
+        return [
+            pltpu.make_async_copy(
+                source.at[block_id], target.at[slot], buf_sem.at[index, slot]
+            )
+            for index, (source, target) in enumerate(((rows_hbm, rows_buf), (low_hbm, low_buf)))
+        ]
+
+    for one in block_loads(3):
+        one.start()
     head = 2 * rank + half
     peers = []
     for step in range(1, LINE):
@@ -986,6 +999,108 @@
     dz_sum[...] = jnp.zeros_like(dz_sum)
     sums[...] = jnp.zeros_like(sums)
     grad_in[...] = jnp.zeros_like(grad_in)
+    grad_acc[...] = jnp.zeros_like(grad_acc)
+    core = place + 1 - 2 * half
+
+    def place_in(block_id, owner):
+        return jnp.where(block_id == owner, 1, 0)
+
+    def leaving(slot):
+        return pltpu.make_async_remote_copy(
+            src_ref=leave.at[slot],
+            dst_ref=came.at[slot],
+            send_sem=core_sem.at[slot],
+            recv_sem=came_sem.at[slot],
+            device_id={"seq": core},
+            device_id_type=MESH_ID,
+        )
+
+    def add_came(slot):
+        leaving(slot).wait_recv()
+
+        def one(chunk, _):
+            partial[slot, chunk] = to_low(
+                partial[slot, chunk].astype(jnp.float32)
+                + came[slot, span(chunk, 128), :].astype(jnp.float32)
+            )
+            return 0
+
+        lax.fori_loop(0, 4, one, 0)
+
+    def bucket_sums():
+        diag[...] = jnp.zeros_like(diag)
+
+        def one(group, _):
+            rows = dz_sum[span(group, 8), :]
+            wide = jnp.concatenate([rows, jnp.zeros((8, WIDE - 2 * BLOCK), jnp.float32)], axis=1)
+            diag[...] += pltpu.roll(wide, lax.rem(WIDE - 8 * group, WIDE), 1)
+            return 0
+
+        lax.fori_loop(0, BLOCK // 8, one, 0)
+        line = diag[...]
+        row = lax.broadcasted_iota(jnp.int32, (8, WIDE), 0)
+        for step in (1, 2, 4):
+            line = jnp.where(row // step % 2 == 1, pltpu.roll(line, WIDE - step, 1), line)
+        lane = lax.broadcasted_iota(jnp.int32, (8, WIDE), 1)
+        bucket_ids = bucket_of(jnp.where(lane >= WIDE - BLOCK, lane - WIDE - BLOCK, lane - BLOCK))
+        spot = lax.broadcasted_iota(jnp.int32, (1, 256), 1) - BUCKETS * head
+        placed = jnp.zeros((1, 256), jnp.float32)
+        for bucket_id in range(BUCKETS):
+            chosen = jnp.where(bucket_ids == bucket_id, line, 0.0)
+            value = jnp.sum(jnp.sum(chosen, axis=0, keepdims=True), axis=1, keepdims=True)
+            placed = jnp.where(spot == bucket_id, value, placed)
+        sums[2:3, 0:256] = placed
+
+    def block_products(block_id):
+        slot = lax.rem(block_id, 2)
+        for one in block_loads(block_id):
+            one.wait()
+
+        @pl.when(block_id > 0)
+        def _():
+            for one in block_loads(jnp.maximum(block_id - 1, 0)):
+                one.start()
+
+        def one_part(part, _):
+            rows = span(part, 128)
+
+            @pl.when(part < 3)
+            def _():
+                grad_acc[rows, :] += dot_tn(
+                    d_qkv[block_id, :, span(jnp.minimum(part, 2), 128)], rows_buf[slot]
+                )
+
+            @pl.when(part > 0)
+            def _():
+                grad_acc[rows, :] += dot_tn(
+                    d_qkvst[block_id, :, span(lax.rem(part, 3), 128)], low_buf[slot]
+                )
+
+            return 0
+
+        lax.fori_loop(0, 4, one_part, 0)
+        kept_here = lax.rem(block_id, 2) == half
+        mine_slot, core_slot = place_in(block_id, place), place_in(block_id, core)
+
+        def one_chunk(chunk, _):
+            rows = span(chunk, 128)
+            value = to_low(dot_nt(d_qkv[block_id, rows, :], w_qkv[...]))
+
+            @pl.when(kept_here)
+            def _():
+                partial[mine_slot, chunk] = value
+
+            @pl.when(jnp.logical_not(kept_here))
+            def _():
+                leave[core_slot, rows, :] = value
+
+            return 0
+
+        lax.fori_loop(0, 4, one_chunk, 0)
+
+        @pl.when(jnp.logical_not(kept_here))
+        def _():
+            leaving(core_slot).start()
 
     def back_parts(parts, total, grad, values):
         weights = [jnp.exp(part - total) for part in parts]
@@ -1096,12 +1211,22 @@
             def _():
                 next(plane_steps, None)
 
+        @pl.when(turn == 3)
+        def _():
+            bucket_sums()
+
         @pl.when(turn < 3)
         def _():
             token_back(block_id - 1)
 
         d_qkv[block_id, :, 128:256] = to_low(key_acc[block_id])
         d_qkv[block_id, :, 256:384] = to_low(value_acc[block_id])
+        block_products(block_id)
+
+        @pl.when(turn == 2)
+        def _():
+            add_came(place_in(2 + half, place))
+
         for slot, (other, seq_to, rank_to) in enumerate(peers):
             grads_copy(block_id, slot, other, other, seq_to, rank_to).wait_recv()
         d_low = dot_nn(d_got[block_id, 0], w_back[0, 0].reshape(384, D))
@@ -1130,8 +1255,12 @@
         return 0
 
     lax.fori_loop(0, 4, drain, 0)
+    pair_grads[...] = to_low(grad_acc[...])
     for _ in plane_steps:
         pass
+    add_came(place_in(half, place))
+    for slot in range(2):
+        leaving(slot).wait_send()
     for which in range(2):
         rows = pl.ds(128 * which, 128)
         tokens_out[which] = to_low(hidden[which] + total[rows, :])
@@ -1143,19 +1272,18 @@
 
 def backward_chain(
     scal, qkv, d_o, lse_tok, qkvst, lse_st, state_rows, begin, cots, back, kept, vecs, bias,
-    extra, hidden,
+    extra, hidden, rows_all, state_low, w_qkv,
 ):
     low, wide = jnp.bfloat16, jnp.float32
     shapes = (
-        ((4, BLOCK, 384), low),
-        ((4, STATES, 384), low),
         ((4, 64, D), low),
         ((64, D), wide),
         ((8, D), wide),
-        ((BLOCK, 2 * BLOCK), wide),
         ((2, 128, D), wide),
         ((2, 128, D), low),
         ((128, D), low),
+        ((2, 4, 128, D), low),
+        ((512, D), low),
     )
     return pl.pallas_call(
         backward_kernel,
@@ -1166,9 +1294,20 @@
         + any_specs(2)
         + vmem_specs(2)
         + any_specs(1)
+        + vmem_specs(1)
+        + any_specs(2)
         + vmem_specs(1),
-        out_specs=vmem_specs(6) + any_specs(1) + vmem_specs(2),
+        out_specs=vmem_specs(3) + any_specs(1) + vmem_specs(4),
         scratch_shapes=[
+            pltpu.VMEM((BLOCK, 2 * BLOCK), wide),
+            pltpu.VMEM((8, WIDE), wide),
+            pltpu.VMEM((4, BLOCK, 384), low),
+            pltpu.VMEM((4, STATES, 384), low),
+            pltpu.VMEM((2, BLOCK, D), low),
+            pltpu.VMEM((2, STATES, D), low),
+            pltpu.VMEM((2, BLOCK, D), low),
+            pltpu.VMEM((2, BLOCK, D), low),
+            pltpu.VMEM((512, D), wide),
             pltpu.VMEM((4, BLOCK, 128), wide),
             pltpu.VMEM((4, BLOCK, 128), wide),
             pltpu.VMEM((STATES, 128), wide),
@@ -1191,6 +1330,9 @@
             pltpu.SemaphoreType.DMA((2,)),
             pltpu.SemaphoreType.DMA((10,)),
             pltpu.SemaphoreType.DMA((10,)),
+            pltpu.SemaphoreType.DMA((2, 2)),
+            pltpu.SemaphoreType.DMA((2,)),
+            pltpu.SemaphoreType.DMA((2,)),
         ],
         compiler_params=pltpu.CompilerParams(
             collective_id=2, has_side_effects=True, vmem_limit_bytes=VMEM_LIMIT
@@ -1199,7 +1341,7 @@
         name="backward_chain",
     )(
         scal, qkv, d_o, lse_tok, qkvst, lse_st, state_rows, begin, cots, back, kept, vecs, bias,
-        extra, hidden,
+        extra, hidden, rows_all, state_low, w_qkv,
     )
 
 
@@ -2093,14 +2235,13 @@
 
 
 def closing_kernel(
-    d_qkv, w_qkv, tokens, d_hidden, vecs, rows_hbm, low_hbm, d_qkvst_hbm, os_hbm, du_hbm,
-    d_start, dz_hbm, small, out_part,
+    partial, pair_grads, tokens, d_hidden, vecs, os_hbm, du_hbm, d_start, small,
+    out_part,
     inputs_grad, pair_out, sout_out, small_out,
-    rows_all, state_low, d_qkvst, os_rows, du_rows, dz_sum,
-    leave, came, sums, got, final, cross, cross_got,
+    os_rows, du_rows, sums, got, final, cross, cross_got,
     pair_part, pair_near, pair_far,
     work, core_got, near_got, far_got, total, z_part, z_got,
-    diag, small_z, small_p,
+    small_z, small_p,
     line_send, line_recv, way_send, way_recv, pair_send, pair_recv, core_sem,
     ring_send, ring_recv, zs_send, zs_recv, gather_send, gather_recv, small_send, small_recv, local_sem,
 ):
@@ -2108,12 +2249,9 @@
         pltpu.make_async_copy(source, target, local_sem.at[slot])
         for slot, (source, target) in enumerate(
             (
-                (rows_hbm, rows_all),
-                (d_qkvst_hbm, d_qkvst),
-                (low_hbm, state_low),
+                (partial, sums),
                 (os_hbm, os_rows),
                 (du_hbm, du_rows),
-                (dz_hbm, dz_sum),
             )
         )
     ]
@@ -2149,13 +2287,8 @@
             device_id_type=MESH_ID,
         )
 
-    def to_core(which):
-        return moved(
-            leave.at[which], came.at[which], line_send.at[which], line_recv.at[which], {"seq": core}
-        )
-
     def crossing():
-        return moved(cross, cross_got, line_send.at[2], line_recv.at[2], {"seq": other})
+        return moved(cross, cross_got, line_send.at[0], line_recv.at[0], {"seq": other})
 
     near = rank // 2
     at_end = (rank == 0) | (rank == 3)
@@ -2203,29 +2336,9 @@
             final[which] += got[1, which, rank].astype(jnp.float32)
 
     def line_steps():
-        for which, block_id in enumerate((lax.rem(core + 2, 4), core)):
-
-            def partner(chunk, _):
-                rows = span(chunk, ROWS)
-                leave[which, rows, :] = to_low(dot_nt(d_qkv[block_id, rows, :], w_qkv[...]))
-                return 0
-
-            lax.fori_loop(0, CHUNKS, partner, 0)
-            if which == 0:
-                pl.semaphore_wait(barrier, 10)
-            to_core(which).start()
-        for which, block_id in enumerate((other, place)):
-            to_core(which).wait_recv()
-
-            def own(chunk, _):
-                rows = span(chunk, ROWS)
-                sums[which, chunk] = to_low(
-                    dot_nt(d_qkv[block_id, rows, :], w_qkv[...])
-                    + came[which, rows, :].astype(jnp.float32)
-                )
-                return 0
-
-            lax.fori_loop(0, CHUNKS, own, 0)
+        loads[0].wait()
+        pl.semaphore_wait(barrier, 10)
+        for which in (0, 1):
             pass_first(which)
         yield
         for which in (0, 1):
@@ -2255,7 +2368,6 @@
             )
         crossing().wait_send()
         for which in (0, 1):
-            to_core(which).wait_send()
             for target in range(4):
 
                 @pl.when(rank != target)
@@ -2263,35 +2375,9 @@
                     hop(0, which, target).wait_send()
 
     def pair_steps():
-        loads[0].wait()
-        loads[1].wait()
-        loads[2].wait()
-        for chunk in range(4):
-            if chunk < 3:
-                first = 128 * chunk
-
-                def one(block_id, acc):
-                    acc = acc + dot_tn(d_qkv[block_id, :, first : first + 128], rows_all[block_id])
-                    if chunk > 0:
-                        acc = acc + dot_tn(
-                            d_qkvst[block_id, :, first : first + 128], state_low[block_id]
-                        )
-                    return acc
-
-            else:
-
-                def one(block_id, acc):
-                    return acc + dot_tn(d_qkvst[block_id, :, 0:128], state_low[block_id])
-
-            acc = lax.fori_loop(0, 4, one, jnp.zeros((128, D), jnp.float32))
-            low = to_low(acc)
-            first = 128 * chunk
-            while first < 128 * (chunk + 1):
-                owner, inside = first // 160, first % 160
-                size = min(160 - inside, 128 * (chunk + 1) - first)
-                begin = first - 128 * chunk
-                pair_part[owner, inside : inside + size, :] = low[begin : begin + size, :]
-                first += size
+        for owner in range(3):
+            pair_part[owner] = pair_grads[160 * owner : 160 * owner + 160, :]
+        pair_part[3, 0:32, :] = pair_grads[480:512, :]
         pair_part[3, 32:96, :] = to_low(d_start[...])
         pair_part[3, 96:160, :] = jnp.zeros((64, D), jnp.bfloat16)
         for _ in pair_sum(
@@ -2310,8 +2396,8 @@
         full.wait_send()
 
     def sout_steps():
-        loads[3].wait()
-        loads[4].wait()
+        loads[1].wait()
+        loads[2].wait()
         for head in range(LINE):
             low = to_low(dot_tn(os_rows[:, 128 * head : 128 * head + 128], du_rows[...]))
             for piece in range(4):
@@ -2349,41 +2435,7 @@
         for one in out:
             one.wait_send()
 
-    def diag_steps():
-        loads[5].wait()
-        diag[...] = jnp.zeros_like(diag)
-        for part in range(4):
-
-            def one(group, _):
-                rows = dz_sum[span(group, 8), :]
-                wide = jnp.concatenate(
-                    [rows, jnp.zeros((8, WIDE - 2 * BLOCK), jnp.float32)], axis=1
-                )
-                diag[...] += pltpu.roll(wide, lax.rem(WIDE - 8 * group, WIDE), 1)
-                return 0
-
-            lax.fori_loop(16 * part, 16 * part + 16, one, 0)
-            yield
-        total_line = diag[...]
-        row = lax.broadcasted_iota(jnp.int32, (8, WIDE), 0)
-        for step in (1, 2, 4):
-            total_line = jnp.where(
-                row // step % 2 == 1, pltpu.roll(total_line, WIDE - step, 1), total_line
-            )
-        lane = lax.broadcasted_iota(jnp.int32, (8, WIDE), 1)
-        offset = jnp.where(lane >= WIDE - BLOCK, lane - WIDE - BLOCK, lane - BLOCK)
-        bucket_ids = bucket_of(offset)
-        spot = lax.broadcasted_iota(jnp.int32, (1, 256), 1) - BUCKETS * (2 * rank + half)
-        placed = jnp.zeros((1, 256), jnp.float32)
-        for bucket_id in range(BUCKETS):
-            chosen = jnp.where(bucket_ids == bucket_id, total_line, 0.0)
-            value = jnp.sum(jnp.sum(chosen, axis=0, keepdims=True), axis=1, keepdims=True)
-            placed = jnp.where(spot == bucket_id, value, placed)
-        diag[0:1, 0:256] = placed
-
-    extra = sout_steps()
-    run_all(line_steps(), pair_steps(), extra, diag_steps(), extra)
-    small_z[rank, 4:5, 0:256] = diag[0:1, 0:256]
+    run_all(sout_steps(), line_steps(), pair_steps())
 
     def small_over_z(slot, sender, target):
         return moved(
@@ -2419,8 +2471,8 @@
 
 
 def closing(
-    d_qkv, w_qkv, tokens, d_hidden, vecs, rows_all, state_low, d_qkvst, os_rows, du_rows,
-    d_start, dz_sum, small, out_part,
+    partial, pair_grads, tokens, d_hidden, vecs, os_rows, du_rows, d_start, small,
+    out_part,
 ):
     low, wide = jnp.bfloat16, jnp.float32
     shapes = (
@@ -2433,17 +2485,14 @@
     return pl.pallas_call(
         closing_kernel,
         out_shape=[jax.ShapeDtypeStruct(*one) for one in shapes],
-        in_specs=vmem_specs(5) + any_specs(5) + vmem_specs(1) + any_specs(1) + vmem_specs(2),
+        in_specs=any_specs(1)
+        + vmem_specs(4)
+        + any_specs(2)
+        + vmem_specs(3),
         out_specs=vmem_specs(4),
         scratch_shapes=[
-            pltpu.VMEM((4, BLOCK, D), low),
-            pltpu.VMEM((4, BLOCK, D), low),
-            pltpu.VMEM((4, BLOCK, 384), low),
             pltpu.VMEM((256, D), low),
             pltpu.VMEM((256, D), low),
-            pltpu.VMEM((BLOCK, 2 * BLOCK), wide),
-            pltpu.VMEM((2, BLOCK, D), low),
-            pltpu.VMEM((2, BLOCK, D), low),
             pltpu.VMEM((2, 4, 128, D), low),
             pltpu.VMEM((2, 2, 4, 128, D), low),
             pltpu.VMEM((2, 128, D), wide),
@@ -2459,12 +2508,11 @@
             pltpu.VMEM((128, D), wide),
             pltpu.VMEM((4, 64, D), low),
             pltpu.VMEM((4, 64, D), low),
-            pltpu.VMEM((8, WIDE), wide),
             pltpu.VMEM((4, 8, D), wide),
             pltpu.VMEM((8, 8, D), wide),
-            dma((3,)), dma((3,)), dma((2, 4)), dma((2, 2, 4)), dma((12,)), dma((12,)), dma((2,)),
+            dma((1,)), dma((1,)), dma((2, 4)), dma((2, 2, 4)), dma((12,)), dma((12,)), dma((2,)),
             dma((10,)), dma((10,)), dma((3,)), dma((4,)), dma((16,)), dma((8, 2)), dma((10,)),
-            dma((12,)), dma((6,)),
+            dma((12,)), dma((3,)),
         ],
         compiler_params=pltpu.CompilerParams(
             collective_id=6, has_side_effects=True, vmem_limit_bytes=VMEM_LIMIT
@@ -2474,8 +2522,8 @@
         ),
         name="closing",
     )(
-        d_qkv, w_qkv, tokens, d_hidden, vecs, rows_all, state_low, d_qkvst, os_rows, du_rows,
-        d_start, dz_sum, small, out_part,
+        partial, pair_grads, tokens, d_hidden, vecs, os_rows, du_rows, d_start, small,
+        out_part,
     )
 
 
@@ -2601,19 +2649,19 @@
         ff_grads.reshape(ff_grads.shape[2] * 8, D), "tensor", scatter_dimension=0, tiled=True
     )
     (
-        d_qkv, d_qkvst, du_rows, d_start, sums, dz_sum, state_out, tokens_out, out_part,
+        du_rows, d_start, sums, state_out, tokens_out, out_part, partial, pair_grads,
     ) = backward_chain(
         marks, qkv, d_mixed, lse_tok, qkvst, lse_st, state_rows, init_state, cots,
-        back, kept, vecs, bias, extra, hidden_in,
-    )
-    d_qkv, ff_sum = lax.optimization_barrier((d_qkv, ff_sum))
+        back, kept, vecs, bias, extra, hidden_in, rows_all, state_low, w_qkv,
+    )
+    partial, ff_sum = lax.optimization_barrier((partial, ff_sum))
     ff_total = lax.all_gather(ff_sum, plane, axis=0, tiled=True).reshape(8, 2, ff_own, D)
     small = jnp.concatenate(
-        [jnp.zeros((1, D), wide), sums[1:2], mlp_sums[0:1], sums[0:1], jnp.zeros((4, D), wide)]
+        [jnp.zeros((1, D), wide), sums[1:2], mlp_sums[0:1], sums[0:1], sums[2:3], jnp.zeros((3, D), wide)]
     )
     inputs_grad, pair, two_grads, small = closing(
-        d_qkv, w_qkv, inputs, grad_hidden, vecs, rows_all, state_low, d_qkvst,
-        os_rows.reshape(256, D), du_rows.reshape(256, D), d_start, dz_sum, small, out_part,
+        partial, pair_grads, inputs, grad_hidden, vecs, os_rows.reshape(256, D),
+        du_rows.reshape(256, D), d_start, small, out_part,
     )
     pair = pair.reshape(2, PAIR_ROWS, D)
     (

time: 528 us -> 510 us (0.966)
  Pallas kernels: 497 us -> 479 us
    pallas_call x1, Pallas kernels: 104 us -> 83.3 us  [closing(): pl.pallas_call(closing_kernel, out_shape=[jax.ShapeDtypeStruct(*one) for...]
  transfers between devices with their start and end apart: 4 -> 4, of which waited for: 0 -> 0; matrix products, arithmetic and copies ran while one was open for 2% -> 2% of each run, Pallas kernels for 74% -> 73%
where the time goes in v3:
time: 510 us; the launch traced here: 509 us
  Pallas kernels  479 us (94%)
  between operations  14.1 us (3%)
  local copies, waits for them, and re-layouts  13 us (3%)
    pallas_call x1, Pallas kernels, forward_chain(): pl.pallas_call(forward_kernel, out_shape=[jax.ShapeDtypeStruct(*one) for...  113 us
    pallas_call x1, Pallas kernels, backward_chain(): pl.pallas_call(backward_kernel, out_shape=[jax.ShapeDtypeStruct(*one) for...  106 us
    pallas_call x1, Pallas kernels, middle(): pl.pallas_call(middle_kernel, out_shape=[jax.ShapeDtypeStruct(*one) for o...  96.1 us
    pallas_call x1, Pallas kernels, closing(): pl.pallas_call(closing_kernel, out_shape=[jax.ShapeDtypeStruct(*one) for...  83.3 us
    pallas_call x1, Pallas kernels, opening(): pl.pallas_call(opening_kernel, out_shape=[jax.ShapeDtypeStruct(*one) for...  68.9 us
    pallas_call x1, Pallas kernels, finish_grads(): pl.pallas_call(finish_kernel, grid=(8,), out_shape=[square] * 4 + [rows]...  11.4 us
  transfers between devices with their start and end apart: 4, of which 0 were waited for; matrix products, arithmetic and copies ran while one was open for 2% of the time, Pallas kernels for 73%

profile of v3, /device:TPU:0, one launch (start us, length us, event | category | flops | bytes accessed | tf_op | source)
XLA Modules:
  0.0 509.2 jit_solution(11375941294477845358)
XLA Ops:
  7.2 0.0 copy-start
  7.2 0.0 copy-start.5
  7.2 0.0 copy-start.10
  7.2 0.0 copy-start.9
  7.2 0.0 all-gather.4.cloned.1.call-start
  7.3 0.0 copy-start.6
  7.3 0.0 copy-start.7
  7.3 0.0 copy-start.8
  7.3 0.0 copy-start.11
  7.3 0.0 copy-start.12
  7.3 0.6 all-gather.4.cloned.1.call-update
  8.0 0.0 all-gather.6.cloned.1.call-start
  8.0 1.3 constant_dynamic-slice_fusion.1
  9.3 0.1 copy.44
  9.4 0.1 copy.45
  9.6 0.0 copy-done.5
  9.6 0.1 constant_dynamic-slice_fusion.3
  9.7 0.1 copy.43
  9.8 0.0 copy-done
  9.9 0.1 constant_dynamic-slice_fusion.5
  9.9 0.1 copy.42
  10.1 0.0 copy-done.10
  10.1 0.7 copy.36.rel_bias
  10.8 0.0 copy-done.9
  10.8 0.0 copy-done.6
  10.8 0.0 copy-done.7
  10.8 0.0 copy-done.8
  10.8 0.7 stack.35.vecs
  11.5 0.0 copy-done.11
  11.5 0.0 copy-done.12
  11.5 0.1 pad_add_fusion
  11.6 0.7 pad_maximum_fusion.1.back_own
  12.3 1.0 constant_dynamic-slice_fusion.4
  13.2 0.8 pad_maximum_fusion
  14.1 0.7 broadcast_in_dim.15.marks_own
  14.7 68.9 %opening.1 = (bf16[4,512,1024]{2,1,0:T(8,128)(2,1)}, bf16[4,512,384]{2,1,0:T(8,128)(2,1)}, bf16[8,320,1024]{2,1,0:T(8,128)(2,1)}, f32[512,1024]{1,0:T(8,128)}, s...) custom-call(bf16[2,128,1024]{2,1,0:T(8,128)(2,1)} %tokens.5, bf16[1024,256]{1,0:T(8,128)(2,1)} %w_query.1, ...), custom_call_target="tpu_custom_call" | custom-call | flops 30000001024 | bytes 30000000 | tf_op jit(solution)/shard_map/opening/pallas_call | solution.py:2116
  83.6 0.0 all-gather.4.cloned.1.call-done
  83.7 0.0 all-gather.6.cloned.1.call-update
  83.7 0.2 reduce-scatter.2.cloned.1.call-start
  83.9 113.3 %forward_chain.1 = (bf16[4,512,128]{2,1,0:T(8,128)(2,1)}, f32[4,512,1]{2,1,0:T(8,128)}, f32[4,128,1024]{2,1,0:T(8,128)}, bf16[4,512,1024]{2,1,0:T(8,128)(2,1)}, ...) custom-call(s32[4,8,128]{2,1,0:T(8,128)} %get-tuple-element.67.marks, ...), custom_call_target="tpu_custom_call" | custom-call | flops 60000002048 | bytes 60000000 | tf_op jit(solution)/shard_map/forward_chain/pallas_call | solution.py:891
  197.2 0.0 all-gather.6.cloned.1.call-done
  197.2 96.1 %middle.1 = (f32[2,128,1024]{2,1,0:T(8,128)}, f32[2,128,1024]{2,1,0:T(8,128)}, bf16[4,512,128]{2,1,0:T(8,128)(2,1)}, f32[8,1024]{1,0:T(8,128)}, bf16[8,384,1024]...) custom-call(bf16[4,512,128]{2,1,0:T(8,128)(2,1)} %get-tuple-element.74.mixed, bf16[2,128,1024]{2,1,0:T(8,128)(2,1)} %tokens.5, ...), custom_call_target="tpu_custom_call" | custom-call | flops 60000002048 | bytes 60000000 | tf_op jit(solution)/shard_map/middle/pallas_call | solution.py:1860
  293.3 0.0 reduce-scatter.2.cloned.1.call-update
  293.4 0.3 all-gather.8.cloned.1.call-start
  293.6 106.1 %backward_chain.1 = (bf16[4,64,1024]{2,1,0:T(8,128)(2,1)}, f32[64,1024]{1,0:T(8,128)}, f32[8,1024]{1,0:T(8,128)}, f32[2,128,1024]{2,1,0:T(8,128)}, bf16[2,128,10...) custom-call(s32[4,8,128]{2,1,0:T(8,128)} %get-tuple-element.67.marks, ...), custom_call_target="tpu_custom_call" | custom-call | flops 40000000000 | bytes 40000000 | tf_op jit(solution)/shard_map/backward_chain/pallas_call | solution.py:1288
  399.7 0.0 reduce-scatter.2.cloned.1.call-done
  399.8 0.0 all-gather.8.cloned.1.call-update
  399.8 0.8 slice.28
  400.6 0.9 fusion.2
  401.5 0.7 concatenate.11.small
  402.1 83.3 %closing.1 = (f32[2,128,1024]{2,1,0:T(8,128)}, bf16[2,4,160,1024]{3,2,1,0:T(8,128)(2,1)}, bf16[8,64,1024]{2,1,0:T(8,128)(2,1)}, f32[8,1024]{1,0:T(8,128)}) custom-call(bf16[2,4,128,1024]{3,2,1,0:T(8,128)(2,1)} %get-tuple-element.94.partial, bf16[512,1024]{1,0:T(8,128)(2,1)} %get-tuple-element.95.pair_grads, bf16[2,128,1024]{2,1,0:T(8,128)(2,1)} %tokens.5, ...), custom_call_target="tpu_custom_call" | custom-call | flops 30000001024 | bytes 30000000 | tf_op jit(solution)/shard_map/closing/pallas_call | solution.py:2485
  485.5 0.7 slice_reduce_fusion
  486.2 0.1 reshape_squeeze.3
  486.3 0.6 fusion
  486.8 1.5 fusion.1
  488.4 11.4 %finish_grads.1 = (f32[1024,256]{1,0:T(8,128)}, f32[1024,256]{1,0:T(8,128)}, f32[1024,256]{1,0:T(8,128)}, f32[1024,256]{1,0:T(8,128)}, f32[256,1024]{1,0:T(8,128...) custom-call(bf16[2,640,1024]{2,1,0:T(8,128)(2,1)} %bitcast.36, ...), custom_call_target="tpu_custom_call" | custom-call | tf_op jit(solution)/shard_map/finish_grads/pallas_call | solution.py:2560
  499.9 0.0 copy-start.3
  499.9 0.0 copy-done.4
  499.9 0.0 copy-start.1
  499.9 0.8 copy.49
  500.7 0.0 copy-done.2
  500.7 1.0 copy.50
  501.7 0.0 copy-done.3
  501.7 1.0 copy.51
  (9 shorter events, 0.0 us)
Async XLA Ops:
  7.2 2.7 copy-start
  7.2 2.4 copy-start.5
  7.2 2.9 copy-start.10
  7.2 3.6 copy-start.9
  7.2 76.4 %all-gather.4.cloned.1.call-start = ((), (), s32[]{:S(2)}) async-start(), calls=%async_computation.1 | async-start | bytes 4718592 | tf_op jit(solution)/shard_map/all_gather | solution.py:2616
  7.3 3.5 copy-start.6
  7.3 3.5 copy-start.7
  7.3 3.5 copy-start.8
  7.3 4.2 copy-start.11
  7.3 4.2 copy-start.12
  8.0 189.3 %all-gather.6.cloned.1.call-start = ((), (), s32[]{:S(2)}) async-start(), calls=%async_computation.2 | async-start | bytes 2621440 | tf_op jit(solution)/shard_map/all_gather | solution.py:2640
  83.7 316.1 %reduce-scatter.2.cloned.1.call-start = ((), (), s32[]{:S(2)}) async-start(), calls=%async_computation.3 | async-start | bytes 2621440 | tf_op jit(solution)/shard_map/reduce_scatter | solution.py:2648
  293.4 195.0 %all-gather.8.cloned.1.call-start = ((), (), s32[]{:S(2)}) async-start(), calls=%async_computation.4 | async-start | bytes 4718592 | tf_op jit(solution)/shard_map/all_gather | solution.py:2658
  488.4 11.5 %copy-start.4 = (bf16[2,128,1024]{2,1,0:T(8,128)(2,1)S(1)}, bf16[2,128,1024]{2,1,0:T(8,128)(2,1)}, u32[]{:S(2)}) copy-start(bf16[2,128,1024]{2,1,0:T(8,128)(2,1)} %get-tuple-element.160) | copy-start | bytes 1572868
  488.4 12.3 %copy-start.2 = (f32[2,128,1024]{2,1,0:T(8,128)S(1)}, f32[2,128,1024]{2,1,0:T(8,128)}, u32[]{:S(2)}) copy-start(f32[2,128,1024]{2,1,0:T(8,128)} %get-tuple-element.91) | copy-start | bytes 3145732
  499.9 1.8 copy-start.3
  499.9 2.8 copy-start.1
Sparse Core Ops, SparseCore 0:
  10.0 54.7 all-gather.3
  83.8 61.5 all-gather.5
  293.5 51.9 reduce-scatter.1
  399.9 55.0 all-gather.7

commit v4 on v3

--- a/solution.py
+++ b/solution.py
@@ -964,7 +964,7 @@
         one.start()
     head = 2 * rank + half
     peers = []
-    for step in range(1, LINE):
+    for step in (4, 3, 5, 2, 6, 1, 7):
         other = lax.rem(head + step, LINE)
         peers.append((other, place - half + lax.rem(other, 2), other // 2))
     barrier = pltpu.get_barrier_semaphore()
@@ -2235,7 +2235,7 @@
 
 
 def closing_kernel(
-    partial, pair_grads, tokens, d_hidden, vecs, os_hbm, du_hbm, d_start, small,
+    partial, pair_grads, tokens, d_hidden, vecs, os_hbm, du_hbm, d_start, mlp_sums, state_sums,
     out_part,
     inputs_grad, pair_out, sout_out, small_out,
     os_rows, du_rows, sums, got, final, cross, cross_got,
@@ -2335,6 +2335,19 @@
             hop(1, which, rank).wait_recv()
             final[which] += got[1, which, rank].astype(jnp.float32)
 
+    def small_over_z(slot, sender, target):
+        return moved(
+            small_z.at[sender], small_z.at[sender], small_send.at[slot], small_recv.at[sender],
+            {"tensor": target},
+        )
+
+    def small_over_plane(slot, sender, target):
+        return moved(
+            small_p.at[sender], small_p.at[sender], small_send.at[3 + slot],
+            small_recv.at[4 + sender],
+            {"dp": target // 4, "seq": lax.rem(target, 4)},
+        )
+
     def line_steps():
         loads[0].wait()
         pl.semaphore_wait(barrier, 10)
@@ -2354,7 +2367,11 @@
             yield
         crossing().wait_recv()
         final[0] = cross_got[...].astype(jnp.float32)
-        small_z[rank] = small[...]
+        small_z[rank] = jnp.zeros((8, D), jnp.float32)
+        for row, source in enumerate(
+            (state_sums[1:2, :], mlp_sums[0:1, :], state_sums[0:1, :], state_sums[2:3, :])
+        ):
+            small_z[rank, row + 1 : row + 2, :] = source
         for which, row_set in ((1, mine), (0, 1 - mine)):
             grad = final[which]
             centered, scale = norm_parts(tokens[row_set].astype(jnp.float32))
@@ -2366,7 +2383,26 @@
                 - jnp.mean(lifted, axis=-1, keepdims=True)
                 - normed * jnp.mean(lifted * normed, axis=-1, keepdims=True)
             )
+        for slot, target in enumerate(ranks):
+            small_over_z(slot, rank, target).start()
         crossing().wait_send()
+        yield
+        for slot, target in enumerate(ranks):
+            small_over_z(slot, target, target).wait_recv()
+        small_p[me] = small_z[0] + small_z[1] + small_z[2] + small_z[3]
+        for slot, target in enumerate(spots_of):
+            small_over_plane(slot, me, target).start()
+        yield
+        for slot, target in enumerate(spots_of):
+            small_over_plane(slot, target, target).wait_recv()
+        acc = small_p[0]
+        for target in range(1, 8):
+            acc = acc + small_p[target]
+        small_out[...] = acc
+        for slot, target in enumerate(ranks):
+            small_over_z(slot, rank, target).wait_send()
+        for slot, target in enumerate(spots_of):
+            small_over_plane(slot, me, target).wait_send()
         for which in (0, 1):
             for target in range(4):
 
@@ -2437,41 +2473,9 @@
 
     run_all(sout_steps(), line_steps(), pair_steps())
 
-    def small_over_z(slot, sender, target):
-        return moved(
-            small_z.at[sender], small_z.at[sender], small_send.at[slot], small_recv.at[sender],
-            {"tensor": target},
-        )
-
-    for slot, target in enumerate(ranks):
-        small_over_z(slot, rank, target).start()
-    for slot, target in enumerate(ranks):
-        small_over_z(slot, target, target).wait_recv()
-    small_p[me] = small_z[0] + small_z[1] + small_z[2] + small_z[3]
-
-    def small_over_plane(slot, sender, target):
-        return moved(
-            small_p.at[sender], small_p.at[sender], small_send.at[3 + slot],
-            small_recv.at[4 + sender],
-            {"dp": target // 4, "seq": lax.rem(target, 4)},
-        )
-
-    for slot, target in enumerate(spots_of):
-        small_over_plane(slot, me, target).start()
-    for slot, target in enumerate(spots_of):
-        small_over_plane(slot, target, target).wait_recv()
-    acc = small_p[0]
-    for target in range(1, 8):
-        acc = acc + small_p[target]
-    small_out[...] = acc
-    for slot, target in enumerate(ranks):
-        small_over_z(slot, rank, target).wait_send()
-    for slot, target in enumerate(spots_of):
-        small_over_plane(slot, me, target).wait_send()
-
 
 def closing(
-    partial, pair_grads, tokens, d_hidden, vecs, os_rows, du_rows, d_start, small,
+    partial, pair_grads, tokens, d_hidden, vecs, os_rows, du_rows, d_start, mlp_sums, state_sums,
     out_part,
 ):
     low, wide = jnp.bfloat16, jnp.float32
@@ -2488,7 +2492,7 @@
         in_specs=any_specs(1)
         + vmem_specs(4)
         + any_specs(2)
-        + vmem_specs(3),
+        + vmem_specs(4),
         out_specs=vmem_specs(4),
         scratch_shapes=[
             pltpu.VMEM((256, D), low),
@@ -2522,8 +2526,8 @@
         ),
         name="closing",
     )(
-        partial, pair_grads, tokens, d_hidden, vecs, os_rows, du_rows, d_start, small,
-        out_part,
+        partial, pair_grads, tokens, d_hidden, vecs, os_rows, du_rows, d_start, mlp_sums,
+        state_sums, out_part,
     )
 
 
@@ -2656,12 +2660,9 @@
     )
     partial, ff_sum = lax.optimization_barrier((partial, ff_sum))
     ff_total = lax.all_gather(ff_sum, plane, axis=0, tiled=True).reshape(8, 2, ff_own, D)
-    small = jnp.concatenate(
-        [jnp.zeros((1, D), wide), sums[1:2], mlp_sums[0:1], sums[0:1], sums[2:3], jnp.zeros((3, D), wide)]
-    )
     inputs_grad, pair, two_grads, small = closing(
         partial, pair_grads, inputs, grad_hidden, vecs, os_rows.reshape(256, D),
-        du_rows.reshape(256, D), d_start, small, out_part,
+        du_rows.reshape(256, D), d_start, mlp_sums, sums, out_part,
     )
     pair = pair.reshape(2, PAIR_ROWS, D)
     (

time: 510 us -> 504 us (0.988)
    pallas_call x1, Pallas kernels: 83.3 us -> 77.4 us  [closing(): pl.pallas_call(closing_kernel, out_shape=[jax.ShapeDtypeStruct(*one) for...]
where the time goes in v4:
time: 504 us; the launch traced here: 503 us
  Pallas kernels  475 us (94%)
  between operations  14.1 us (3%)
  local copies, waits for them, and re-layouts  11.4 us (2%)
    pallas_call x1, Pallas kernels, forward_chain(): pl.pallas_call(forward_kernel, out_shape=[jax.ShapeDtypeStruct(*one) for...  113 us
    pallas_call x1, Pallas kernels, backward_chain(): pl.pallas_call(backward_kernel, out_shape=[jax.ShapeDtypeStruct(*one) for...  107 us
    pallas_call x1, Pallas kernels, middle(): pl.pallas_call(middle_kernel, out_shape=[jax.ShapeDtypeStruct(*one) for o...  96.1 us
    pallas_call x1, Pallas kernels, closing(): pl.pallas_call(closing_kernel, out_shape=[jax.ShapeDtypeStruct(*one) for...  77.4 us
    pallas_call x1, Pallas kernels, opening(): pl.pallas_call(opening_kernel, out_shape=[jax.ShapeDtypeStruct(*one) for...  68.9 us
    pallas_call x1, Pallas kernels, finish_grads(): pl.pallas_call(finish_kernel, grid=(8,), out_shape=[square] * 4 + [rows]...  11.4 us
  transfers between devices with their start and end apart: 4, of which 0 were waited for; matrix products, arithmetic and copies ran while one was open for 2% of the time, Pallas kernels for 73%

profile of v4, /device:TPU:0, one launch (start us, length us, event | category | flops | bytes accessed | tf_op | source)
XLA Modules:
  0.0 502.9 jit_solution(8940281382722928023)
XLA Ops:
  7.2 0.0 copy-start
  7.2 0.0 copy-start.6
  7.2 0.0 copy-start.5
  7.2 0.0 copy-start.10
  7.2 0.0 all-gather.4.cloned.1.call-start
  7.3 0.0 copy-start.7
  7.3 0.0 copy-start.8
  7.3 0.0 copy-start.9
  7.3 0.0 copy-start.11
  7.3 0.0 copy-start.12
  7.3 0.6 all-gather.4.cloned.1.call-update
  8.0 0.0 all-gather.6.cloned.1.call-start
  8.0 1.6 copy.36.rel_bias
  9.6 0.0 copy-done
  9.6 0.1 constant_dynamic-slice_fusion.5
  9.7 0.1 copy.42
  9.8 1.1 constant_dynamic-slice_fusion.3
  10.9 0.1 copy.43
  11.0 0.0 copy-done.6
  11.0 0.0 copy-done.5
  11.1 0.2 constant_dynamic-slice_fusion.1
  11.3 0.1 copy.45
  11.4 0.1 copy.44
  11.5 0.0 copy-done.10
  11.5 0.0 copy-done.7
  11.6 0.0 copy-done.8
  11.6 0.0 copy-done.9
  11.6 0.7 stack.35.vecs
  12.2 0.0 copy-done.11
  12.2 0.0 copy-done.12
  12.2 0.1 pad_add_fusion
  12.3 0.7 pad_maximum_fusion.1.back_own
  13.0 1.0 constant_dynamic-slice_fusion.4
  14.0 0.8 pad_maximum_fusion
  14.8 0.7 broadcast_in_dim.4.marks_own
  15.5 68.9 %opening.1 = (bf16[4,512,1024]{2,1,0:T(8,128)(2,1)}, bf16[4,512,384]{2,1,0:T(8,128)(2,1)}, bf16[8,320,1024]{2,1,0:T(8,128)(2,1)}, f32[512,1024]{1,0:T(8,128)}, s...) custom-call(bf16[2,128,1024]{2,1,0:T(8,128)(2,1)} %tokens.5, bf16[1024,256]{1,0:T(8,128)(2,1)} %w_query.1, ...), custom_call_target="tpu_custom_call" | custom-call | flops 30000001024 | bytes 30000000 | tf_op jit(solution)/shard_map/opening/pallas_call | solution.py:2116
  84.4 0.0 all-gather.4.cloned.1.call-done
  84.4 0.0 all-gather.6.cloned.1.call-update
  84.4 0.2 reduce-scatter.2.cloned.1.call-start
  84.7 113.3 %forward_chain.1 = (bf16[4,512,128]{2,1,0:T(8,128)(2,1)}, f32[4,512,1]{2,1,0:T(8,128)}, f32[4,128,1024]{2,1,0:T(8,128)}, bf16[4,512,1024]{2,1,0:T(8,128)(2,1)}, ...) custom-call(s32[4,8,128]{2,1,0:T(8,128)} %get-tuple-element.67.marks, ...), custom_call_target="tpu_custom_call" | custom-call | flops 60000002048 | bytes 60000000 | tf_op jit(solution)/shard_map/forward_chain/pallas_call | solution.py:891
  197.9 0.0 all-gather.6.cloned.1.call-done
  198.0 96.1 %middle.1 = (f32[2,128,1024]{2,1,0:T(8,128)}, f32[2,128,1024]{2,1,0:T(8,128)}, bf16[4,512,128]{2,1,0:T(8,128)(2,1)}, f32[8,1024]{1,0:T(8,128)}, bf16[8,384,1024]...) custom-call(bf16[4,512,128]{2,1,0:T(8,128)(2,1)} %get-tuple-element.74.mixed, bf16[2,128,1024]{2,1,0:T(8,128)(2,1)} %tokens.5, ...), custom_call_target="tpu_custom_call" | custom-call | flops 60000002048 | bytes 60000000 | tf_op jit(solution)/shard_map/middle/pallas_call | solution.py:1860
  294.0 0.0 reduce-scatter.2.cloned.1.call-update
  294.1 0.3 all-gather.8.cloned.1.call-start
  294.3 107.5 %backward_chain.1 = (bf16[4,64,1024]{2,1,0:T(8,128)(2,1)}, f32[64,1024]{1,0:T(8,128)}, f32[8,1024]{1,0:T(8,128)}, f32[2,128,1024]{2,1,0:T(8,128)}, bf16[2,128,10...) custom-call(s32[4,8,128]{2,1,0:T(8,128)} %get-tuple-element.67.marks, ...), custom_call_target="tpu_custom_call" | custom-call | flops 40000000000 | bytes 40000000 | tf_op jit(solution)/shard_map/backward_chain/pallas_call | solution.py:1288
  401.8 0.0 reduce-scatter.2.cloned.1.call-done
  401.8 0.0 all-gather.8.cloned.1.call-update
  401.9 77.4 %closing.1 = (f32[2,128,1024]{2,1,0:T(8,128)}, bf16[2,4,160,1024]{3,2,1,0:T(8,128)(2,1)}, bf16[8,64,1024]{2,1,0:T(8,128)(2,1)}, f32[8,1024]{1,0:T(8,128)}) custom-call(bf16[2,4,128,1024]{3,2,1,0:T(8,128)(2,1)} %get-tuple-element.94.partial, bf16[512,1024]{1,0:T(8,128)(2,1)} %get-tuple-element.95.pair_grads, bf16[2,128,1024]{2,1,0:T(8,128)(2,1)} %tokens.5, ...), custom_call_target="tpu_custom_call" | custom-call | flops 30000001024 | bytes 30000000 | tf_op jit(solution)/shard_map/closing/pallas_call | solution.py:2489
  479.3 0.7 slice_reduce_fusion
  480.0 0.1 reshape_squeeze.3
  480.1 0.6 fusion
  480.6 1.5 fusion.1
  482.2 0.0 all-gather.8.cloned.1.call-done
  482.2 0.0 copy-start.4
  482.2 11.4 %finish_grads.1 = (f32[1024,256]{1,0:T(8,128)}, f32[1024,256]{1,0:T(8,128)}, f32[1024,256]{1,0:T(8,128)}, f32[1024,256]{1,0:T(8,128)}, f32[256,1024]{1,0:T(8,128...) custom-call(bf16[2,640,1024]{2,1,0:T(8,128)(2,1)} %bitcast.36, ...), custom_call_target="tpu_custom_call" | custom-call | tf_op jit(solution)/shard_map/finish_grads/pallas_call | solution.py:2564
  493.6 0.0 copy-start.3
  493.6 0.0 copy-done.4
  493.6 0.0 copy-start.1
  493.7 0.8 copy.49
  494.4 0.0 copy-done.2
  494.5 1.0 copy.50
  495.4 0.0 copy-done.3
  495.4 1.0 copy.51
  496.4 0.0 copy-done.1
  (4 shorter events, 0.0 us)
Async XLA Ops:
  7.2 2.4 copy-start
  7.2 3.8 copy-start.6
  7.2 3.8 copy-start.5
  7.2 4.3 copy-start.10
  7.2 77.2 %all-gather.4.cloned.1.call-start = ((), (), s32[]{:S(2)}) async-start(), calls=%async_computation.1 | async-start | bytes 4718592 | tf_op jit(solution)/shard_map/all_gather | solution.py:2620
  7.3 4.3 copy-start.7
  7.3 4.3 copy-start.8
  7.3 4.3 copy-start.9
  7.3 4.9 copy-start.11
  7.3 4.9 copy-start.12
  8.0 190.0 %all-gather.6.cloned.1.call-start = ((), (), s32[]{:S(2)}) async-start(), calls=%async_computation.2 | async-start | bytes 2621440 | tf_op jit(solution)/shard_map/all_gather | solution.py:2644
  84.4 317.4 %reduce-scatter.2.cloned.1.call-start = ((), (), s32[]{:S(2)}) async-start(), calls=%async_computation.3 | async-start | bytes 2621440 | tf_op jit(solution)/shard_map/reduce_scatter | solution.py:2652
  294.1 188.1 %all-gather.8.cloned.1.call-start = ((), (), s32[]{:S(2)}) async-start(), calls=%async_computation.4 | async-start | bytes 4718592 | tf_op jit(solution)/shard_map/all_gather | solution.py:2662
  482.2 11.5 %copy-start.4 = (bf16[2,128,1024]{2,1,0:T(8,128)(2,1)S(1)}, bf16[2,128,1024]{2,1,0:T(8,128)(2,1)}, u32[]{:S(2)}) copy-start(bf16[2,128,1024]{2,1,0:T(8,128)(2,1)} %get-tuple-element.157) | copy-start | bytes 1572868
  482.2 12.3 %copy-start.2 = (f32[2,128,1024]{2,1,0:T(8,128)S(1)}, f32[2,128,1024]{2,1,0:T(8,128)}, u32[]{:S(2)}) copy-start(f32[2,128,1024]{2,1,0:T(8,128)} %get-tuple-element.91) | copy-start | bytes 3145732
  493.6 1.8 copy-start.3
  493.6 2.8 copy-start.1
Sparse Core Ops, SparseCore 0:
  10.0 55.5 all-gather.3
  84.6 61.5 all-gather.5
  294.2 51.8 reduce-scatter.1
  402.0 52.7 all-gather.7

commit v5 on v4

--- a/solution.py
+++ b/solution.py
@@ -924,12 +924,13 @@
 
 def backward_kernel(
     scal, qkv, d_o, lse_tok, qkvst, lse_st, state_rows, begin, cots, back, kept, vecs, bias,
-    extra, hidden, rows_hbm, low_hbm, w_qkv,
-    du_rows, d_start, sums, state_out, tokens_out, out_part, partial, pair_grads,
+    extra, hidden, rows_hbm, low_hbm, w_qkv, os_rows,
+    du_rows, d_start, sums, state_out, tokens_out, out_part, partial, pair_grads, sout_part,
     dz_sum, diag, d_qkv, d_qkvst, rows_buf, low_buf, leave, came, grad_acc,
     key_acc, value_acc, st_key, st_value, dos_rows, dos_got, d_got, grad_in,
     states, w_back, w_sout, work, core_got, near_got, far_got, total,
     send_sem, recv_sem, local_sem, side_sem, ring_send, ring_recv, buf_sem, core_sem, came_sem,
+    near_two, far_two, two_send, two_recv,
 ):
     place, half, rank = line_place()
     own_rows = pl.ds(pl.multiple_of(half * 64, 64), 64)
@@ -981,6 +982,32 @@
         work, core_got, near_got, far_got, total, 384, ring_send, ring_recv
     )
     next(plane_steps)
+    short = pl.ds(0, 128)
+    sout_steps = plane_scatter(
+        work.at[:, short, :], core_got.at[:, short, :], near_two, far_two, total.at[short, :],
+        128, two_send, two_recv,
+    )
+    next(sout_steps)
+
+    def sout_products():
+        def one(index, _):
+            part = to_low(
+                dot_tn(os_rows[:, span(index, 128)], du_rows[...].reshape(256, D))
+            )
+            for block in range(4):
+                work[4 * lax.rem(index, 2) + block, span(index // 2, 32), :] = part[
+                    32 * block : 32 * block + 32, :
+                ]
+            return 0
+
+        lax.fori_loop(0, LINE, one, 0)
+
+    def plane_results():
+        for which in range(2):
+            rows = pl.ds(128 * which, 128)
+            tokens_out[which] = to_low(hidden[which] + total[rows, :])
+        out_part[...] = to_low(total[256:384, :])
+
 
     def aside(block_id, row_set):
         return pltpu.make_async_remote_copy(
@@ -1180,6 +1207,15 @@
         for slot, (other, seq_to, rank_to) in enumerate(peers):
             mixed_copy(block_id, slot, head, other, seq_to, rank_to).start()
         dos_got[block_id, span(head, 64), :] = dos_rows[block_id, :, span(head, 128)]
+
+        @pl.when(turn > 0)
+        def _():
+            block_products(block_id + 1)
+
+        @pl.when(turn == 3)
+        def _():
+            sout_products()
+
         for slot, (other, seq_to, rank_to) in enumerate(peers):
             mixed_copy(block_id, slot, other, other, seq_to, rank_to).wait_recv()
 
@@ -1205,15 +1241,21 @@
             grads_copy(block_id, slot, head, other, seq_to, rank_to).start()
         d_got[block_id, head] = d_qkvst[block_id, span(head, 64), :]
 
-        for step in range(4):
+        for step in range(3):
 
             @pl.when(turn == step)
             def _():
-                next(plane_steps, None)
+                next(plane_steps)
+                if step == 2:
+                    next(plane_steps, None)
+                    plane_results()
 
         @pl.when(turn == 3)
         def _():
+            next(sout_steps)
+            add_came(place_in(2 + half, place))
             bucket_sums()
+            next(sout_steps)
 
         @pl.when(turn < 3)
         def _():
@@ -1221,11 +1263,10 @@
 
         d_qkv[block_id, :, 128:256] = to_low(key_acc[block_id])
         d_qkv[block_id, :, 256:384] = to_low(value_acc[block_id])
-        block_products(block_id)
-
-        @pl.when(turn == 2)
+        @pl.when(turn == 3)
         def _():
-            add_came(place_in(2 + half, place))
+            block_products(0)
+            next(sout_steps)
 
         for slot, (other, seq_to, rank_to) in enumerate(peers):
             grads_copy(block_id, slot, other, other, seq_to, rank_to).wait_recv()
@@ -1256,15 +1297,12 @@
 
     lax.fori_loop(0, 4, drain, 0)
     pair_grads[...] = to_low(grad_acc[...])
-    for _ in plane_steps:
+    for _ in sout_steps:
         pass
+    sout_part[...] = to_low(total[0:128, :])
     add_came(place_in(half, place))
     for slot in range(2):
         leaving(slot).wait_send()
-    for which in range(2):
-        rows = pl.ds(128 * which, 128)
-        tokens_out[which] = to_low(hidden[which] + total[rows, :])
-    out_part[...] = to_low(total[256:384, :])
     loads[1].wait()
     aside(beside, place // 2).wait_send()
     aside(place, 1 - place // 2).wait_recv()
@@ -1272,7 +1310,7 @@
 
 def backward_chain(
     scal, qkv, d_o, lse_tok, qkvst, lse_st, state_rows, begin, cots, back, kept, vecs, bias,
-    extra, hidden, rows_all, state_low, w_qkv,
+    extra, hidden, rows_all, state_low, w_qkv, os_rows,
 ):
     low, wide = jnp.bfloat16, jnp.float32
     shapes = (
@@ -1284,6 +1322,7 @@
         ((128, D), low),
         ((2, 4, 128, D), low),
         ((512, D), low),
+        ((128, D), low),
     )
     return pl.pallas_call(
         backward_kernel,
@@ -1296,8 +1335,8 @@
         + any_specs(1)
         + vmem_specs(1)
         + any_specs(2)
-        + vmem_specs(1),
-        out_specs=vmem_specs(3) + any_specs(1) + vmem_specs(4),
+        + vmem_specs(2),
+        out_specs=vmem_specs(3) + any_specs(1) + vmem_specs(5),
         scratch_shapes=[
             pltpu.VMEM((BLOCK, 2 * BLOCK), wide),
             pltpu.VMEM((8, WIDE), wide),
@@ -1333,15 +1372,19 @@
             pltpu.SemaphoreType.DMA((2, 2)),
             pltpu.SemaphoreType.DMA((2,)),
             pltpu.SemaphoreType.DMA((2,)),
+            pltpu.VMEM((4, 64, D), low),
+            pltpu.VMEM((2, 64, D), low),
+            pltpu.SemaphoreType.DMA((10,)),
+            pltpu.SemaphoreType.DMA((10,)),
         ],
         compiler_params=pltpu.CompilerParams(
-            collective_id=2, has_side_effects=True, vmem_limit_bytes=VMEM_LIMIT
+            collective_id=2, has_side_effects=True, vmem_limit_bytes=63 * 1024 * 1024
         ),
         cost_estimate=pl.CostEstimate(flops=40000000000, bytes_accessed=40000000, transcendentals=0),
         name="backward_chain",
     )(
         scal, qkv, d_o, lse_tok, qkvst, lse_st, state_rows, begin, cots, back, kept, vecs, bias,
-        extra, hidden, rows_all, state_low, w_qkv,
+        extra, hidden, rows_all, state_low, w_qkv, os_rows,
     )
 
 
@@ -1666,80 +1709,85 @@
     loads[0].wait()
     loads[1].wait()
     loads[2].wait()
-    owners = (me, me_c, at_x, at_y, x_c, y_c, at_d, d_c)
+    order = (
+        (me, 0), (me, 1), (me_c, 0), (me_c, 1), (at_x, 0), (at_y, 1), (x_c, 0), (y_c, 1),
+        (at_x, 1), (at_y, 0), (x_c, 1), (y_c, 0), (at_d, 0), (at_d, 1), (d_c, 0), (d_c, 1),
+    )
+
+    def before_four():
+        swap[3].start()
+        wait_of["x", 0].wait_recv()
+        on_x0.start()
+        to_core[0].start()
+        wait_of["y", 1].wait_recv()
+        on_y1.start()
+        to_core[1].start()
+
+    def before_eight():
+        wait_of["x", 1].wait_recv()
+        to_core[2].start()
+        wait_of["y", 0].wait_recv()
+        to_core[3].start()
+
+    def before_eleven():
+        swap[1].start()
+        wait_of["yc", 0].wait_recv()
+
+    def before_twelve():
+        swap[2].start()
+        wait_of["d", 0].wait_recv()
+        to_core[4].start()
+        wait_of["d", 1].wait_recv()
+        to_core[5].start()
+
+    def before_fourteen():
+        add_core(1, at_x)
+        near[2].start()
+        add_core(2, at_y)
+        near[3].start()
+        wait_of["dc", 0].wait_recv()
+
+    ahead = {
+        2: wait_of["mc", 0].wait_recv,
+        3: wait_of["mc", 1].wait_recv,
+        4: before_four,
+        6: wait_of["xc", 0].wait_recv,
+        7: wait_of["yc", 1].wait_recv,
+        8: before_eight,
+        10: wait_of["xc", 1].wait_recv,
+        11: before_eleven,
+        12: before_twelve,
+        14: before_fourteen,
+        15: wait_of["dc", 1].wait_recv,
+    }
 
     def one_chunk(turn, _):
-        @pl.when(turn == 1)
-        def _():
-            wait_of["mc", 0].wait_recv()
-            wait_of["mc", 1].wait_recv()
-
-        @pl.when(turn == 2)
-        def _():
-            swap[3].start()
-            wait_of["x", 0].wait_recv()
-            on_x0.start()
-            wait_of["y", 1].wait_recv()
-            on_y1.start()
-            to_core[0].start()
-            to_core[1].start()
-            wait_of["x", 1].wait_recv()
-            to_core[2].start()
-            wait_of["y", 0].wait_recv()
-            to_core[3].start()
-
-        @pl.when(turn == 4)
-        def _():
-            wait_of["xc", 0].wait_recv()
-            wait_of["xc", 1].wait_recv()
-
-        @pl.when(turn == 5)
-        def _():
-            swap[1].start()
-            wait_of["yc", 0].wait_recv()
-            wait_of["yc", 1].wait_recv()
-
-        @pl.when(turn == 6)
-        def _():
-            swap[2].start()
-            wait_of["d", 0].wait_recv()
-            to_core[4].start()
-            wait_of["d", 1].wait_recv()
-            to_core[5].start()
-            add_core(1, at_x)
-            near[2].start()
-            add_core(2, at_y)
-            near[3].start()
-
-        @pl.when(turn == 7)
-        def _():
-            wait_of["dc", 0].wait_recv()
-            wait_of["dc", 1].wait_recv()
-
-        owner = owners[7]
-        for index in range(7):
-            owner = jnp.where(turn == index, owners[index], owner)
+        for value, action in ahead.items():
+
+            @pl.when(turn == value)
+            def _():
+                action()
+
+        owner, which = order[15]
+        for index in range(15):
+            owner = jnp.where(turn == index, order[index][0], owner)
+            which = jnp.where(turn == index, order[index][1], which)
         up_rows = up[...].reshape(4 * ff_own, D)
         down_rows = down[...].reshape(4 * ff_own, D)
-
-        def part(which, _):
-            rows = span(which, 128)
-            pre = dot_nt(mid_all[owner, rows, :], up_rows)
-            square = pre * pre
-            bend = jnp.tanh(GELU_SCALE * (pre + 0.044715 * (pre * square)))
-            gl_all[owner, rows, :] = to_low(0.5 * pre * (1.0 + bend))
-            slope = 0.5 * (1.0 + bend) + 0.5 * pre * (1.0 - bend * bend) * (
-                GELU_SCALE * (1.0 + 3.0 * 0.044715 * square)
-            )
-            grad = to_low(dot_nt(cot_all[owner, rows, :], down_rows) * slope)
-            dpre_all[owner, rows, :] = grad
-            work[owner, rows, :] = to_low(dot_nn(grad, up_rows))
-            return 0
-
-        lax.fori_loop(0, 2, part, 0)
+        rows = span(which, 128)
+        pre = dot_nt(mid_all[owner, rows, :], up_rows)
+        square = pre * pre
+        bend = jnp.tanh(GELU_SCALE * (pre + 0.044715 * (pre * square)))
+        gl_all[owner, rows, :] = to_low(0.5 * pre * (1.0 + bend))
+        slope = 0.5 * (1.0 + bend) + 0.5 * pre * (1.0 - bend * bend) * (
+            GELU_SCALE * (1.0 + 3.0 * 0.044715 * square)
+        )
+        grad = to_low(dot_nt(cot_all[owner, rows, :], down_rows) * slope)
+        dpre_all[owner, rows, :] = grad
+        work[owner, rows, :] = to_low(dot_nn(grad, up_rows))
         return 0
 
-    lax.fori_loop(0, 8, one_chunk, 0)
+    lax.fori_loop(0, 16, one_chunk, 0)
     swap[0].start()
     add_core(0, at_d)
     near[0].start()
@@ -1766,7 +1814,7 @@
 
         return 0
 
-    lax.fori_loop(0, 8, grads, 0)
+    lax.fori_loop(0, NEAR_GRADS, grads, 0)
     near[0].wait_recv()
     add_into(at_y, views[0], near_got[0])
     far[0].start()
@@ -1786,6 +1834,7 @@
         return 0
 
     lax.fori_loop(0, 8, outward, 0)
+    lax.fori_loop(NEAR_GRADS, FAR_GRADS, grads, 0)
     for slot, view in enumerate(views):
         far[slot].wait_recv()
         total[view, :] = work[me, view, :].astype(wide) + far_got[slot].astype(wide)
@@ -1823,6 +1872,7 @@
     for slot, (_, seq_to, rank_to) in enumerate(peers):
         line_copy(slot, here, place, rank, seq_to, rank_to).start()
     d_line[place, span(rank, 128), :] = d_rows[mine, :, span(head, 128)]
+    lax.fori_loop(FAR_GRADS, 8, grads, 0)
     for index in range(LINE):
         columns = pl.ds(128 * index, 128)
         part = dot_tn(mixed_rows[0, :, columns], d_low[0]) + dot_tn(
@@ -1843,6 +1893,8 @@
 
 
 GELU_SCALE = 0.7978845608028654
+NEAR_GRADS = 3
+FAR_GRADS = 4
 
 
 def middle(mixed, tokens, kept, spread, cot_all, vecs):
@@ -1898,7 +1950,7 @@
 
 
 def opening_kernel(
-    tokens, w_query, w_key, w_value, w_sout, w_out, begin, vecs, rel_bias, marks_own,
+    tokens, w_query, w_key, w_value, w_sout, w_out, begin, vecs, marks_own,
     rows_all, qkv, kept, table, marks, w_qkv,
     begin_rows, bias_rows, stage, send_sem, core_sem, recv_sem, piece_send, piece_recv, ring_send, ring_recv,
     mark_send, mark_recv, local_sem,
@@ -2080,7 +2132,12 @@
         bucket_ids = bucket_of(jnp.where(lane >= WIDE - BLOCK, lane - WIDE - BLOCK, lane - BLOCK))
         first = jnp.zeros((8, WIDE), jnp.float32)
         for bucket_id in range(BUCKETS):
-            first = jnp.where(bucket_ids == bucket_id, rel_bias[bucket_id, half], first)
+            value = jnp.where(
+                half == 0,
+                vecs[4:5, bucket_id : bucket_id + 1],
+                vecs[4:5, BUCKETS + bucket_id : BUCKETS + bucket_id + 1],
+            )
+            first = jnp.where(bucket_ids == bucket_id, value, first)
         row = lax.broadcasted_iota(jnp.int32, (8, WIDE), 0)
         for step in (1, 2, 4):
             first = jnp.where(row // step % 2 == 1, pltpu.roll(first, step, 1), first)
@@ -2102,7 +2159,7 @@
         mark_move(slot, target, target).wait_recv()
 
 
-def opening(tokens, w_query, w_key, w_value, w_sout, w_out, begin, vecs, rel_bias, marks):
+def opening(tokens, w_query, w_key, w_value, w_sout, w_out, begin, vecs, marks):
     low, wide = jnp.bfloat16, jnp.float32
     shapes = (
         ((4, BLOCK, D), low),
@@ -2118,9 +2175,7 @@
         out_shape=[jax.ShapeDtypeStruct(*one) for one in shapes],
         in_specs=vmem_specs(1)
         + any_specs(6)
-        + vmem_specs(1)
-        + [pl.BlockSpec(memory_space=pltpu.SMEM)]
-        + vmem_specs(1),
+        + vmem_specs(2),
         out_specs=vmem_specs(6),
         scratch_shapes=[
             pltpu.VMEM((16, D), wide),
@@ -2144,7 +2199,7 @@
             flops=30000000000, bytes_accessed=30000000, transcendentals=0
         ),
         name="opening",
-    )(tokens, w_query, w_key, w_value, w_sout, w_out, begin, vecs, rel_bias, marks)
+    )(tokens, w_query, w_key, w_value, w_sout, w_out, begin, vecs, marks)
     rows_all, qkv, kept, table, marks, w_qkv = outs
     return rows_all, qkv, kept.reshape(8, 4, 80, D), table, marks, w_qkv
 
@@ -2235,23 +2290,21 @@
 
 
 def closing_kernel(
-    partial, pair_grads, tokens, d_hidden, vecs, os_hbm, du_hbm, d_start, mlp_sums, state_sums,
-    out_part,
+    partial, pair_grads, tokens, d_hidden, vecs, d_start, mlp_sums, state_sums, out_part,
+    sout_part,
     inputs_grad, pair_out, sout_out, small_out,
-    os_rows, du_rows, sums, got, final, cross, cross_got,
+    sums, got, final, cross, cross_got,
     pair_part, pair_near, pair_far,
-    work, core_got, near_got, far_got, total, z_part, z_got,
+    z_part, z_got,
     small_z, small_p,
     line_send, line_recv, way_send, way_recv, pair_send, pair_recv, core_sem,
-    ring_send, ring_recv, zs_send, zs_recv, gather_send, gather_recv, small_send, small_recv, local_sem,
+    zs_send, zs_recv, gather_send, gather_recv, small_send, small_recv, local_sem,
 ):
     loads = [
         pltpu.make_async_copy(source, target, local_sem.at[slot])
         for slot, (source, target) in enumerate(
             (
                 (partial, sums),
-                (os_hbm, os_rows),
-                (du_hbm, du_rows),
             )
         )
     ]
@@ -2350,7 +2403,6 @@
 
     def line_steps():
         loads[0].wait()
-        pl.semaphore_wait(barrier, 10)
         for which in (0, 1):
             pass_first(which)
         yield
@@ -2432,19 +2484,7 @@
         full.wait_send()
 
     def sout_steps():
-        loads[1].wait()
-        loads[2].wait()
-        for head in range(LINE):
-            low = to_low(dot_tn(os_rows[:, 128 * head : 128 * head + 128], du_rows[...]))
-            for piece in range(4):
-                work[
-                    4 * (head % 2) + piece, 32 * (head // 2) : 32 * (head // 2) + 32, :
-                ] = low[32 * piece : 32 * piece + 32, :]
-        for _ in plane_scatter(
-            work, core_got, near_got, far_got, total, 128, ring_send, ring_recv
-        ):
-            yield
-        z_part[:, 0:32, :] = to_low(total[...]).reshape(4, 32, D)
+        z_part[:, 0:32, :] = sout_part[...].reshape(4, 32, D)
         z_part[:, 32:64, :] = out_part[...].reshape(4, 32, D)
         out = [
             moved(
@@ -2471,12 +2511,12 @@
         for one in out:
             one.wait_send()
 
-    run_all(sout_steps(), line_steps(), pair_steps())
+    pl.semaphore_wait(barrier, 10)
+    run_all(sout_steps(), pair_steps(), line_steps())
 
 
 def closing(
-    partial, pair_grads, tokens, d_hidden, vecs, os_rows, du_rows, d_start, mlp_sums, state_sums,
-    out_part,
+    partial, pair_grads, tokens, d_hidden, vecs, d_start, mlp_sums, state_sums, out_part, sout_part,
 ):
     low, wide = jnp.bfloat16, jnp.float32
     shapes = (
@@ -2490,13 +2530,9 @@
         closing_kernel,
         out_shape=[jax.ShapeDtypeStruct(*one) for one in shapes],
         in_specs=any_specs(1)
-        + vmem_specs(4)
-        + any_specs(2)
-        + vmem_specs(4),
+        + vmem_specs(9),
         out_specs=vmem_specs(4),
         scratch_shapes=[
-            pltpu.VMEM((256, D), low),
-            pltpu.VMEM((256, D), low),
             pltpu.VMEM((2, 4, 128, D), low),
             pltpu.VMEM((2, 2, 4, 128, D), low),
             pltpu.VMEM((2, 128, D), wide),
@@ -2505,18 +2541,13 @@
             pltpu.VMEM((4, PAIR_ROWS // 4, D), low),
             pltpu.VMEM((4, PAIR_ROWS // 8, D), low),
             pltpu.VMEM((2, PAIR_ROWS // 8, D), low),
-            pltpu.VMEM((8, 128, D), low),
-            pltpu.VMEM((4, 128, D), low),
-            pltpu.VMEM((4, 64, D), low),
-            pltpu.VMEM((2, 64, D), low),
-            pltpu.VMEM((128, D), wide),
             pltpu.VMEM((4, 64, D), low),
             pltpu.VMEM((4, 64, D), low),
             pltpu.VMEM((4, 8, D), wide),
             pltpu.VMEM((8, 8, D), wide),
             dma((1,)), dma((1,)), dma((2, 4)), dma((2, 2, 4)), dma((12,)), dma((12,)), dma((2,)),
-            dma((10,)), dma((10,)), dma((3,)), dma((4,)), dma((16,)), dma((8, 2)), dma((10,)),
-            dma((12,)), dma((3,)),
+            dma((3,)), dma((4,)), dma((16,)), dma((8, 2)), dma((10,)),
+            dma((12,)), dma((1,)),
         ],
         compiler_params=pltpu.CompilerParams(
             collective_id=6, has_side_effects=True, vmem_limit_bytes=VMEM_LIMIT
@@ -2526,8 +2557,8 @@
         ),
         name="closing",
     )(
-        partial, pair_grads, tokens, d_hidden, vecs, os_rows, du_rows, d_start, mlp_sums,
-        state_sums, out_part,
+        partial, pair_grads, tokens, d_hidden, vecs, d_start, mlp_sums, state_sums, out_part,
+        sout_part,
     )
 
 
@@ -2613,13 +2644,20 @@
     spot = 4 * lax.axis_index("dp") + place
     gate_value = jax.nn.sigmoid(gate_bias)
     vecs = jnp.stack(
-        [state_gain, gate_value, mlp_gain, attn_gain] + [jnp.zeros_like(gate_value)] * 4
+        [
+            state_gain,
+            gate_value,
+            mlp_gain,
+            attn_gain,
+            jnp.pad(jnp.concatenate([rel_bias[:, 0], rel_bias[:, 1]]), (0, D - 2 * BUCKETS)),
+        ]
+        + [jnp.zeros_like(gate_value)] * 3
     )
     marks = jnp.concatenate([seg_starts[:, 0], lengths, jnp.zeros((4,), jnp.int32)])
     marks = jnp.broadcast_to(marks[:, None], (8, 128))
     cot_used = lax.all_gather(out_cot.reshape(256, D), plane, axis=0, tiled=True)
     rows_all, qkv, kept, bias, marks, w_qkv = opening(
-        inputs, w_query, w_key, w_value, w_sout, w_out, init_state, vecs, rel_bias, marks
+        inputs, w_query, w_key, w_value, w_sout, w_out, init_state, vecs, marks
     )
 
     ff_own = w_up.shape[1] // 8
@@ -2653,16 +2691,17 @@
         ff_grads.reshape(ff_grads.shape[2] * 8, D), "tensor", scatter_dimension=0, tiled=True
     )
     (
-        du_rows, d_start, sums, state_out, tokens_out, out_part, partial, pair_grads,
+        _, d_start, sums, state_out, tokens_out, out_part, partial, pair_grads, sout_part,
     ) = backward_chain(
         marks, qkv, d_mixed, lse_tok, qkvst, lse_st, state_rows, init_state, cots,
         back, kept, vecs, bias, extra, hidden_in, rows_all, state_low, w_qkv,
+        os_rows.reshape(256, D),
     )
     partial, ff_sum = lax.optimization_barrier((partial, ff_sum))
     ff_total = lax.all_gather(ff_sum, plane, axis=0, tiled=True).reshape(8, 2, ff_own, D)
     inputs_grad, pair, two_grads, small = closing(
-        partial, pair_grads, inputs, grad_hidden, vecs, os_rows.reshape(256, D),
-        du_rows.reshape(256, D), d_start, mlp_sums, sums, out_part,
+        partial, pair_grads, inputs, grad_hidden, vecs, d_start, mlp_sums, sums, out_part,
+        sout_part,
     )
     pair = pair.reshape(2, PAIR_ROWS, D)
     (

time: 504 us -> 486 us (0.964)
  Pallas kernels: 475 us -> 458 us
    pallas_call x1, Pallas kernels: 96.1 us -> 78.5 us  [middle(): pl.pallas_call(middle_kernel, out_shape=[jax.ShapeDtypeStruct(*one) for o...]
  transfers between devices with their start and end apart: 4 -> 4, of which waited for: 0 -> 0; matrix products, arithmetic and copies ran while one was open for 2% -> 2% of each run, Pallas kernels for 73% -> 76%
where the time goes in v5:
time: 486 us
  Pallas kernels  458 us (94%)
  between operations  14.1 us (3%)
  local copies, waits for them, and re-layouts  10.8 us (2%)
    pallas_call x1, Pallas kernels, forward_chain(): pl.pallas_call(forward_kernel, out_shape=[jax.ShapeDtypeStruct(*one) for...  113 us
    pallas_call x1, Pallas kernels, backward_chain(): pl.pallas_call(backward_kernel, out_shape=[jax.ShapeDtypeStruct(*one) for...  113 us
    pallas_call x1, Pallas kernels, middle(): pl.pallas_call(middle_kernel, out_shape=[jax.ShapeDtypeStruct(*one) for o...  78.5 us
    pallas_call x1, Pallas kernels, closing(): pl.pallas_call(closing_kernel, out_shape=[jax.ShapeDtypeStruct(*one) for...  73.4 us
    pallas_call x1, Pallas kernels, opening(): pl.pallas_call(opening_kernel, out_shape=[jax.ShapeDtypeStruct(*one) for...  68.8 us
    pallas_call x1, Pallas kernels, finish_grads(): pl.pallas_call(finish_kernel, grid=(8,), out_shape=[square] * 4 + [rows]...  11.4 us
  transfers between devices with their start and end apart: 4, of which 0 were waited for; matrix products, arithmetic and copies ran while one was open for 2% of the time, Pallas kernels for 76%

profile of v5, /device:TPU:0, one launch (start us, length us, event | category | flops | bytes accessed | tf_op | source)
XLA Modules:
  0.0 485.7 jit_solution(17627612734105600083)
XLA Ops:
  7.2 0.0 copy-start.4
  7.2 0.0 copy-start.3
  7.2 0.0 copy-start.9
  7.2 0.0 copy-start.8
  7.2 0.0 all-gather.4.cloned.1.call-start
  7.3 0.0 copy-start.5
  7.3 0.0 copy-start.6
  7.3 0.0 copy-start.7
  7.3 0.0 copy-start.10
  7.3 0.0 copy-start.11
  7.3 0.6 all-gather.4.cloned.1.call-update
  8.0 0.0 all-gather.6.cloned.1.call-start
  8.0 1.0 constant_dynamic-slice_fusion.5
  9.0 0.1 copy.41
  9.2 1.1 constant_dynamic-slice_fusion.3
  10.3 0.1 copy.42
  10.4 0.0 copy-done.4
  10.4 0.0 copy-done.3
  10.4 0.2 constant_dynamic-slice_fusion.1
  10.6 0.1 copy.44
  10.7 0.1 copy.43
  10.8 0.0 copy-done.9
  10.9 0.1 select_maximum_fusion
  10.9 0.0 copy-done.8
  11.0 0.0 copy-done.5
  11.0 0.0 copy-done.6
  11.0 0.0 copy-done.7
  11.0 0.7 stack.39.vecs
  11.7 0.0 copy-done.10
  11.7 0.0 copy-done.11
  11.7 0.1 pad_add_fusion
  11.8 0.7 pad_maximum_fusion.1.back_own
  12.5 1.0 constant_dynamic-slice_fusion.4
  13.4 0.8 pad_maximum_fusion
  14.3 0.7 broadcast_in_dim.4.marks_own
  14.9 68.8 %opening.1 = (bf16[4,512,1024]{2,1,0:T(8,128)(2,1)}, bf16[4,512,384]{2,1,0:T(8,128)(2,1)}, bf16[8,320,1024]{2,1,0:T(8,128)(2,1)}, f32[512,1024]{1,0:T(8,128)}, s...) custom-call(bf16[2,128,1024]{2,1,0:T(8,128)(2,1)} %tokens.5, bf16[1024,256]{1,0:T(8,128)(2,1)} %w_query.1, ...), custom_call_target="tpu_custom_call" | custom-call | flops 30000001024 | bytes 30000000 | tf_op jit(solution)/shard_map/opening/pallas_call | solution.py:2173
  83.7 0.0 all-gather.4.cloned.1.call-done
  83.8 0.0 all-gather.6.cloned.1.call-update
  83.8 0.2 reduce-scatter.2.cloned.1.call-start
  84.0 113.3 %forward_chain.1 = (bf16[4,512,128]{2,1,0:T(8,128)(2,1)}, f32[4,512,1]{2,1,0:T(8,128)}, f32[4,128,1024]{2,1,0:T(8,128)}, bf16[4,512,1024]{2,1,0:T(8,128)(2,1)}, ...) custom-call(s32[4,8,128]{2,1,0:T(8,128)} %get-tuple-element.67.marks, ...), custom_call_target="tpu_custom_call" | custom-call | flops 60000002048 | bytes 60000000 | tf_op jit(solution)/shard_map/forward_chain/pallas_call | solution.py:891
  197.3 0.0 all-gather.6.cloned.1.call-done
  197.3 78.5 %middle.1 = (f32[2,128,1024]{2,1,0:T(8,128)}, f32[2,128,1024]{2,1,0:T(8,128)}, bf16[4,512,128]{2,1,0:T(8,128)(2,1)}, f32[8,1024]{1,0:T(8,128)}, bf16[8,384,1024]...) custom-call(bf16[4,512,128]{2,1,0:T(8,128)(2,1)} %get-tuple-element.74.mixed, bf16[2,128,1024]{2,1,0:T(8,128)(2,1)} %tokens.5, ...), custom_call_target="tpu_custom_call" | custom-call | flops 60000002048 | bytes 60000000 | tf_op jit(solution)/shard_map/middle/pallas_call | solution.py:1912
  275.9 0.0 reduce-scatter.2.cloned.1.call-update
  275.9 0.3 all-gather.8.cloned.1.call-start
  276.2 112.5 %backward_chain.1 = (bf16[4,64,1024]{2,1,0:T(8,128)(2,1)}, f32[64,1024]{1,0:T(8,128)}, f32[8,1024]{1,0:T(8,128)}, f32[2,128,1024]{2,1,0:T(8,128)}, bf16[2,128,10...) custom-call(s32[4,8,128]{2,1,0:T(8,128)} %get-tuple-element.67.marks, ...), custom_call_target="tpu_custom_call" | custom-call | flops 40000000000 | bytes 40000000 | tf_op jit(solution)/shard_map/backward_chain/pallas_call | solution.py:1327
  388.7 0.0 reduce-scatter.2.cloned.1.call-done
  388.7 0.0 all-gather.8.cloned.1.call-update
  388.7 73.4 %closing.1 = (f32[2,128,1024]{2,1,0:T(8,128)}, bf16[2,4,160,1024]{3,2,1,0:T(8,128)(2,1)}, bf16[8,64,1024]{2,1,0:T(8,128)(2,1)}, f32[8,1024]{1,0:T(8,128)}) custom-call(bf16[2,4,128,1024]{3,2,1,0:T(8,128)(2,1)} %get-tuple-element.95.partial, bf16[512,1024]{1,0:T(8,128)(2,1)} %get-tuple-element.96.pair_grads, bf16[2,128,1024]{2,1,0:T(8,128)(2,1)} %tokens.5, ...), custom_call_target="tpu_custom_call" | custom-call | flops 30000001024 | bytes 30000000 | tf_op jit(solution)/shard_map/closing/pallas_call | solution.py:2529
  462.1 0.7 slice_reduce_fusion
  462.8 0.1 reshape_squeeze.3
  462.9 0.6 fusion
  463.5 1.5 fusion.1
  465.0 0.0 all-gather.8.cloned.1.call-done
  465.0 0.0 copy-start.2
  465.0 0.0 copy-start
  465.0 11.4 %finish_grads.1 = (f32[1024,256]{1,0:T(8,128)}, f32[1024,256]{1,0:T(8,128)}, f32[1024,256]{1,0:T(8,128)}, f32[1024,256]{1,0:T(8,128)}, f32[256,1024]{1,0:T(8,128...) custom-call(bf16[2,640,1024]{2,1,0:T(8,128)(2,1)} %bitcast.40, ...), custom_call_target="tpu_custom_call" | custom-call | tf_op jit(solution)/shard_map/finish_grads/pallas_call | solution.py:2595
  476.4 0.0 copy-start.1
  476.4 0.0 copy-done.2
  476.5 0.8 copy.48
  477.3 0.0 copy-done
  477.3 1.0 copy.49
  478.2 0.0 copy-done.1
  478.2 1.0 copy.50
  (5 shorter events, 0.0 us)
Async XLA Ops:
  7.2 3.2 copy-start.4
  7.2 3.2 copy-start.3
  7.2 3.6 copy-start.9
  7.2 3.7 copy-start.8
  7.2 76.5 %all-gather.4.cloned.1.call-start = ((), (), s32[]{:S(2)}) async-start(), calls=%async_computation.1 | async-start | bytes 4718592 | tf_op jit(solution)/shard_map/all_gather | solution.py:2658
  7.3 3.7 copy-start.5
  7.3 3.7 copy-start.6
  7.3 3.7 copy-start.7
  7.3 4.4 copy-start.10
  7.3 4.4 copy-start.11
  8.0 189.3 %all-gather.6.cloned.1.call-start = ((), (), s32[]{:S(2)}) async-start(), calls=%async_computation.2 | async-start | bytes 2621440 | tf_op jit(solution)/shard_map/all_gather | solution.py:2682
  83.8 304.9 %reduce-scatter.2.cloned.1.call-start = ((), (), s32[]{:S(2)}) async-start(), calls=%async_computation.3 | async-start | bytes 2621440 | tf_op jit(solution)/shard_map/reduce_scatter | solution.py:2690
  275.9 189.1 %all-gather.8.cloned.1.call-start = ((), (), s32[]{:S(2)}) async-start(), calls=%async_computation.4 | async-start | bytes 4718592 | tf_op jit(solution)/shard_map/all_gather | solution.py:2701
  465.0 11.5 %copy-start.2 = (bf16[2,128,1024]{2,1,0:T(8,128)(2,1)S(1)}, bf16[2,128,1024]{2,1,0:T(8,128)(2,1)}, u32[]{:S(2)}) copy-start(bf16[2,128,1024]{2,1,0:T(8,128)(2,1)} %get-tuple-element.159) | copy-start | bytes 1572868
  465.0 12.3 %copy-start = (f32[2,128,1024]{2,1,0:T(8,128)S(1)}, f32[2,128,1024]{2,1,0:T(8,128)}, u32[]{:S(2)}) copy-start(f32[2,128,1024]{2,1,0:T(8,128)} %get-tuple-element.92) | copy-start | bytes 3145732
  476.4 1.8 copy-start.1
Sparse Core Ops, SparseCore 0:
  10.0 54.8 all-gather.3
  83.9 61.5 all-gather.5
  276.0 53.6 reduce-scatter.1
  388.9 52.9 all-gather.7

commit v6 on v5

--- a/solution.py
+++ b/solution.py
@@ -2563,8 +2563,8 @@
 
 
 def finish_kernel(
-    pair, pair_tail, two, ff,
-    query, key, value, squery, out, sout, up, down, state,
+    pair, pair_tail, two, ff, small,
+    query, key, value, squery, out, sout, up, down, state, gain_0, gain_1, gain_2, gain_3, biases,
 ):
     step = pl.program_id(0)
     wide = jnp.float32
@@ -2581,9 +2581,19 @@
     @pl.when(step == 0)
     def _():
         state[...] = pair_tail[...].reshape(128, D).astype(wide)
-
-
-def finish_grads(pair, two, ff):
+        for row, target in enumerate((gain_0, gain_1, gain_2, gain_3)):
+            target[...] = small[row, :]
+        turned = jnp.broadcast_to(small[4:5, 0 : LINE * BUCKETS], (8, LINE * BUCKETS)).T
+        rank = lax.axis_index("tensor")
+        column = lax.broadcasted_iota(jnp.int32, (BUCKETS, 2), 1)
+        found = jnp.zeros((BUCKETS, 2), wide)
+        for head in range(LINE):
+            part = turned[BUCKETS * head : BUCKETS * head + BUCKETS, 0:2]
+            found = jnp.where(column + 2 * rank == head, part, found)
+        biases[...] = found
+
+
+def finish_grads(pair, two, ff, small):
     wide = jnp.float32
     turned = [
         pl.BlockSpec((D, 128), lambda i, w=which: (0, jnp.clip(i - 2 * w, 0, 1)))
@@ -2595,20 +2605,26 @@
     return pl.pallas_call(
         finish_kernel,
         grid=(8,),
-        out_shape=[square] * 4 + [rows] * 2 + [whole] * 2 + [jax.ShapeDtypeStruct((128, D), wide)],
+        out_shape=[square] * 4 + [rows] * 2 + [whole] * 2
+        + [jax.ShapeDtypeStruct((128, D), wide)]
+        + [jax.ShapeDtypeStruct((D,), wide)] * 4
+        + [jax.ShapeDtypeStruct((BUCKETS, 2), wide)],
         in_specs=[
             pl.BlockSpec((1, 128, D), lambda i: (i % 2, i // 2, 0)),
             pl.BlockSpec((2, 64, D), lambda i: (0, 8, 0)),
             pl.BlockSpec((1, 64, D), lambda i: (i, 0, 0)),
             pl.BlockSpec((1, 2, 128, D), lambda i: (i, 0, 0, 0)),
+            pl.BlockSpec((8, D), lambda i: (0, 0)),
         ],
         out_specs=turned
         + [pl.BlockSpec((32, D), lambda i: (i, 0))] * 2
         + [pl.BlockSpec((D, 128), lambda i: (0, i)), pl.BlockSpec((128, D), lambda i: (i, 0))]
-        + [pl.BlockSpec((128, D), lambda i: (0, 0))],
+        + [pl.BlockSpec((128, D), lambda i: (0, 0))]
+        + [pl.BlockSpec((D,), lambda i: (0,))] * 4
+        + [pl.BlockSpec((BUCKETS, 2), lambda i: (0, 0))],
         compiler_params=pltpu.CompilerParams(vmem_limit_bytes=VMEM_LIMIT),
         name="finish_grads",
-    )(pair, pair, two, ff)
+    )(pair, pair, two, ff, small)
 
 
 def swap_seq(value):
@@ -2706,19 +2722,16 @@
     pair = pair.reshape(2, PAIR_ROWS, D)
     (
         query_grad, key_grad, value_grad, squery_grad, out_grad, sout_grad, up_grad, down_grad,
-        state_grad,
-    ) = finish_grads(pair, two_grads, ff_total)
-    bias_grad = lax.dynamic_slice_in_dim(
-        small[4, : LINE * BUCKETS].reshape(4, 2, BUCKETS), lax.axis_index("tensor"), 1, 0
-    )[0].T
+        state_grad, attn_gain_grad, state_gain_grad, mlp_gain_grad, gate_grad, bias_grad,
+    ) = finish_grads(pair, two_grads, ff_total, small)
     return (
         tokens_out,
         state_out[:, None],
         inputs_grad,
         state_grad,
-        small[0],
-        small[1],
-        small[2],
+        attn_gain_grad,
+        state_gain_grad,
+        mlp_gain_grad,
         query_grad,
         key_grad,
         value_grad,
@@ -2728,7 +2741,7 @@
         up_grad,
         down_grad,
         bias_grad,
-        small[3],
+        gate_grad,
     )
 
 

time: 486 us -> 486 us (level)
  transfers between devices with their start and end apart: 4 -> 4, of which waited for: 0 -> 0; matrix products, arithmetic and copies ran while one was open for 2% -> 1% of each run, Pallas kernels for 76% -> 76%
where the time goes in v6:
time: 486 us; the launch traced here: 485 us
  Pallas kernels  459 us (94%)
  between operations  14.1 us (3%)
  local copies, waits for them, and re-layouts  9.32 us (2%)
    pallas_call x1, Pallas kernels, forward_chain(): pl.pallas_call(forward_kernel, out_shape=[jax.ShapeDtypeStruct(*one) for...  113 us
    pallas_call x1, Pallas kernels, backward_chain(): pl.pallas_call(backward_kernel, out_shape=[jax.ShapeDtypeStruct(*one) for...  112 us
    pallas_call x1, Pallas kernels, middle(): pl.pallas_call(middle_kernel, out_shape=[jax.ShapeDtypeStruct(*one) for o...  78.6 us
    pallas_call x1, Pallas kernels, closing(): pl.pallas_call(closing_kernel, out_shape=[jax.ShapeDtypeStruct(*one) for...  73.8 us
    pallas_call x1, Pallas kernels, opening(): pl.pallas_call(opening_kernel, out_shape=[jax.ShapeDtypeStruct(*one) for...  68.8 us
    pallas_call x1, Pallas kernels, finish_grads(): pl.pallas_call(finish_kernel, grid=(8,), out_shape=[square] * 4 + [rows]...  11.7 us
  transfers between devices with their start and end apart: 4, of which 0 were waited for; matrix products, arithmetic and copies ran while one was open for 1% of the time, Pallas kernels for 76%

profile of v6, /device:TPU:0, one launch (start us, length us, event | category | flops | bytes accessed | tf_op | source)
XLA Modules:
  0.0 485.1 jit_solution(9310500465743021896)
XLA Ops:
  7.2 0.0 copy-start.4
  7.2 0.0 copy-start.3
  7.2 0.0 copy-start.9
  7.2 0.0 copy-start.8
  7.2 0.0 all-gather.4.cloned.1.call-start
  7.3 0.0 copy-start.5
  7.3 0.0 copy-start.6
  7.3 0.0 copy-start.7
  7.3 0.0 copy-start.10
  7.3 0.0 copy-start.11
  7.3 0.6 all-gather.4.cloned.1.call-update
  8.0 0.0 all-gather.6.cloned.1.call-start
  8.0 1.0 constant_dynamic-slice_fusion.4
  9.0 0.1 copy.42
  9.2 1.1 constant_dynamic-slice_fusion.2
  10.2 0.1 copy.43
  10.4 0.0 copy-done.4
  10.4 0.0 copy-done.3
  10.4 0.2 constant_dynamic-slice_fusion
  10.6 0.1 copy.45
  10.7 0.1 copy.44
  10.8 0.0 copy-done.9
  10.9 0.1 select_maximum_fusion
  10.9 0.0 copy-done.8
  11.0 0.0 copy-done.5
  11.0 0.0 copy-done.6
  11.0 0.0 copy-done.7
  11.0 0.7 stack.39.vecs
  11.7 0.0 copy-done.10
  11.7 0.0 copy-done.11
  11.7 0.1 pad_add_fusion
  11.8 0.7 pad_maximum_fusion.1.back_own
  12.5 1.0 constant_dynamic-slice_fusion.3
  13.4 0.8 pad_maximum_fusion
  14.3 0.7 broadcast_in_dim.4.marks_own
  14.9 68.8 %opening.1 = (bf16[4,512,1024]{2,1,0:T(8,128)(2,1)}, bf16[4,512,384]{2,1,0:T(8,128)(2,1)}, bf16[8,320,1024]{2,1,0:T(8,128)(2,1)}, f32[512,1024]{1,0:T(8,128)}, s...) custom-call(bf16[2,128,1024]{2,1,0:T(8,128)(2,1)} %tokens.5, bf16[1024,256]{1,0:T(8,128)(2,1)} %w_query.1, ...), custom_call_target="tpu_custom_call" | custom-call | flops 30000001024 | bytes 30000000 | tf_op jit(solution)/shard_map/opening/pallas_call | solution.py:2173
  83.7 0.0 all-gather.4.cloned.1.call-done
  83.8 0.0 all-gather.6.cloned.1.call-update
  83.8 0.2 reduce-scatter.2.cloned.1.call-start
  84.0 113.3 %forward_chain.1 = (bf16[4,512,128]{2,1,0:T(8,128)(2,1)}, f32[4,512,1]{2,1,0:T(8,128)}, f32[4,128,1024]{2,1,0:T(8,128)}, bf16[4,512,1024]{2,1,0:T(8,128)(2,1)}, ...) custom-call(s32[4,8,128]{2,1,0:T(8,128)} %get-tuple-element.72.marks, ...), custom_call_target="tpu_custom_call" | custom-call | flops 60000002048 | bytes 60000000 | tf_op jit(solution)/shard_map/forward_chain/pallas_call | solution.py:891
  197.3 0.0 all-gather.6.cloned.1.call-done
  197.4 78.6 %middle.1 = (f32[2,128,1024]{2,1,0:T(8,128)}, f32[2,128,1024]{2,1,0:T(8,128)}, bf16[4,512,128]{2,1,0:T(8,128)(2,1)}, f32[8,1024]{1,0:T(8,128)}, bf16[8,384,1024]...) custom-call(bf16[4,512,128]{2,1,0:T(8,128)(2,1)} %get-tuple-element.79.mixed, bf16[2,128,1024]{2,1,0:T(8,128)(2,1)} %tokens.5, ...), custom_call_target="tpu_custom_call" | custom-call | flops 60000002048 | bytes 60000000 | tf_op jit(solution)/shard_map/middle/pallas_call | solution.py:1912
  276.0 0.0 reduce-scatter.2.cloned.1.call-update
  276.0 0.3 all-gather.8.cloned.1.call-start
  276.3 112.5 %backward_chain.1 = (bf16[4,64,1024]{2,1,0:T(8,128)(2,1)}, f32[64,1024]{1,0:T(8,128)}, f32[8,1024]{1,0:T(8,128)}, f32[2,128,1024]{2,1,0:T(8,128)}, bf16[2,128,10...) custom-call(s32[4,8,128]{2,1,0:T(8,128)} %get-tuple-element.72.marks, ...), custom_call_target="tpu_custom_call" | custom-call | flops 40000000000 | bytes 40000000 | tf_op jit(solution)/shard_map/backward_chain/pallas_call | solution.py:1327
  388.8 0.0 reduce-scatter.2.cloned.1.call-done
  388.8 0.0 all-gather.8.cloned.1.call-update
  388.8 73.8 %closing.1 = (f32[2,128,1024]{2,1,0:T(8,128)}, bf16[2,4,160,1024]{3,2,1,0:T(8,128)(2,1)}, bf16[8,64,1024]{2,1,0:T(8,128)(2,1)}, f32[8,1024]{1,0:T(8,128)}) custom-call(bf16[2,4,128,1024]{3,2,1,0:T(8,128)(2,1)} %get-tuple-element.100.partial, bf16[512,1024]{1,0:T(8,128)(2,1)} %get-tuple-element.101.pair_grads, bf16[2,128,1024]{2,1,0:T(8,128)(2,1)} %tokens.5, ...), custom_call_target="tpu_custom_call" | custom-call | flops 30000001024 | bytes 30000000 | tf_op jit(solution)/shard_map/closing/pallas_call | solution.py:2529
  462.7 0.0 all-gather.8.cloned.1.call-done
  462.7 0.0 copy-start.2
  462.7 0.0 copy-start
  462.7 11.7 %finish_grads.1 = (f32[1024,256]{1,0:T(8,128)}, f32[1024,256]{1,0:T(8,128)}, f32[1024,256]{1,0:T(8,128)}, f32[1024,256]{1,0:T(8,128)}, f32[256,1024]{1,0:T(8,128...) custom-call(bf16[2,640,1024]{2,1,0:T(8,128)(2,1)} %bitcast.32, ...), custom_call_target="tpu_custom_call" | custom-call | tf_op jit(solution)/shard_map/finish_grads/pallas_call | solution.py:2605
  474.4 0.0 copy-start.1
  474.4 1.4 copy.41
  475.9 0.0 copy-done.2
  475.9 0.8 copy.49
  476.7 0.0 copy-done
  476.7 1.0 copy.50
  477.6 0.0 copy-done.1
  477.6 1.0 copy.51
  (5 shorter events, 0.0 us)
Async XLA Ops:
  7.2 3.2 copy-start.4
  7.2 3.2 copy-start.3
  7.2 3.6 copy-start.9
  7.2 3.7 copy-start.8
  7.2 76.5 %all-gather.4.cloned.1.call-start = ((), (), s32[]{:S(2)}) async-start(), calls=%async_computation.1 | async-start | bytes 4718592 | tf_op jit(solution)/shard_map/all_gather | solution.py:2674
  7.3 3.7 copy-start.5
  7.3 3.7 copy-start.6
  7.3 3.7 copy-start.7
  7.3 4.4 copy-start.10
  7.3 4.4 copy-start.11
  8.0 189.4 %all-gather.6.cloned.1.call-start = ((), (), s32[]{:S(2)}) async-start(), calls=%async_computation.2 | async-start | bytes 2621440 | tf_op jit(solution)/shard_map/all_gather | solution.py:2698
  83.8 305.0 %reduce-scatter.2.cloned.1.call-start = ((), (), s32[]{:S(2)}) async-start(), calls=%async_computation.3 | async-start | bytes 2621440 | tf_op jit(solution)/shard_map/reduce_scatter | solution.py:2706
  276.0 186.7 %all-gather.8.cloned.1.call-start = ((), (), s32[]{:S(2)}) async-start(), calls=%async_computation.4 | async-start | bytes 4718592 | tf_op jit(solution)/shard_map/all_gather | solution.py:2717
  462.7 13.2 %copy-start.2 = (bf16[2,128,1024]{2,1,0:T(8,128)(2,1)S(1)}, bf16[2,128,1024]{2,1,0:T(8,128)(2,1)}, u32[]{:S(2)}) copy-start(bf16[2,128,1024]{2,1,0:T(8,128)(2,1)} %get-tuple-element.165) | copy-start | bytes 1572868
  462.7 14.0 %copy-start = (f32[2,128,1024]{2,1,0:T(8,128)S(1)}, f32[2,128,1024]{2,1,0:T(8,128)}, u32[]{:S(2)}) copy-start(f32[2,128,1024]{2,1,0:T(8,128)} %get-tuple-element.97) | copy-start | bytes 3145732
  474.4 3.2 copy-start.1
Sparse Core Ops, SparseCore 0:
  10.0 54.8 all-gather.3
  83.9 61.6 all-gather.5
  276.1 53.6 reduce-scatter.1
  389.0 52.8 all-gather.7

commit v7 on v6

--- a/solution.py
+++ b/solution.py
@@ -2583,13 +2583,12 @@
         state[...] = pair_tail[...].reshape(128, D).astype(wide)
         for row, target in enumerate((gain_0, gain_1, gain_2, gain_3)):
             target[...] = small[row, :]
-        turned = jnp.broadcast_to(small[4:5, 0 : LINE * BUCKETS], (8, LINE * BUCKETS)).T
         rank = lax.axis_index("tensor")
-        column = lax.broadcasted_iota(jnp.int32, (BUCKETS, 2), 1)
-        found = jnp.zeros((BUCKETS, 2), wide)
+        row = lax.broadcasted_iota(jnp.int32, (2, BUCKETS), 0)
+        found = jnp.zeros((2, BUCKETS), wide)
         for head in range(LINE):
-            part = turned[BUCKETS * head : BUCKETS * head + BUCKETS, 0:2]
-            found = jnp.where(column + 2 * rank == head, part, found)
+            part = small[4:5, BUCKETS * head : BUCKETS * head + BUCKETS]
+            found = jnp.where(row + 2 * rank == head, part, found)
         biases[...] = found
 
 
@@ -2608,7 +2607,7 @@
         out_shape=[square] * 4 + [rows] * 2 + [whole] * 2
         + [jax.ShapeDtypeStruct((128, D), wide)]
         + [jax.ShapeDtypeStruct((D,), wide)] * 4
-        + [jax.ShapeDtypeStruct((BUCKETS, 2), wide)],
+        + [jax.ShapeDtypeStruct((2, BUCKETS), wide)],
         in_specs=[
             pl.BlockSpec((1, 128, D), lambda i: (i % 2, i // 2, 0)),
             pl.BlockSpec((2, 64, D), lambda i: (0, 8, 0)),
@@ -2621,7 +2620,7 @@
         + [pl.BlockSpec((D, 128), lambda i: (0, i)), pl.BlockSpec((128, D), lambda i: (i, 0))]
         + [pl.BlockSpec((128, D), lambda i: (0, 0))]
         + [pl.BlockSpec((D,), lambda i: (0,))] * 4
-        + [pl.BlockSpec((BUCKETS, 2), lambda i: (0, 0))],
+        + [pl.BlockSpec((2, BUCKETS), lambda i: (0, 0))],
         compiler_params=pltpu.CompilerParams(vmem_limit_bytes=VMEM_LIMIT),
         name="finish_grads",
     )(pair, pair, two, ff, small)
@@ -2740,7 +2739,7 @@
         sout_grad,
         up_grad,
         down_grad,
-        bias_grad,
+        bias_grad.T,
         gate_grad,
     )
 

time: 486 us -> 485 us (level)
  no operation moved by 1% of the time
where the time goes in v7:
time: 485 us; the launch traced here: 484 us
  Pallas kernels  459 us (95%)
  between operations  14.1 us (3%)
  local copies, waits for them, and re-layouts  7.88 us (2%)
    pallas_call x1, Pallas kernels, forward_chain(): pl.pallas_call(forward_kernel, out_shape=[jax.ShapeDtypeStruct(*one) for...  113 us
    pallas_call x1, Pallas kernels, backward_chain(): pl.pallas_call(backward_kernel, out_shape=[jax.ShapeDtypeStruct(*one) for...  112 us
    pallas_call x1, Pallas kernels, middle(): pl.pallas_call(middle_kernel, out_shape=[jax.ShapeDtypeStruct(*one) for o...  78.6 us
    pallas_call x1, Pallas kernels, closing(): pl.pallas_call(closing_kernel, out_shape=[jax.ShapeDtypeStruct(*one) for...  73.8 us
    pallas_call x1, Pallas kernels, opening(): pl.pallas_call(opening_kernel, out_shape=[jax.ShapeDtypeStruct(*one) for...  68.8 us
    pallas_call x1, Pallas kernels, finish_grads(): pl.pallas_call(finish_kernel, grid=(8,), out_shape=[square] * 4 + [rows]...  12 us
  transfers between devices with their start and end apart: 4, of which 0 were waited for; matrix products, arithmetic and copies ran while one was open for 1% of the time, Pallas kernels for 76%

profile of v7, /device:TPU:0, one launch (start us, length us, event | category | flops | bytes accessed | tf_op | source)
XLA Modules:
  0.0 484.1 jit_solution(3368915074652927288)
XLA Ops:
  7.2 0.0 copy-start.4
  7.2 0.0 copy-start.3
  7.2 0.0 copy-start.9
  7.2 0.0 copy-start.8
  7.2 0.0 all-gather.4.cloned.1.call-start
  7.3 0.0 copy-start.5
  7.3 0.0 copy-start.6
  7.3 0.0 copy-start.7
  7.3 0.0 copy-start.10
  7.3 0.0 copy-start.11
  7.3 0.6 all-gather.4.cloned.1.call-update
  8.0 0.0 all-gather.6.cloned.1.call-start
  8.0 1.0 constant_dynamic-slice_fusion.4
  9.0 0.1 copy.41
  9.2 1.1 constant_dynamic-slice_fusion.2
  10.2 0.1 copy.42
  10.4 0.0 copy-done.4
  10.4 0.0 copy-done.3
  10.4 0.2 constant_dynamic-slice_fusion
  10.6 0.1 copy.44
  10.7 0.1 copy.43
  10.8 0.0 copy-done.9
  10.9 0.1 select_maximum_fusion
  10.9 0.0 copy-done.8
  11.0 0.0 copy-done.5
  11.0 0.0 copy-done.6
  11.0 0.0 copy-done.7
  11.0 0.7 stack.39.vecs
  11.7 0.0 copy-done.10
  11.7 0.0 copy-done.11
  11.7 0.1 pad_add_fusion
  11.8 0.7 pad_maximum_fusion.1.back_own
  12.5 1.0 constant_dynamic-slice_fusion.3
  13.4 0.8 pad_maximum_fusion
  14.3 0.7 broadcast_in_dim.4.marks_own
  14.9 68.8 %opening.1 = (bf16[4,512,1024]{2,1,0:T(8,128)(2,1)}, bf16[4,512,384]{2,1,0:T(8,128)(2,1)}, bf16[8,320,1024]{2,1,0:T(8,128)(2,1)}, f32[512,1024]{1,0:T(8,128)}, s...) custom-call(bf16[2,128,1024]{2,1,0:T(8,128)(2,1)} %tokens.5, bf16[1024,256]{1,0:T(8,128)(2,1)} %w_query.1, ...), custom_call_target="tpu_custom_call" | custom-call | flops 30000001024 | bytes 30000000 | tf_op jit(solution)/shard_map/opening/pallas_call | solution.py:2173
  83.7 0.0 all-gather.4.cloned.1.call-done
  83.8 0.0 all-gather.6.cloned.1.call-update
  83.8 0.2 reduce-scatter.2.cloned.1.call-start
  84.0 113.3 %forward_chain.1 = (bf16[4,512,128]{2,1,0:T(8,128)(2,1)}, f32[4,512,1]{2,1,0:T(8,128)}, f32[4,128,1024]{2,1,0:T(8,128)}, bf16[4,512,1024]{2,1,0:T(8,128)(2,1)}, ...) custom-call(s32[4,8,128]{2,1,0:T(8,128)} %get-tuple-element.72.marks, ...), custom_call_target="tpu_custom_call" | custom-call | flops 60000002048 | bytes 60000000 | tf_op jit(solution)/shard_map/forward_chain/pallas_call | solution.py:891
  197.3 0.0 all-gather.6.cloned.1.call-done
  197.4 78.6 %middle.1 = (f32[2,128,1024]{2,1,0:T(8,128)}, f32[2,128,1024]{2,1,0:T(8,128)}, bf16[4,512,128]{2,1,0:T(8,128)(2,1)}, f32[8,1024]{1,0:T(8,128)}, bf16[8,384,1024]...) custom-call(bf16[4,512,128]{2,1,0:T(8,128)(2,1)} %get-tuple-element.79.mixed, bf16[2,128,1024]{2,1,0:T(8,128)(2,1)} %tokens.5, ...), custom_call_target="tpu_custom_call" | custom-call | flops 60000002048 | bytes 60000000 | tf_op jit(solution)/shard_map/middle/pallas_call | solution.py:1912
  276.0 0.0 reduce-scatter.2.cloned.1.call-update
  276.0 0.3 all-gather.8.cloned.1.call-start
  276.3 112.5 %backward_chain.1 = (bf16[4,64,1024]{2,1,0:T(8,128)(2,1)}, f32[64,1024]{1,0:T(8,128)}, f32[8,1024]{1,0:T(8,128)}, f32[2,128,1024]{2,1,0:T(8,128)}, bf16[2,128,10...) custom-call(s32[4,8,128]{2,1,0:T(8,128)} %get-tuple-element.72.marks, ...), custom_call_target="tpu_custom_call" | custom-call | flops 40000000000 | bytes 40000000 | tf_op jit(solution)/shard_map/backward_chain/pallas_call | solution.py:1327
  388.8 0.0 reduce-scatter.2.cloned.1.call-done
  388.8 0.0 all-gather.8.cloned.1.call-update
  388.8 73.8 %closing.1 = (f32[2,128,1024]{2,1,0:T(8,128)}, bf16[2,4,160,1024]{3,2,1,0:T(8,128)(2,1)}, bf16[8,64,1024]{2,1,0:T(8,128)(2,1)}, f32[8,1024]{1,0:T(8,128)}) custom-call(bf16[2,4,128,1024]{3,2,1,0:T(8,128)(2,1)} %get-tuple-element.100.partial, bf16[512,1024]{1,0:T(8,128)(2,1)} %get-tuple-element.101.pair_grads, bf16[2,128,1024]{2,1,0:T(8,128)(2,1)} %tokens.5, ...), custom_call_target="tpu_custom_call" | custom-call | flops 30000001024 | bytes 30000000 | tf_op jit(solution)/shard_map/closing/pallas_call | solution.py:2529
  462.7 0.0 all-gather.8.cloned.1.call-done
  462.7 0.0 copy-start.2
  462.7 0.0 copy-start
  462.7 12.0 %finish_grads.1 = (f32[1024,256]{1,0:T(8,128)}, f32[1024,256]{1,0:T(8,128)}, f32[1024,256]{1,0:T(8,128)}, f32[1024,256]{1,0:T(8,128)}, f32[256,1024]{1,0:T(8,128...) custom-call(bf16[2,640,1024]{2,1,0:T(8,128)(2,1)} %bitcast.33, ...), custom_call_target="tpu_custom_call" | custom-call | tf_op jit(solution)/shard_map/finish_grads/pallas_call | solution.py:2604
  474.8 0.0 copy-start.1
  474.8 0.0 copy-done.2
  474.8 0.8 copy.48
  475.6 0.0 copy-done
  475.6 1.0 copy.49
  476.5 0.0 copy-done.1
  476.6 1.0 copy.50
  (5 shorter events, 0.0 us)
Async XLA Ops:
  7.2 3.2 copy-start.4
  7.2 3.2 copy-start.3
  7.2 3.6 copy-start.9
  7.2 3.7 copy-start.8
  7.2 76.5 %all-gather.4.cloned.1.call-start = ((), (), s32[]{:S(2)}) async-start(), calls=%async_computation.1 | async-start | bytes 4718592 | tf_op jit(solution)/shard_map/all_gather | solution.py:2673
  7.3 3.7 copy-start.5
  7.3 3.7 copy-start.6
  7.3 3.7 copy-start.7
  7.3 4.4 copy-start.10
  7.3 4.4 copy-start.11
  8.0 189.4 %all-gather.6.cloned.1.call-start = ((), (), s32[]{:S(2)}) async-start(), calls=%async_computation.2 | async-start | bytes 2621440 | tf_op jit(solution)/shard_map/all_gather | solution.py:2697
  83.8 305.0 %reduce-scatter.2.cloned.1.call-start = ((), (), s32[]{:S(2)}) async-start(), calls=%async_computation.3 | async-start | bytes 2621440 | tf_op jit(solution)/shard_map/reduce_scatter | solution.py:2705
  276.0 186.7 %all-gather.8.cloned.1.call-start = ((), (), s32[]{:S(2)}) async-start(), calls=%async_computation.4 | async-start | bytes 4718592 | tf_op jit(solution)/shard_map/all_gather | solution.py:2716
  462.7 12.1 %copy-start.2 = (bf16[2,128,1024]{2,1,0:T(8,128)(2,1)S(1)}, bf16[2,128,1024]{2,1,0:T(8,128)(2,1)}, u32[]{:S(2)}) copy-start(bf16[2,128,1024]{2,1,0:T(8,128)(2,1)} %get-tuple-element.165) | copy-start | bytes 1572868
  462.7 12.9 %copy-start = (f32[2,128,1024]{2,1,0:T(8,128)S(1)}, f32[2,128,1024]{2,1,0:T(8,128)}, u32[]{:S(2)}) copy-start(f32[2,128,1024]{2,1,0:T(8,128)} %get-tuple-element.97) | copy-start | bytes 3145732
  474.8 1.8 copy-start.1
Sparse Core Ops, SparseCore 0:
  10.0 54.8 all-gather.3
  83.9 61.6 all-gather.5
  276.1 53.6 reduce-scatter.1
  389.0 52.8 all-gather.7
